TPU v7x, 128 devices: a whole 4x4x4 slice. The times are simulated.
128 devices in a mesh: row: 8 (over y_lo, z), col: 16 (over y_hi, x, core).
Axes of the slice: x: 4, y: 4 (y_hi: 2, y_lo: 2; y = y_hi * 2 + y_lo), z: 4, core: 2. Of those that a mesh axis runs over, the one named last changes fastest.
Arguments:
- tokens: bfloat16 [2, 192, 256, 512], P(None, 'row', 'col'), may hold values from -6 to 6
- w_qkv: bfloat16 [512, 1536], replicated, may hold values from -0.25 to 0.25
- w_out: bfloat16 [512, 512], replicated, may hold values from -0.25 to 0.25
- q_saved: bfloat16 [2, 192, 256, 512], P(None, 'row', 'col'), may hold values from -4 to 4
- k_saved: bfloat16 [2, 192, 256, 512], P(None, 'row', 'col'), may hold values from -4 to 4
- v_saved: bfloat16 [2, 192, 256, 512], P(None, 'row', 'col'), may hold values from -4 to 4
- scale_exp: int32 [2, 24, 32, 24], P(None, 'row', 'col'), may hold values from -1 to 1
- grad_out: bfloat16 [2, 192, 256, 512], P(None, 'row', 'col'), may hold values from -6 to 6
- crop_start: int32 [2, 2], replicated, may hold values from 0 to 3
Outputs:
- grad_tokens: bfloat16 [2, 192, 256, 512], P(None, 'row', 'col')
- grad_w_qkv: float32 [512, 1536], P('row', 'col')
- grad_w_out: float32 [512, 512], P('row', 'col')
Inputs may be any that keep to these rules, and one draw needn't show every extreme that they name: crop_start[b] holds the first row and the first column of the region of frame b that the loss covers.
All inputs are finite; a program needn't handle non-finite values.
Results may differ from a plain program's by a relative error of at most 0.017.
Values may be sent and summed in bfloat16 or wider, within the bound.
No kernel may reach another device: no remote copies, remote signals or barrier semaphores. Data moves between devices by JAX's collectives and lax.ppermute only.
A program may use at most 128 MiB of HBM per device.

v0:
```python
import math

import jax
import jax.numpy as jnp
from jax import lax
from jax.sharding import PartitionSpec as P

HEADS = 8
RADIUS = 4
BLOCK = 8


max_norm = 1000.0
masked_score = -1e30
tiny_square = 1e-06


def passed_along(array, axis, by):
    size = lax.axis_size(axis)
    pairs = [(i, i + by) for i in range(size) if 0 <= i + by < size]
    return lax.ppermute(array, axis, pairs)


def padded_2(cells, sides, width):
    for axis, dim in sides:
        count = lax.axis_size(axis)
        ends = count - 1
        head = lax.slice_in_dim(cells, 0, width, axis=dim)
        tail = lax.slice_in_dim(cells, cells.shape[dim] - width, cells.shape[dim], axis=dim)
        cells = jnp.concatenate(
            [
                lax.ppermute(tail, axis, [(i, (i + 1) % count) for i in range(ends)]),
                cells,
                lax.ppermute(head, axis, [((i + 1) % count, i) for i in range(ends)]),
            ],
            axis=dim,
        )
    return cells


def product(form, left, right):
    return jnp.einsum(form, left, right, preferred_element_type=jnp.float32)


def dequantize(mantissa, exponent):
    members, height, breadth, features = mantissa.shape
    heads = exponent.shape[3]
    factor = jnp.exp2(exponent.astype(jnp.float32))
    factor = jnp.repeat(jnp.repeat(factor, BLOCK, axis=1), BLOCK, axis=2)
    scaled = (
        mantissa.astype(jnp.float32).reshape(members, height, breadth, heads, features // heads)
        * factor[..., None]
    )
    return scaled.reshape(members, height, breadth, features).astype(jnp.bfloat16)


def query_tiles(tensor):
    height, breadth, features = tensor.shape
    blocked = tensor.reshape(
        height // BLOCK, BLOCK, breadth // BLOCK, BLOCK, HEADS, features // HEADS
    )
    return blocked.transpose(0, 2, 1, 3, 4, 5).reshape(
        height // BLOCK, breadth // BLOCK, BLOCK * BLOCK, HEADS, features // HEADS
    )


def query_untile(tile_set, height, breadth):
    tile_rows, tile_cols = (tile_set.shape[0], tile_set.shape[1])
    features = tile_set.shape[3] * tile_set.shape[4]
    blocked = tile_set.reshape(tile_rows, tile_cols, BLOCK, BLOCK, features)
    return blocked.transpose(0, 2, 1, 3, 4).reshape(height, breadth, features)


def key_tiles(padded):
    height, breadth, features = padded.shape
    tile_rows = height // BLOCK - 1
    tile_cols = breadth // BLOCK - 1
    blocked = padded.reshape(tile_rows + 1, BLOCK, tile_cols + 1, BLOCK, features)
    paired = jnp.stack([blocked[:-1], blocked[1:]], axis=1).reshape(
        tile_rows, 2 * BLOCK, tile_cols + 1, BLOCK, features
    )
    paired = jnp.stack([paired[:, :, :-1], paired[:, :, 1:]], axis=3).reshape(
        tile_rows, 2 * BLOCK, tile_cols, 2 * BLOCK, features
    )
    return paired.transpose(0, 2, 1, 3, 4).reshape(
        tile_rows, tile_cols, 4 * BLOCK * BLOCK, HEADS, features // HEADS
    )


def fold_keys(tile_set):
    tile_rows, tile_cols = (tile_set.shape[0], tile_set.shape[1])
    features = tile_set.shape[3] * tile_set.shape[4]
    tile_grid = tile_set.reshape(tile_rows, tile_cols, 2, BLOCK, 2, BLOCK, features).transpose(
        0, 2, 3, 1, 4, 5, 6
    )
    zero_row = jnp.zeros((1, BLOCK, tile_cols, 2, BLOCK, features), tile_set.dtype)
    summed = jnp.concatenate([tile_grid[:, 0], zero_row], 0) + jnp.concatenate(
        [zero_row, tile_grid[:, 1]], 0
    )
    zero_col = jnp.zeros((tile_rows + 1, BLOCK, 1, BLOCK, features), tile_set.dtype)
    summed = jnp.concatenate([summed[:, :, :, 0], zero_col], 2) + jnp.concatenate(
        [zero_col, summed[:, :, :, 1]], 2
    )
    return summed.reshape((tile_rows + 1) * BLOCK, (tile_cols + 1) * BLOCK, features)


def key_valid(anchor, tile_count, extent):
    position = (
        anchor
        + BLOCK * jnp.arange(tile_count, dtype=jnp.int32)[:, None]
        + jnp.arange(2 * BLOCK, dtype=jnp.int32)[None, :]
    )
    return (position >= 0) & (position < extent)


def window_mask():
    reach = (
        jnp.arange(2 * BLOCK, dtype=jnp.int32)[None, :]
        - jnp.arange(BLOCK, dtype=jnp.int32)[:, None]
    )
    inside = (reach >= 0) & (reach <= 2 * RADIUS)
    return (inside[:, None, :, None] & inside[None, :, None, :]).reshape(
        BLOCK * BLOCK, 4 * BLOCK * BLOCK
    )


def attend(
    queries, grads_attn, keys_pad, values_pad, row_anchor, col_anchor, frame_rows, frame_cols
):
    height, breadth, features = queries.shape
    score_scale = 1.0 / math.sqrt(features // HEADS)
    q_tiles = query_tiles(queries)
    g_tiles = query_tiles(grads_attn)
    k_tiles = key_tiles(keys_pad)
    v_tiles = key_tiles(values_pad)
    tile_rows, tile_cols = (q_tiles.shape[0], q_tiles.shape[1])
    row_ok = key_valid(row_anchor, tile_rows, frame_rows)
    col_ok = key_valid(col_anchor, tile_cols, frame_cols)
    keys_ok = (row_ok[:, None, :, None] & col_ok[None, :, None, :]).reshape(
        tile_rows, tile_cols, 1, 1, 4 * BLOCK * BLOCK
    )
    allowed = keys_ok & window_mask()[None, None, None]
    scores = product("ijqhd,ijkhd->ijhqk", q_tiles, k_tiles) * score_scale
    scores = jnp.where(allowed, scores, masked_score)
    row_max = jnp.max(scores, axis=-1, keepdims=True)
    weights = jnp.exp(scores - row_max)
    softmax = weights / jnp.sum(weights, axis=-1, keepdims=True)
    softmax_half = softmax.astype(jnp.bfloat16)
    out_tiles = product("ijhqk,ijkhd->ijqhd", softmax_half, v_tiles).astype(jnp.bfloat16)
    row_delta = product("ijqhd,ijqhd->ijhq", g_tiles, out_tiles)
    grad_probs = product("ijqhd,ijkhd->ijhqk", g_tiles, v_tiles)
    grad_scores = (softmax * (grad_probs - row_delta[..., None]) * score_scale).astype(jnp.bfloat16)
    grad_q_tiles = product("ijhqk,ijkhd->ijqhd", grad_scores, k_tiles)
    grad_k_tiles = product("ijhqk,ijqhd->ijkhd", grad_scores, q_tiles)
    grad_v_tiles = product("ijhqk,ijqhd->ijkhd", softmax_half, g_tiles)
    return (
        query_untile(out_tiles, height, breadth),
        query_untile(grad_q_tiles, height, breadth),
        fold_keys(grad_k_tiles),
        fold_keys(grad_v_tiles),
    )


def return_rims(padded_grads):
    interior = padded_grads[:, :, :, RADIUS:-RADIUS]
    for offset in (1, -1):
        border_part = (
            padded_grads[:, :, :, -RADIUS:] if offset == 1 else padded_grads[:, :, :, :RADIUS]
        )
        arrived = passed_along(border_part, "col", offset)
        if offset == 1:
            interior = interior.at[:, :, :, :RADIUS].add(arrived)
        else:
            interior = interior.at[:, :, :, -RADIUS:].add(arrived)
    owned = interior[:, :, RADIUS:-RADIUS]
    for offset in (1, -1):
        border_part = interior[:, :, -RADIUS:] if offset == 1 else interior[:, :, :RADIUS]
        arrived = passed_along(border_part, "row", offset)
        if offset == 1:
            owned = owned.at[:, :, :RADIUS].add(arrived)
        else:
            owned = owned.at[:, :, -RADIUS:].add(arrived)
    return owned


def body(tokens, w_qkv, w_out, q_saved, k_saved, v_saved, scale_exp, grad_out, crop_start):
    members, height, breadth, features = tokens.shape
    queries = dequantize(q_saved, scale_exp[..., :HEADS])
    keys_full = dequantize(k_saved, scale_exp[..., HEADS : 2 * HEADS])
    values = dequantize(v_saved, scale_exp[..., 2 * HEADS :])
    row_index = lax.axis_index("row")
    col_index = lax.axis_index("col")
    frame_rows = height * lax.axis_size("row")
    frame_cols = breadth * lax.axis_size("col")
    row_place = row_index * height + jnp.arange(height, dtype=jnp.int32)
    col_place = col_index * breadth + jnp.arange(breadth, dtype=jnp.int32)
    inside = (row_place[None, :, None] >= crop_start[:, 0][:, None, None]) & (
        col_place[None, None, :] >= crop_start[:, 1][:, None, None]
    )
    masked = jnp.where(inside[..., None], grad_out, jnp.zeros_like(grad_out))
    flat_grad = masked.reshape(-1, features)
    grad_attn = lax.dot_general(
        flat_grad, w_out, (((1,), (1,)), ((), ())), preferred_element_type=jnp.float32
    )
    grad_attn = grad_attn.astype(jnp.bfloat16).reshape(masked.shape)
    stacked = jnp.stack([keys_full, values])
    padded = padded_2(stacked, (("row", 2), ("col", 3)), RADIUS)

    def one_member(member):
        q_member, g_member, k_member, v_member = member
        return attend(
            q_member,
            g_member,
            k_member,
            v_member,
            row_index * height - RADIUS,
            col_index * breadth - RADIUS,
            frame_rows,
            frame_cols,
        )

    attn_out, grad_query, grad_k_pad, grad_v_pad = lax.map(
        one_member, (queries, grad_attn, padded[0], padded[1])
    )
    owned = return_rims(jnp.stack([grad_k_pad, grad_v_pad]))
    grad_key, grad_value = (owned[0], owned[1])
    flat_qkv = (
        jnp.concatenate([grad_query, grad_key, grad_value], axis=-1)
        .astype(jnp.bfloat16)
        .reshape(-1, 3 * features)
    )
    grad_tokens = lax.dot_general(
        flat_qkv, w_qkv, (((1,), (1,)), ((), ())), preferred_element_type=jnp.float32
    )
    grad_tokens = grad_tokens.astype(jnp.bfloat16).reshape(tokens.shape)
    raw_qkv = lax.dot_general(
        tokens.reshape(-1, features),
        flat_qkv,
        (((0,), (0,)), ((), ())),
        preferred_element_type=jnp.float32,
    )
    raw_out = lax.dot_general(
        attn_out.reshape(-1, features),
        flat_grad,
        (((0,), (0,)), ((), ())),
        preferred_element_type=jnp.float32,
    )
    whole_qkv, whole_out = lax.psum((raw_qkv, raw_out), ("row", "col"))
    squares = jnp.sum(whole_qkv * whole_qkv) + jnp.sum(whole_out * whole_out)
    rows_each = features // lax.axis_size("row")
    qkv_cols = 3 * features // lax.axis_size("col")
    out_cols = features // lax.axis_size("col")
    part_qkv = lax.dynamic_slice(
        whole_qkv, (row_index * rows_each, col_index * qkv_cols), (rows_each, qkv_cols)
    )
    part_out = lax.dynamic_slice(
        whole_out, (row_index * rows_each, col_index * out_cols), (rows_each, out_cols)
    )
    factor = jnp.minimum(1.0, max_norm / jnp.sqrt(squares + tiny_square))
    return (grad_tokens, factor * part_qkv, factor * part_out)


def solution(mesh):
    placed = (
        P(None, "row", "col", None),
        P(),
        P(),
        P(None, "row", "col", None),
        P(None, "row", "col", None),
        P(None, "row", "col", None),
        P(None, "row", "col", None),
        P(None, "row", "col", None),
        P(),
    )
    return jax.shard_map(
        body,
        mesh=mesh,
        in_specs=placed,
        out_specs=(P(None, "row", "col", None), P("row", "col"), P("row", "col")),
        check_vma=False,
    )
```

profile of v0, /device:TPU:1, one launch (start us, length us, event | category | flops | bytes accessed | tf_op | source)
XLA Modules:
  0.0 482.4 jit_solution(6654649221721645921)
XLA Ops:
  10.3 3.8 mul.121
  16.3 3.7 mul.125
  25.1 5.7 %collective-permute-start = (bf16[2,2,4,16,512]{4,3,2,1,0:T(8,128)(2,1)}, bf16[2,2,4,16,512]{4,3,2,1,0:T(8,128)(2,1)}, u32[]{:S(2)}, u32[]{:S(2)}) collective-permute-start(bf16[2,2,4,16,512]{4,3,2,1,0:T(8,128)(2,1)} %get-tuple-element.293), channel_id=1, source_target_pairs={{0,16},{16,32},{32,48},{48,64},{64,80},{80,96},{96,112},{1,17},{17... | collective-permute-start | bytes 786440 | tf_op jit(solution)/shard_map/ppermute | solution.py:32
  33.1 3.8 mul.131
  57.5 190.2 %while.24 = (s32[]{:T(128)}, bf16[2,24,16,512]{3,2,1,0:T(8,128)(2,1)}, bf16[2,24,16,512]{3,1,2,0:T(8,128)(2,1)}, f32[2,32,24,512]{3,1,2,0:T(8,128)}, f32[2,32,24...) while((s32[]{:T(128)}, ...), condition=%wide.region_3.4_spmd.clone, body=%wide.region_0.3_spmd.sunk.clone | while | flops 621461056 | bytes 255329296 | solution.py:222
  67.9 4.5 copy.197
  76.2 3.4 copy.199
  81.9 3.3 fusion.117
  86.2 4.4 fusion.120
  98.1 3.5 multiply_convert_fusion.6
  107.3 4.4 convolution_bitcast_fusion.12
  111.8 5.9 %copy.204 = f32[3,2,256,8,64]{4,3,2,1,0:T(8,128)} copy(f32[3,2,256,8,64]{2,4,3,1,0:T(8,128)} %convolution_bitcast_fusion.12) | data formatting | bytes 6291456 | tf_op jit(solution)/shard_map/while/body/eval_jaxpr/ijhqk,ijqhd->ijkhd/transpose | solution.py:42
  117.6 6.2 %reshape.552 = f32[3,2,2,8,2,8,512]{6,5,4,3,2,1,0:T(8,128)} reshape(f32[3,2,256,8,64]{4,3,2,1,0:T(8,128)} %copy.204) | data formatting | bytes 6291456 | tf_op jit(solution)/shard_map/while/body/eval_jaxpr/reshape | solution.py:93
  130.3 5.9 %copy.206 = f32[3,2,256,8,64]{4,3,2,1,0:T(8,128)} copy(f32[3,2,256,8,64]{2,4,3,1,0:T(8,128)} %convolution_bitcast_fusion.13) | data formatting | bytes 6291456 | tf_op jit(solution)/shard_map/while/body/eval_jaxpr/ijhqk,ijqhd->ijkhd/transpose | solution.py:42
  136.2 6.2 %reshape.553 = f32[3,2,2,8,2,8,512]{6,5,4,3,2,1,0:T(8,128)} reshape(f32[3,2,256,8,64]{4,3,2,1,0:T(8,128)} %copy.206) | data formatting | bytes 6291456 | tf_op jit(solution)/shard_map/while/body/eval_jaxpr/reshape | solution.py:93
  163.0 4.5 copy.197
  171.3 3.4 copy.199
  177.1 3.3 fusion.117
  181.3 4.4 fusion.120
  193.2 3.5 multiply_convert_fusion.6
  202.5 4.4 convolution_bitcast_fusion.12
  206.9 5.9 %copy.204 = f32[3,2,256,8,64]{4,3,2,1,0:T(8,128)} copy(f32[3,2,256,8,64]{2,4,3,1,0:T(8,128)} %convolution_bitcast_fusion.12) | data formatting | bytes 6291456 | tf_op jit(solution)/shard_map/while/body/eval_jaxpr/ijhqk,ijqhd->ijkhd/transpose | solution.py:42
  212.8 6.2 %reshape.552 = f32[3,2,2,8,2,8,512]{6,5,4,3,2,1,0:T(8,128)} reshape(f32[3,2,256,8,64]{4,3,2,1,0:T(8,128)} %copy.204) | data formatting | bytes 6291456 | tf_op jit(solution)/shard_map/while/body/eval_jaxpr/reshape | solution.py:93
  225.5 5.9 %copy.206 = f32[3,2,256,8,64]{4,3,2,1,0:T(8,128)} copy(f32[3,2,256,8,64]{2,4,3,1,0:T(8,128)} %convolution_bitcast_fusion.13) | data formatting | bytes 6291456 | tf_op jit(solution)/shard_map/while/body/eval_jaxpr/ijhqk,ijqhd->ijkhd/transpose | solution.py:42
  231.3 6.2 %reshape.553 = f32[3,2,2,8,2,8,512]{6,5,4,3,2,1,0:T(8,128)} reshape(f32[3,2,256,8,64]{4,3,2,1,0:T(8,128)} %copy.206) | data formatting | bytes 6291456 | tf_op jit(solution)/shard_map/while/body/eval_jaxpr/reshape | solution.py:93
  249.2 4.5 collective-permute-start.4
  254.6 10.9 %collective-permute-done.4 = f32[2,2,32,4,512]{4,2,3,1,0:T(8,128)S(1)} collective-permute-done((f32[2,2,32,4,512]{4,2,3,1,0:T(8,128)S(1)}, f32[2,2,32,4,512]{4,2,3,1,0:T(8,128)S(1)}, u32[]{:S(2)}, u32[]{:S(2)}) %collective-permute-start.4) | collective-permute-done | bytes 1048608 | tf_op jit(solution)/shard_map/ppermute | solution.py:21
  267.9 15.2 %collective-permute-done.5 = f32[2,2,32,4,512]{4,2,3,1,0:T(8,128)S(1)} collective-permute-done((f32[2,2,32,4,512]{4,2,3,1,0:T(8,128)S(1)}, f32[2,2,32,4,512]{4,2,3,1,0:T(8,128)S(1)}, u32[]{:S(2)}, u32[]{:S(2)}) %collective-permute-start.5) | collective-permute-done | bytes 1048608 | tf_op jit(solution)/shard_map/ppermute | solution.py:21
  293.0 3.7 collective-permute-done.7
  297.2 3.2 convolution_bitcast_fusion.3
  304.6 162.9 %all-reduce.11.cloned.1.call-done = (f32[512,1536]{0,1:T(8,128)}, f32[512,512]{1,0:T(8,128)}) async-done(((f32[512,1536]{0,1:T(8,128)}, f32[512,512]{1,0:T(8,128)}), (f32[512,1536]{0,1:T(8,128)}, f32[512,512]{1,0:T(8,128)})) %all-reduce.11.cloned.1.call-update) | async-done | bytes 4194320 | tf_op jit(solution)/shard_map/psum | solution.py:248
  467.6 3.4 multiply_reduce_fusion.1
  (240 shorter events, 149.3 us)
Async XLA Ops:
  7.2 295.2 %copy-start = (bf16[512,1536]{1,0:T(8,128)(2,1)S(1)}, bf16[512,1536]{1,0:T(8,128)(2,1)}, u32[]{:S(2)}) copy-start(bf16[512,1536]{1,0:T(8,128)(2,1)} %param.20) | copy-start | bytes 4718596
  7.2 460.4 %all-reduce.11.cloned.1.call-start = ((), (), s32[]{:S(2)}) async-start(), calls=%async_computation | async-start | bytes 8388608 | tf_op jit(solution)/shard_map/psum | solution.py:248
  23.8 14.9 %collective-permute-start.1 = (bf16[2,2,4,16,512]{4,3,2,1,0:T(8,128)(2,1)}, bf16[2,2,4,16,512]{4,3,2,1,0:T(8,128)(2,1)S(1)}, u32[]{:S(2)}, u32[]{:S(2)}) collective-permute-start(bf16[2,2,4,16,512]{4,3,2,1,0:T(8,128)(2,1)} %get-tuple-element.294), channel_id=1, source_target_pairs={{16,0},{32,16},{48,32},{64,48},{80,64},{96,80},{112,96},{17,1},{33... | collective-permute-start | bytes 786440 | tf_op jit(solution)/shard_map/ppermute | solution.py:34
  25.1 13.6 %collective-permute-start = (bf16[2,2,4,16,512]{4,3,2,1,0:T(8,128)(2,1)}, bf16[2,2,4,16,512]{4,3,2,1,0:T(8,128)(2,1)}, u32[]{:S(2)}, u32[]{:S(2)}) collective-permute-start(bf16[2,2,4,16,512]{4,3,2,1,0:T(8,128)(2,1)} %get-tuple-element.293), channel_id=1, source_target_pairs={{0,16},{16,32},{32,48},{48,64},{64,80},{80,96},{96,112},{1,17},{17... | collective-permute-start | bytes 786440 | tf_op jit(solution)/shard_map/ppermute | solution.py:32
  33.0 3.8 copy-start.20
  36.8 9.6 %copy-start.23 = (bf16[512,512]{1,0:T(8,128)(2,1)S(1)}, bf16[512,512]{1,0:T(8,128)(2,1)}, u32[]{:S(2)}) copy-start(bf16[512,512]{1,0:T(8,128)(2,1)} %param.21) | copy-start | bytes 1572868
  37.2 10.7 %copy-start.14 = (f32[2,24,16,512]{3,2,1,0:T(8,128)S(1)}, f32[2,24,16,512]{3,2,1,0:T(8,128)}, u32[]{:S(2)}) copy-start(f32[2,24,16,512]{3,2,1,0:T(8,128)} %mul.131) | copy-start | bytes 4718596
  37.2 10.7 %copy-start.19 = (bf16[2,24,16,512]{3,2,1,0:T(8,128)(2,1)S(1)}, bf16[2,24,16,512]{3,2,1,0:T(8,128)(2,1)}, u32[]{:S(2)}) copy-start(bf16[2,24,16,512]{3,2,1,0:T(8,128)(2,1)} %param.22) | copy-start | bytes 2359300
  38.7 10.4 %copy-start.16 = (bf16[2,24,16,512]{3,2,1,0:T(8,128)(2,1)}, bf16[2,24,16,512]{3,2,1,0:T(8,128)(2,1)S(1)}, u32[]{:S(2)}) copy-start(bf16[2,24,16,512]{3,2,1,0:T(8,128)(2,1)S(1)} %broadcast_select_fusion) | copy-start | bytes 2359300
  40.4 10.9 %collective-permute-start.3 = (bf16[2,2,32,4,512]{4,3,2,1,0:T(4,128)(2,1)S(1)}, bf16[2,2,32,4,512]{4,3,2,1,0:T(4,128)(2,1)S(1)}, u32[]{:S(2)}, u32[]{:S(2)}) collective-permute-start(bf16[2,2,32,4,512]{4,3,2,1,0:T(4,128)(2,1)S(1)} %get-tuple-element.292), channel_id=1, source_target_pairs={{1,0},{2,1},{3,2},{4,3},{5,4},{6,5},{7,6},{8,7},{9,8},{10,9},{11,1... | collective-permute-start | bytes 1572872 | tf_op jit(solution)/shard_map/ppermute | solution.py:34
  43.3 9.2 %collective-permute-start.2 = (bf16[2,2,32,4,512]{4,3,2,1,0:T(4,128)(2,1)S(1)}, bf16[2,2,32,4,512]{4,3,2,1,0:T(4,128)(2,1)S(1)}, u32[]{:S(2)}, u32[]{:S(2)}) collective-permute-start(bf16[2,2,32,4,512]{4,3,2,1,0:T(4,128)(2,1)S(1)} %get-tuple-element.291), channel_id=1, source_target_pairs={{0,1},{1,2},{2,3},{3,4},{4,5},{5,6},{6,7},{7,8},{8,9},{9,10},{10,1... | collective-permute-start | bytes 1572872 | tf_op jit(solution)/shard_map/ppermute | solution.py:32
  67.9 4.5 copy-start.7
  86.2 4.4 copy-start.5
  86.2 4.4 copy-start.6
  104.2 3.1 copy-start.4
  145.0 2.8 copy-start.11
  163.0 4.5 copy-start.7
  181.3 4.4 copy-start.5
  181.3 4.4 copy-start.6
  199.3 3.1 copy-start.4
  240.2 2.8 copy-start.11
  247.8 6.0 %copy-start.10 = (f32[2,32,24,512]{3,1,2,0:T(8,128)S(1)}, f32[2,32,24,512]{3,1,2,0:T(8,128)}, u32[]{:S(2)}) copy-start(f32[2,32,24,512]{3,1,2,0:T(8,128)} %get-tuple-element.223) | copy-start | bytes 9437188
  247.8 6.0 %copy-start.13 = (f32[2,32,24,512]{3,1,2,0:T(8,128)S(1)}, f32[2,32,24,512]{3,1,2,0:T(8,128)}, u32[]{:S(2)}) copy-start(f32[2,32,24,512]{3,1,2,0:T(8,128)} %get-tuple-element.224) | copy-start | bytes 9437188
  249.2 16.3 %collective-permute-start.4 = (f32[2,2,32,4,512]{4,2,3,1,0:T(8,128)S(1)}, f32[2,2,32,4,512]{4,2,3,1,0:T(8,128)S(1)}, u32[]{:S(2)}, u32[]{:S(2)}) collective-permute-start(f32[2,2,32,4,512]{4,2,3,1,0:T(8,128)S(1)} %fusion.46), channel_id=1, source_target_pairs={{0,1},{1,2},{2,3},{3,4},{4,5},{5,6},{6,7},{7,8},{8,9},{9,10},{10,1... | collective-permute-start | bytes 3145736 | tf_op jit(solution)/shard_map/ppermute | solution.py:21
  265.8 22.1 %copy-start.17 = (bf16[2,24,16,512]{3,2,1,0:T(8,128)(2,1)S(1)}, bf16[2,24,16,512]{3,2,1,0:T(8,128)(2,1)}, u32[]{:S(2)}) copy-start(bf16[2,24,16,512]{3,2,1,0:T(8,128)(2,1)} %copy-done.16) | copy-start | bytes 2359300
  265.9 22.1 %copy-start.22 = (bf16[2,24,16,512]{3,2,1,0:T(8,128)(2,1)S(1)}, bf16[2,24,16,512]{3,2,1,0:T(8,128)(2,1)}, u32[]{:S(2)}) copy-start(bf16[2,24,16,512]{3,2,1,0:T(8,128)(2,1)} %get-tuple-element.225) | copy-start | bytes 2359300
  265.9 17.3 %collective-permute-start.5 = (f32[2,2,32,4,512]{4,2,3,1,0:T(8,128)S(1)}, f32[2,2,32,4,512]{4,2,3,1,0:T(8,128)S(1)}, u32[]{:S(2)}, u32[]{:S(2)}) collective-permute-start(f32[2,2,32,4,512]{4,2,3,1,0:T(8,128)S(1)} %get-tuple-element.283), channel_id=1, source_target_pairs={{1,0},{2,1},{3,2},{4,3},{5,4},{6,5},{7,6},{8,7},{9,8},{10,9},{11,1... | collective-permute-start | bytes 3145736 | tf_op jit(solution)/shard_map/ppermute | solution.py:21
  283.7 9.0 %collective-permute-start.6 = (f32[2,2,4,16,512]{4,2,3,1,0:T(4,128)S(1)}, f32[2,2,4,16,512]{4,2,3,1,0:T(4,128)S(1)}, u32[]{:S(2)}, u32[]{:S(2)}) collective-permute-start(f32[2,2,4,16,512]{4,2,3,1,0:T(4,128)S(1)} %get-tuple-element.286), channel_id=1, source_target_pairs={{0,16},{16,32},{32,48},{48,64},{64,80},{80,96},{96,112},{1,17},{17... | collective-permute-start | bytes 1572872 | tf_op jit(solution)/shard_map/ppermute | solution.py:21
  286.6 10.1 %collective-permute-start.7 = (f32[2,2,4,16,512]{4,2,3,1,0:T(4,128)S(1)}, f32[2,2,4,16,512]{4,2,3,1,0:T(4,128)S(1)}, u32[]{:S(2)}, u32[]{:S(2)}) collective-permute-start(f32[2,2,4,16,512]{4,2,3,1,0:T(4,128)S(1)} %get-tuple-element.285), channel_id=1, source_target_pairs={{16,0},{32,16},{48,32},{64,48},{80,64},{96,80},{112,96},{17,1},{33... | collective-permute-start | bytes 1572872 | tf_op jit(solution)/shard_map/ppermute | solution.py:21
  290.2 7.0 %copy-start.18 = (bf16[2,24,16,512]{3,1,2,0:T(8,128)(2,1)S(1)}, bf16[2,24,16,512]{3,1,2,0:T(8,128)(2,1)}, u32[]{:S(2)}) copy-start(bf16[2,24,16,512]{3,1,2,0:T(8,128)(2,1)} %get-tuple-element.222) | copy-start | bytes 2359300
  290.2 7.0 %copy-start.21 = (bf16[2,24,16,512]{3,2,1,0:T(8,128)(2,1)S(1)}, bf16[2,24,16,512]{3,2,1,0:T(8,128)(2,1)}, u32[]{:S(2)}) copy-start(bf16[2,24,16,512]{3,2,1,0:T(8,128)(2,1)} %param.19) | copy-start | bytes 2359300
  467.6 3.4 copy-start.15
  (16 other events, 30.8 us)
Sparse Core Ops, SparseCore 0:
  300.6 166.9 all-reduce.10
where the time goes:
time: 485 us; the launch traced here: 482 us
  waiting for transfers between devices  199 us (41%)
  local copies, waits for them, and re-layouts  163 us (34%)
  matrix products  43.6 us (9%)
  other arithmetic  37 us (8%)
  starting transfers between devices  23.8 us (5%)
  between operations  15.7 us (3%)
    psum x1, waiting for transfers between devices, body(): whole_qkv, whole_out = lax.psum((raw_qkv, raw_out), ('row', 'col'))  163 us
    dot_general x12, matrix products, product(): return jnp.einsum(form, left, right, preferred_element_type=jnp.float32)  34.9 us
    ppermute x4, waiting for transfers between devices, passed_along(): return lax.ppermute(array, axis, pairs)  32.3 us
    reshape x8, local copies, waits for them, and re-layouts, key_tiles(): paired.transpose(0, 2, 1, 3, 4)  27.9 us
    transpose x6, local copies, waits for them, and re-layouts, product(): return jnp.einsum(form, left, right, preferred_element_type=jnp.float32)  26.7 us
    reshape x4, local copies, waits for them, and re-layouts, fold_keys(): tile_set.reshape(tile_rows, tile_cols, 2, BLOCK, 2, BLOCK, features)  25 us
    while x54, local copies, waits for them, and re-layouts  18.2 us
    mul x9, local copies, waits for them, and re-layouts, dequantize(): mantissa.astype(jnp.float32)  17.7 us
  transfers between devices with their start and end apart: 9, of which 7 were waited for; matrix products, arithmetic and copies ran while one was open for 4% of the time, Pallas kernels for 0%

commit v1 on v0

v1 whole, which is shorter than its diff:
```python
import jax
import jax.numpy as jnp
from jax import lax
from jax.experimental import pallas as pl
from jax.experimental.pallas import tpu as pltpu
from jax.sharding import PartitionSpec as P

HEADS = 8
RADIUS = 4
BLOCK = 8
GROUP = 4

max_norm = 1000.0
masked_score = -1e30
tiny_square = 1e-06

f32 = jnp.float32
bf16 = jnp.bfloat16
VMEM = pl.BlockSpec(memory_space=pltpu.VMEM)
COLS = ("pair", "core")
SMEM = pl.BlockSpec(memory_space=pltpu.SMEM)


def call(kernel, outs, ins, scratch=(), smem=(), flops=0, limit=56 << 20):
    moved = sum(a.size * a.dtype.itemsize for a in list(ins) + list(outs))
    return pl.pallas_call(
        kernel,
        out_shape=outs,
        in_specs=[SMEM if n in smem else VMEM for n in range(len(ins))],
        out_specs=jax.tree.map(lambda _: VMEM, outs),
        scratch_shapes=list(scratch),
        compiler_params=pltpu.CompilerParams(vmem_limit_bytes=limit),
        cost_estimate=pl.CostEstimate(
            flops=flops, bytes_accessed=moved, transcendentals=0
        ),
    )(*ins)


def shape(*dims, dtype=bf16):
    return jax.ShapeDtypeStruct(dims, dtype)


def turn(x):
    return pltpu.roll(x, 4, 1)


def sublane(x):
    return lax.broadcasted_iota(jnp.int32, x.shape, 1)


def block_of(ref, fac_ref, part, b, i, j, rows, features):
    tiles = fac_ref.shape[2]
    factor = fac_ref[b, i, j : j + 1, part * features : (part + 1) * features]
    del tiles
    x = ref[b, rows, 8 * j : 8 * j + 8, :].astype(f32)
    return x * factor[None]


def edge_kernel(k_ref, v_ref, fac_ref, up_ref, down_ref, left_ref, right_ref):
    members, height, breadth, features = k_ref.shape
    tiles, last = breadth // 8, height // 8 - 1
    for b in range(members):
        for n, ref in enumerate((k_ref, v_ref)):
            top = [block_of(ref, fac_ref, n + 1, b, 0, j, pl.ds(0, 4), features) for j in range(tiles)]
            up_ref[n, b] = jnp.concatenate(top, 1).astype(bf16)
            low = [
                block_of(ref, fac_ref, n + 1, b, last, j, pl.ds(height - 4, 4), features)
                for j in range(tiles)
            ]
            down_ref[n, b] = jnp.concatenate(low, 1).astype(bf16)
        for i in range(height // 8):
            rows = pl.ds(8 * i, 8)
            k0 = block_of(k_ref, fac_ref, 1, b, i, 0, rows, features)
            v0 = block_of(v_ref, fac_ref, 2, b, i, 0, rows, features)
            k1 = block_of(k_ref, fac_ref, 1, b, i, tiles - 1, rows, features)
            v1 = block_of(v_ref, fac_ref, 2, b, i, tiles - 1, rows, features)
            low = sublane(k0) < 4
            left_ref[b, rows] = jnp.where(low, k0, turn(v0)).astype(bf16)
            right_ref[b, rows] = jnp.where(low, turn(v1), k1).astype(bf16)


def corner_kernel(top_ref, bottom_ref, left_ref, right_ref):
    parts, members, rows, breadth, features = top_ref.shape
    for b in range(members):
        for n, ref in enumerate((top_ref, bottom_ref)):
            k0 = ref[0, b, :, 0:8, :].astype(f32)
            v0 = ref[1, b, :, 0:8, :].astype(f32)
            k1 = ref[0, b, :, breadth - 8 : breadth, :].astype(f32)
            v1 = ref[1, b, :, breadth - 8 : breadth, :].astype(f32)
            low = sublane(k0) < 4
            left_ref[b, 4 * n : 4 * n + 4] = jnp.where(low, k0, turn(v0)).astype(bf16)
            right_ref[b, 4 * n : 4 * n + 4] = jnp.where(low, turn(v1), k1).astype(bf16)


def prepare_kernel(place_ref, q_ref, g_ref, fac_ref, w_ref, qs_ref, gm_ref, do_ref):
    members, height, breadth, features = q_ref.shape
    tiles = breadth // 8
    for b in range(members):
        for i in range(height // 8):
            rows = pl.ds(8 * i, 8)
            parts = [block_of(q_ref, fac_ref, 0, b, i, j, rows, features) for j in range(tiles)]
            qs_ref[b, rows] = (jnp.concatenate(parts, 1) * 0.125).astype(bf16)
            g = g_ref[b, rows].astype(f32)
            r = lax.broadcasted_iota(jnp.int32, g.shape, 0) + (8 * i + place_ref[0])
            c = lax.broadcasted_iota(jnp.int32, g.shape, 1) + place_ref[1]
            keep = (r >= place_ref[2 + 2 * b]) & (c >= place_ref[3 + 2 * b])
            gm = jnp.where(keep, g, 0.0).astype(bf16)
            gm_ref[b, rows] = gm
            do = lax.dot_general(
                gm.reshape(8 * breadth, features), w_ref[...], (((1,), (1,)), ((), ())),
                preferred_element_type=f32,
            )
            do_ref[b, rows] = do.astype(bf16).reshape(8, breadth, features)


def attend_kernel(
    place_ref, qs_ref, do_ref, k_ref, v_ref, fac_ref, gm_ref, tok_ref,
    top_ref, bottom_ref, left_ref, right_ref, cl_ref, cr_ref,
    dq_ref, first_ref, dk_ref, dv_ref, dl_ref, dr_ref,
    kt_ref, vt_ref, dkt_ref, dvt_ref, o_ref,
):
    members, height, breadth, features = qs_ref.shape
    strips, tiles = height // 8, breadth // 8
    heads_lanes = features // HEADS
    wide = GROUP * heads_lanes
    groups = HEADS // GROUP
    frame_rows, frame_cols = place_ref[6], place_ref[7]

    def put(b, rows, kblocks, vblocks, lmsg, rmsg):
        low = sublane(lmsg) < 4
        for ref, blocks, lm, rm in (
            (kt_ref, kblocks, lmsg, rmsg),
            (vt_ref, vblocks, turn(lmsg), turn(rmsg)),
        ):
            for t in range(tiles):
                before = lm if t == 0 else blocks[t - 1]
                after = rm if t == tiles - 1 else blocks[t + 1]
                rim = jnp.where(low, after, before)
                ref[b, t, rows] = jnp.concatenate([blocks[t], rim], 1).astype(bf16)

    for b in range(members):
        for n, ref in enumerate((top_ref, bottom_ref)):
            halo = slice(0, 4) if n == 0 else slice(height + 4, height + 8)
            kb = [ref[0, b, :, 8 * j : 8 * j + 8, :].astype(f32) for j in range(tiles)]
            vb = [ref[1, b, :, 8 * j : 8 * j + 8, :].astype(f32) for j in range(tiles)]
            put(b, halo, kb, vb, cl_ref[b, 4 * n : 4 * n + 4].astype(f32), cr_ref[b, 4 * n : 4 * n + 4].astype(f32))
        for i in range(strips):
            rows = pl.ds(8 * i, 8)
            kb = [block_of(k_ref, fac_ref, 1, b, i, j, rows, features) for j in range(tiles)]
            vb = [block_of(v_ref, fac_ref, 2, b, i, j, rows, features) for j in range(tiles)]
            put(b, slice(8 * i + 4, 8 * i + 12), kb, vb, left_ref[b, rows].astype(f32), right_ref[b, rows].astype(f32))

    for b in range(members):
        for t in range(tiles):
            dkt_ref[b, t, 0:8] = jnp.zeros((8, 16, features), f32)
            dvt_ref[b, t, 0:8] = jnp.zeros((8, 16, features), f32)

    lane = lax.broadcasted_iota(jnp.int32, (1, wide), 1) // heads_lanes
    head_mask = [(lane == h).astype(f32).astype(bf16) for h in range(GROUP)]
    half = lax.broadcasted_iota(jnp.int32, (64, 2 * heads_lanes), 1) < heads_lanes

    def spread(x):
        return jnp.concatenate([x * m for m in head_mask], 0)

    def gather(x):
        return jnp.concatenate(
            [
                jnp.where(half, x[128 * n : 128 * n + 64, 128 * n : 128 * n + 128],
                          x[128 * n + 64 : 128 * n + 128, 128 * n : 128 * n + 128])
                for n in range(GROUP // 2)
            ],
            1,
        )

    def bias_of(i, t):
        qn = lax.broadcasted_iota(jnp.int32, (64, 256), 0)
        kn = lax.broadcasted_iota(jnp.int32, (64, 256), 1)
        qr, qc = qn // 8, qn % 8
        kr, ks = kn // 16, kn % 16
        kc = jnp.where(ks < 8, ks, jnp.where(ks < 12, ks, ks - 16))
        row = place_ref[0] + 8 * i - 4 + kr
        col = place_ref[1] + 8 * t + kc
        ok = (kr >= qr) & (kr <= qr + 8) & (kc >= qc - 4) & (kc <= qc + 4)
        ok &= (row >= 0) & (row < frame_rows) & (col >= 0) & (col < frame_cols)
        return jnp.where(ok, 0.0, masked_score)

    def step(n, _):
        b, i = n // strips, n % strips
        rows = pl.ds(8 * i, 8)
        q8 = qs_ref[b, rows].astype(f32)
        g8 = do_ref[b, rows].astype(f32)
        outs, grads = [], []
        for t in range(tiles):
            bias = bias_of(i, t)
            bias4 = jnp.concatenate([bias] * GROUP, 0)
            q64 = q8[:, 8 * t : 8 * t + 8].reshape(64, features).astype(bf16)
            g64 = g8[:, 8 * t : 8 * t + 8].reshape(64, features).astype(bf16)
            keys = pl.ds(8 * i, 16)
            ot, dqt = [], []
            for g in range(groups):
                lanes = slice(g * wide, (g + 1) * wide)
                qx, gx = spread(q64[:, lanes]), spread(g64[:, lanes])
                k = kt_ref[b, t, keys, :, lanes].reshape(256, wide)
                v = vt_ref[b, t, keys, :, lanes].reshape(256, wide)
                across = (((1,), (1,)), ((), ()))
                s = lax.dot_general(qx, k, across, preferred_element_type=f32) + bias4
                w = jnp.exp(s - jnp.max(s, 1, keepdims=True))
                p = w * (1.0 / jnp.sum(w, 1, keepdims=True))
                ph = p.astype(bf16)
                o = jnp.dot(ph, v, preferred_element_type=f32).astype(bf16).astype(f32)
                delta = jnp.sum(o * gx.astype(f32), 1, keepdims=True)
                dp = lax.dot_general(gx, v, across, preferred_element_type=f32)
                ds = (p * (dp - delta)).astype(bf16)
                dq = jnp.dot(ds, k, preferred_element_type=f32)
                down = (((0,), (0,)), ((), ()))
                dk = lax.dot_general(ds, qx, down, preferred_element_type=f32).reshape(16, 16, wide)
                dv = lax.dot_general(ph, gx, down, preferred_element_type=f32).reshape(16, 16, wide)
                ot.append(gather(o))
                dqt.append(gather(dq) * 0.125)
                for ref, x in ((dkt_ref, dk), (dvt_ref, dv)):
                    ref[b, t, rows, :, lanes] = ref[b, t, rows, :, lanes] + x[0:8]
                    ref[b, t, pl.ds(8 * i + 8, 8), :, lanes] = x[8:16]
            outs.append(jnp.concatenate(ot, 1).reshape(8, 8, features))
            grads.append(jnp.concatenate(dqt, 1).reshape(8, 8, features))
        o_ref[b, rows] = jnp.concatenate(outs, 1).astype(bf16)
        dq_ref[b, rows] = jnp.concatenate(grads, 1).astype(bf16)
        return 0

    lax.fori_loop(0, members * strips, step, 0)

    for b in range(members):
        for r in range(0, height + 8, 8):
            rows = slice(r, r + 8)
            rims = []
            for ref, out in ((dkt_ref, dk_ref), (dvt_ref, dv_ref)):
                rim = [ref[b, t, rows, 8:16] for t in range(tiles)]
                low = sublane(rim[0]) < 4
                own = []
                for t in range(tiles):
                    x = ref[b, t, rows, 0:8]
                    if t > 0:
                        x = x + jnp.where(low, rim[t - 1], 0.0)
                    if t < tiles - 1:
                        x = x + jnp.where(low, 0.0, rim[t + 1])
                    own.append(x)
                out[b, rows] = jnp.concatenate(own, 1)
                rims.append((rim[0], rim[tiles - 1]))
            (kl, kr), (vl, vr) = rims
            dl_ref[b, rows] = jnp.where(low, turn(vl), kl).astype(bf16)
            dr_ref[b, rows] = jnp.where(low, kr, turn(vr)).astype(bf16)

    cells = members * height * breadth
    down = (((0,), (0,)), ((), ()))
    first_ref[:, 0:features] = lax.dot_general(
        tok_ref[...].reshape(cells, features), dq_ref[...].reshape(cells, features), down,
        preferred_element_type=f32,
    ).astype(first_ref.dtype)
    first_ref[:, features:] = lax.dot_general(
        o_ref[...].reshape(cells, features), gm_ref[...].reshape(cells, features), down,
        preferred_element_type=f32,
    ).astype(first_ref.dtype)


def rim_kernel(dk_ref, dv_ref, fl_ref, fr_ref, dkc_ref, dvc_ref, up_ref, down_ref):
    members, tall, breadth, features = dk_ref.shape
    height = tall - 8
    last = breadth - 8
    for b in range(members):
        for r in range(0, tall, 4):
            rows = slice(r, r + 4)
            fl = fl_ref[b, rows].astype(f32)
            fr = fr_ref[b, rows].astype(f32)
            low = sublane(fl) < 4
            adds = (
                (jnp.where(low, fl, 0.0), jnp.where(low, 0.0, fr)),
                (jnp.where(low, turn(fl), 0.0), jnp.where(low, 0.0, turn(fr))),
            )
            for n, (ref, out) in enumerate(((dk_ref, dkc_ref), (dv_ref, dvc_ref))):
                x = ref[b, rows]
                parts = [x[:, 8 * j : 8 * j + 8] for j in range(breadth // 8)]
                parts[0] = parts[0] + adds[n][0]
                parts[-1] = parts[-1] + adds[n][1]
                x = jnp.concatenate(parts, 1)
                if r == 0:
                    up_ref[n, b] = x.astype(bf16)
                elif r == tall - 4:
                    down_ref[n, b] = x.astype(bf16)
                else:
                    out[b, r - 4 : r] = x
    del last, height


def finish_kernel(
    core_ref, dk_ref, dv_ref, ft_ref, fb_ref, dq_ref, tok_ref, w_ref, first_ref,
    gt_ref, keep_ref, send_ref, kv_ref, all_ref,
):
    members, height, breadth, features = dk_ref.shape
    for n, ref in enumerate((dk_ref, dv_ref)):
        lanes = slice(n * features, (n + 1) * features)
        for b in range(members):
            for r in range(0, height, 4):
                x = ref[b, r : r + 4]
                if r == 0:
                    x = x + ft_ref[n, b].astype(f32)
                if r == height - 4:
                    x = x + fb_ref[n, b].astype(f32)
                kv_ref[b, r : r + 4, :, lanes] = x.astype(bf16)
    cells = members * height * breadth
    down = (((0,), (0,)), ((), ()))
    across = (((1,), (1,)), ((), ()))
    kv = kv_ref[...].reshape(cells, 2 * features)
    all_ref[:, 0:features] = first_ref[:, 0:features]
    all_ref[:, features : 3 * features] = lax.dot_general(
        tok_ref[...].reshape(cells, features), kv, down, preferred_element_type=f32
    )
    gt = lax.dot_general(
        dq_ref[...].reshape(cells, features), w_ref[:, 0:features], across, preferred_element_type=f32
    ) + lax.dot_general(kv, w_ref[:, features:], across, preferred_element_type=f32)
    gt_ref[...] = gt.astype(bf16).reshape(members, height, breadth, features)

    rows, pairs, deep, wide = keep_ref.shape
    count = 2 * pairs
    main, rest = 3 * features // count, features // count
    lane = lax.broadcasted_iota(jnp.int32, (features, wide), 1)

    def window(ref, start, end):
        base, off = start // wide * wide, start % wide
        x = ref[:, base : base + wide]
        if off:
            x = pltpu.roll(x, wide - off, 1)
        if end > base + wide:
            y = pltpu.roll(ref[:, base + wide : base + 2 * wide], wide - off, 1)
            x = jnp.where(lane < wide - off, x, y)
        return x

    def block(c):
        x = window(all_ref, main * c, main * (c + 1))
        base, off = rest * c // wide * wide, rest * c % wide
        y = first_ref[:, features + base : features + base + wide]
        if off != main:
            y = pltpu.roll(y, (main - off) % wide, 1)
        return jnp.where(lane < main, x, y).astype(bf16).reshape(rows, deep, wide)

    mine = core_ref[0] == 0
    for p in range(pairs):
        even, odd = block(2 * p), block(2 * p + 1)
        keep_ref[:, p] = jnp.where(mine, even, odd)
        send_ref[:, p] = jnp.where(mine, odd, even)


def total_kernel(x_ref, sum_ref, square_ref):
    x = jnp.sum(x_ref[...].astype(f32), 0)
    sum_ref[...] = x
    square = jnp.sum(x * x, 0, keepdims=True)
    square_ref[...] = jnp.broadcast_to(square, square_ref.shape)


def clip_kernel(x_ref, square_ref, qkv_ref, out_ref):
    total = jnp.sum(jnp.sum(square_ref[...], 0, keepdims=True), 1, keepdims=True)
    clip = jnp.minimum(1.0, max_norm / jnp.sqrt(total + tiny_square))
    x = x_ref[...] * clip
    main = qkv_ref.shape[1]
    qkv_ref[...] = x[:, 0:main]
    out_ref[...] = pltpu.roll(x, x.shape[1] - main, 1)[:, 0 : out_ref.shape[1]]


def shift(x, axis, by):
    size = lax.axis_size(axis)
    return lax.ppermute(x, axis, [(i, i + by) for i in range(size) if 0 <= i + by < size])


def body(tokens, w_qkv, w_out, q_saved, k_saved, v_saved, scale_exp, grad_out, crop_start):
    members, height, breadth, features = tokens.shape
    row_index, col_index = lax.axis_index("row"), lax.axis_index(COLS)
    frame_rows = height * lax.axis_size("row")
    frame_cols = breadth * lax.axis_size(COLS)
    place = jnp.concatenate(
        [
            jnp.stack([row_index * height, col_index * breadth]).astype(jnp.int32),
            crop_start.reshape(-1),
            jnp.array([frame_rows, frame_cols], jnp.int32),
        ]
    )
    factor = jnp.repeat(jnp.exp2(scale_exp.astype(f32)), features // HEADS, axis=3)

    up, down, left, right = call(
        edge_kernel,
        (
            shape(2, members, 4, breadth, features),
            shape(2, members, 4, breadth, features),
            shape(members, height, 8, features),
            shape(members, height, 8, features),
        ),
        (k_saved, v_saved, factor),
    )
    top, bottom = shift(down, "row", 1), shift(up, "row", -1)
    from_left, from_right = shift(right, COLS, 1), shift(left, COLS, -1)
    qs, gm, do = call(
        prepare_kernel,
        (shape(*tokens.shape),) * 3,
        (place, q_saved, grad_out, factor, w_out),
        smem=(0,),
    )
    cleft, cright = call(
        corner_kernel,
        (shape(members, 8, 8, features),) * 2,
        (top, bottom),
    )
    corner_left, corner_right = shift(cright, COLS, 1), shift(cleft, COLS, -1)
    tall = height + 8
    tile_shape = (members, breadth // 8, tall, 16, features)
    dq, first, dk, dv, dl, dr = call(
        attend_kernel,
        (
            shape(*tokens.shape),
            shape(features, 2 * features, dtype=f32),
            shape(members, tall, breadth, features, dtype=f32),
            shape(members, tall, breadth, features, dtype=f32),
            shape(members, tall, 8, features),
            shape(members, tall, 8, features),
        ),
        (place, qs, do, k_saved, v_saved, factor, gm, tokens,
         top, bottom, from_left, from_right, corner_left, corner_right),
        scratch=(
            pltpu.VMEM(tile_shape, bf16),
            pltpu.VMEM(tile_shape, bf16),
            pltpu.VMEM(tile_shape, f32),
            pltpu.VMEM(tile_shape, f32),
            pltpu.VMEM(tokens.shape, bf16),
        ),
        smem=(0,),
    )
    back_left, back_right = shift(dr, COLS, 1), shift(dl, COLS, -1)
    dkc, dvc, gup, gdown = call(
        rim_kernel,
        (
            shape(members, height, breadth, features, dtype=f32),
            shape(members, height, breadth, features, dtype=f32),
            shape(2, members, 4, breadth, features),
            shape(2, members, 4, breadth, features),
        ),
        (dk, dv, back_left, back_right),
    )
    back_top, back_bottom = shift(gdown, "row", 1), shift(gup, "row", -1)
    rows, pairs = lax.axis_size("row"), lax.axis_size("pair")
    core = lax.axis_index("core")
    deep = features // rows
    wide = 4 * features // (2 * pairs)
    grad_tokens, keep, send = call(
        finish_kernel,
        (shape(*tokens.shape), shape(rows, pairs, deep, wide), shape(rows, pairs, deep, wide)),
        (core.astype(jnp.int32).reshape(1), dkc, dvc, back_top, back_bottom, dq, tokens, w_qkv, first),
        scratch=(
            pltpu.VMEM((members, height, breadth, 2 * features), bf16),
            pltpu.VMEM((features, 3 * features), f32),
        ),
        smem=(0,),
    )
    other = lax.ppermute(send, "core", [(0, 1), (1, 0)])
    both = (keep.astype(f32) + other.astype(f32)).astype(bf16).reshape(rows * pairs, deep, wide)
    parts = lax.all_to_all(both, ("row", "pair"), 0, 0, tiled=True)
    total, square = call(
        total_kernel,
        (shape(deep, wide, dtype=f32), shape(2 * rows * pairs, wide, dtype=f32)),
        (parts,),
    )
    squares = lax.all_to_all(square, ("row", "pair", "core"), 0, 0, tiled=True)
    main = 3 * features // (2 * pairs)
    grad_qkv, grad_out_w = call(
        clip_kernel,
        (shape(deep, main, dtype=f32), shape(deep, wide - main, dtype=f32)),
        (total, squares),
    )
    return grad_tokens, grad_qkv, grad_out_w


def solution(mesh):
    rows, cols = mesh.devices.shape
    split = jax.sharding.Mesh(mesh.devices.reshape(rows, cols // 2, 2), ("row",) + COLS)
    cells = P(None, "row", COLS, None)
    return jax.shard_map(
        body,
        mesh=split,
        in_specs=(cells, P(), P(), cells, cells, cells, cells, cells, P()),
        out_specs=(cells, P("row", COLS), P("row", COLS)),
        check_vma=False,
    )
```

time: 485 us -> 163 us (0.34)
  waiting for transfers between devices: 199 us -> 19.8 us
  local copies, waits for them, and re-layouts: 163 us -> 5.52 us
  blocking collectives: 0 us -> 54.4 us
  Pallas kernels: 0 us -> 50 us
  matrix products: 43.6 us -> 0 us
  other arithmetic: 37 us -> 2.94 us
  between operations: 15.7 us -> 0.84 us
    psum x1 -> x0, waiting for transfers between devices: 163 us -> none  [body(): whole_qkv, whole_out = lax.psum((raw_qkv, raw_out), ('row', 'col'))]
    reshape x20 -> x2, local copies, waits for them, and re-layouts: 62.6 us -> 0.82 us  [the longest x1 0.74 us: body(): jnp.repeat(jnp.exp2(scale_exp.astype(f32)), features // HEADS, axis=3)]
    all_to_all x0 -> x2, blocking collectives: none -> 54.4 us  [the longest x1 37.8 us: body(): parts = lax.all_to_all(both, ('row', 'pair'), 0, 0, tiled=True)]
    pallas_call x0 -> x8, Pallas kernels: none -> 50 us  [call(): pl.pallas_call(kernel, out_shape=outs, in_specs=[SMEM if n in smem else V...]
    dot_general x16 -> x0, matrix products: 43.6 us -> none  [the longest x12 34.9 us: product(): return jnp.einsum(form, left, right, preferred_element_type=jnp.float32)]
    transpose x14 -> x0, local copies, waits for them, and re-layouts: 27.4 us -> none  [the longest x6 26.7 us: product(): return jnp.einsum(form, left, right, preferred_element_type=jnp.float32)]
    while x54 -> x0, local copies, waits for them, and re-layouts: 18.2 us -> none
    mul x9 -> x0, local copies, waits for them, and re-layouts: 17.7 us -> none  [dequantize(): mantissa.astype(jnp.float32)]
  transfers between devices with their start and end apart: 9 -> 11, of which waited for: 7 -> 6; matrix products, arithmetic and copies ran while one was open for 4% -> 0% of each run, Pallas kernels for 0% -> 4%
where the time goes in v1:
time: 163 us; the launch traced here: 162 us
  blocking collectives  54.4 us (33%)
  Pallas kernels  50 us (31%)
  starting transfers between devices  28.3 us (17%)
  waiting for transfers between devices  19.8 us (12%)
  local copies, waits for them, and re-layouts  5.52 us (3%)
  other arithmetic  2.94 us (2%)
    pallas_call x8, Pallas kernels, call(): pl.pallas_call(kernel, out_shape=outs, in_specs=[SMEM if n in smem else V...  50 us
    all_to_all x1, blocking collectives, body(): parts = lax.all_to_all(both, ('row', 'pair'), 0, 0, tiled=True)  37.8 us
    ppermute x10, starting transfers between devices, shift(): lax.ppermute(x, axis, [(i, i + by) for i in range(size) if 0 <= i + by <...  28.3 us
    ppermute x10, waiting for transfers between devices, shift(): lax.ppermute(x, axis, [(i, i + by) for i in range(size) if 0 <= i + by <...  16.9 us
    all_to_all x1, blocking collectives, body(): squares = lax.all_to_all(square, ('row', 'pair', 'core'), 0, 0, tiled=True)  16.6 us
    unnamed x25, local copies, waits for them, and re-layouts  4.61 us
  transfers between devices with their start and end apart: 11, of which 6 were waited for; matrix products, arithmetic and copies ran while one was open for 0% of the time, Pallas kernels for 4%

profile of v1, /device:TPU:1, one launch (start us, length us, event | category | flops | bytes accessed | tf_op | source)
XLA Modules:
  0.0 161.8 jit_solution(7490319730869598552)
XLA Ops:
  0.7 0.7 multiply_exponential_fusion
  1.5 0.7 reshape.22.fac_ref
  2.2 2.6 %shard_map.122 = (bf16[2,2,4,16,512]{4,3,2,1,0:T(8,128)(2,1)}, bf16[2,2,4,16,512]{4,3,2,1,0:T(8,128)(2,1)}, bf16[2,24,8,512]{3,2,1,0:T(8,128)(2,1)}, bf16[2,24,8,512]{3,2,1,0:T(8,128)(2,1)}) custom-call(bf16[2,24,16,512]{3,2,1,0:T(8,128)(2,1)} %k_ref.3, bf16[2,24,16,512]{3,2,1,0:T(8,128)(2,1)} %v_ref.3, f32[2,3,2,1536]{3,2,1,0:T(2,128)} %reshape.22.fac_ref), custom_call_target="tpu_custom_call" | custom-call | bytes 2957312 | tf_op jit(solution)/shard_map/pallas_call | solution.py:26
  4.8 4.4 %collective-permute-start = (bf16[2,2,4,16,512]{4,3,2,1,0:T(8,128)(2,1)}, bf16[2,2,4,16,512]{4,3,2,1,0:T(8,128)(2,1)S(1)}, u32[]{:S(2)}, u32[]{:S(2)}) collective-permute-start(bf16[2,2,4,16,512]{4,3,2,1,0:T(8,128)(2,1)} %get-tuple-element.32), channel_id=1, source_target_pairs={{0,16},{16,32},{32,48},{48,64},{64,80},{80,96},{96,112},{1,17},{17... | collective-permute-start | bytes 786440 | tf_op jit(solution)/shard_map/ppermute | solution.py:369
  9.2 1.3 collective-permute-start.1
  10.5 4.0 %collective-permute-start.2 = (bf16[2,24,8,512]{3,2,1,0:T(8,128)(2,1)}, bf16[2,24,8,512]{3,2,1,0:T(8,128)(2,1)S(1)}, u32[]{:S(2)}, u32[]{:S(2)}) collective-permute-start(bf16[2,24,8,512]{3,2,1,0:T(8,128)(2,1)} %get-tuple-element.34), channel_id=1, source_target_pairs={{0,1},{1,2},{2,3},{3,4},{4,5},{5,6},{6,7},{7,8},{8,9},{9,10},{10,1... | collective-permute-start | bytes 1179656 | tf_op jit(solution)/shard_map/ppermute | solution.py:369
  14.5 1.9 %collective-permute-start.3 = (bf16[2,24,8,512]{3,2,1,0:T(8,128)(2,1)}, bf16[2,24,8,512]{3,2,1,0:T(8,128)(2,1)S(1)}, u32[]{:S(2)}, u32[]{:S(2)}) collective-permute-start(bf16[2,24,8,512]{3,2,1,0:T(8,128)(2,1)} %get-tuple-element.35), channel_id=1, source_target_pairs={{1,0},{2,1},{3,2},{4,3},{5,4},{6,5},{7,6},{8,7},{9,8},{10,9},{11,1... | collective-permute-start | bytes 1179656 | tf_op jit(solution)/shard_map/ppermute | solution.py:369
  16.4 2.1 %collective-permute-done.1.bottom_ref = bf16[2,2,4,16,512]{4,3,2,1,0:T(8,128)(2,1)S(1)} collective-permute-done((bf16[2,2,4,16,512]{4,3,2,1,0:T(8,128)(2,1)}, bf16[2,2,4,16,512]{4,3,2,1,0:T(8,128)(2,1)S(1)}, u32[]{:S(2)}, u32[]{:S(2)}) %collective-permute-start.1) | collective-permute-done | bytes 262176 | tf_op jit(solution)/shard_map/ppermute | solution.py:369
  19.2 1.8 %shard_map.123 = (bf16[2,8,8,512]{3,2,1,0:T(8,128)(2,1)}, bf16[2,8,8,512]{3,2,1,0:T(8,128)(2,1)}) custom-call(bf16[2,2,4,16,512]{4,3,2,1,0:T(8,128)(2,1)} %copy-done, bf16[2,2,4,16,512]{4,3,2,1,0:T(8,128)(2,1)} %copy-done.1), custom_call_target="tpu_custom_call" | custom-call | bytes 786432 | tf_op jit(solution)/shard_map/pallas_call | solution.py:26
  21.1 4.7 %collective-permute-start.4 = (bf16[2,8,8,512]{3,2,1,0:T(8,128)(2,1)}, bf16[2,8,8,512]{3,2,1,0:T(8,128)(2,1)S(1)}, u32[]{:S(2)}, u32[]{:S(2)}) collective-permute-start(bf16[2,8,8,512]{3,2,1,0:T(8,128)(2,1)} %get-tuple-element.36), channel_id=1, source_target_pairs={{0,1},{1,2},{2,3},{3,4},{4,5},{5,6},{6,7},{7,8},{8,9},{9,10},{10,1... | collective-permute-start | bytes 393224 | tf_op jit(solution)/shard_map/ppermute | solution.py:369
  25.7 1.9 %collective-permute-start.5 = (bf16[2,8,8,512]{3,2,1,0:T(8,128)(2,1)}, bf16[2,8,8,512]{3,2,1,0:T(8,128)(2,1)S(1)}, u32[]{:S(2)}, u32[]{:S(2)}) collective-permute-start(bf16[2,8,8,512]{3,2,1,0:T(8,128)(2,1)} %get-tuple-element.37), channel_id=1, source_target_pairs={{1,0},{2,1},{3,2},{4,3},{5,4},{6,5},{7,6},{8,7},{9,8},{10,9},{11,1... | collective-permute-start | bytes 393224 | tf_op jit(solution)/shard_map/ppermute | solution.py:369
  28.4 3.9 %shard_map.121 = (bf16[2,24,16,512]{3,2,1,0:T(8,128)(2,1)}, bf16[2,24,16,512]{3,2,1,0:T(8,128)(2,1)}, bf16[2,24,16,512]{3,2,1,0:T(8,128)(2,1)}) custom-call(s32[8]{0:T(128)} %pad_add_fusion.place_ref, bf16[2,24,16,512]{3,2,1,0:T(8,128)(2,1)} %q_ref.1, bf16[2,24,16,512]{3,2,1,0:T(8,128)(2,1)} %g_ref.1, f32[2,3,2,1536]{3,2,1,0:T(2,128)} %reshape.22.fac_ref, ...), custom_call_target="tpu_custom_call" | custom-call | bytes 4530208 | tf_op jit(solution)/shard_map/pallas_call | solution.py:26
  33.2 26.3 %shard_map.124 = (bf16[2,24,16,512]{3,2,1,0:T(8,128)(2,1)}, f32[512,1024]{1,0:T(8,128)}, f32[2,32,16,512]{3,2,1,0:T(8,128)}, f32[2,32,16,512]{3,2,1,0:T(8,128)},...) custom-call(s32[8]{0:T(128)} %pad_add_fusion.place_ref, ...), custom_call_target="tpu_custom_call" | custom-call | bytes 14491680 | tf_op jit(solution)/shard_map/pallas_call | solution.py:26
  59.6 3.6 %collective-permute-start.6 = (bf16[2,32,8,512]{3,2,1,0:T(8,128)(2,1)}, bf16[2,32,8,512]{3,2,1,0:T(8,128)(2,1)S(1)}, u32[]{:S(2)}, u32[]{:S(2)}) collective-permute-start(bf16[2,32,8,512]{3,2,1,0:T(8,128)(2,1)} %get-tuple-element.40), channel_id=1, source_target_pairs={{0,1},{1,2},{2,3},{3,4},{4,5},{5,6},{6,7},{7,8},{8,9},{9,10},{10,1... | collective-permute-start | bytes 1572872 | tf_op jit(solution)/shard_map/ppermute | solution.py:369
  63.2 1.9 %collective-permute-start.7 = (bf16[2,32,8,512]{3,2,1,0:T(8,128)(2,1)}, bf16[2,32,8,512]{3,2,1,0:T(8,128)(2,1)S(1)}, u32[]{:S(2)}, u32[]{:S(2)}) collective-permute-start(bf16[2,32,8,512]{3,2,1,0:T(8,128)(2,1)} %get-tuple-element.41), channel_id=1, source_target_pairs={{1,0},{2,1},{3,2},{4,3},{5,4},{6,5},{7,6},{8,7},{9,8},{10,9},{11,1... | collective-permute-start | bytes 1572872 | tf_op jit(solution)/shard_map/ppermute | solution.py:369
  65.2 4.5 %collective-permute-done.6.fl_ref = bf16[2,32,8,512]{3,2,1,0:T(8,128)(2,1)S(1)} collective-permute-done((bf16[2,32,8,512]{3,2,1,0:T(8,128)(2,1)}, bf16[2,32,8,512]{3,2,1,0:T(8,128)(2,1)S(1)}, u32[]{:S(2)}, u32[]{:S(2)}) %collective-permute-start.6) | collective-permute-done | bytes 524320 | tf_op jit(solution)/shard_map/ppermute | solution.py:369
  69.6 4.3 %collective-permute-done.7.fr_ref = bf16[2,32,8,512]{3,2,1,0:T(8,128)(2,1)S(1)} collective-permute-done((bf16[2,32,8,512]{3,2,1,0:T(8,128)(2,1)}, bf16[2,32,8,512]{3,2,1,0:T(8,128)(2,1)S(1)}, u32[]{:S(2)}, u32[]{:S(2)}) %collective-permute-start.7) | collective-permute-done | bytes 524320 | tf_op jit(solution)/shard_map/ppermute | solution.py:369
  73.9 0.8 copy-done.3
  74.7 4.5 %shard_map.125 = (f32[2,24,16,512]{3,2,1,0:T(8,128)}, f32[2,24,16,512]{3,2,1,0:T(8,128)}, bf16[2,2,4,16,512]{4,3,2,1,0:T(8,128)(2,1)}, bf16[2,2,4,16,512]{4,3,2,1,0:T(8,128)(2,1)}) custom-call(f32[2,32,16,512]{3,2,1,0:T(8,128)} %get-tuple-element.38.dk_ref, f32[2,32,16,512]{3,2,1,0:T(8,128)} %get-tuple-element.39.dv_ref, bf16[2,32,8,512]{3,2,1,0:T(8,128)(2,1)} %copy-done.2, ...), custom_call_target="tpu_custom_call" | custom-call | bytes 8912896 | tf_op jit(solution)/shard_map/pallas_call | solution.py:26
  79.2 3.4 %collective-permute-start.8 = (bf16[2,2,4,16,512]{4,3,2,1,0:T(8,128)(2,1)}, bf16[2,2,4,16,512]{4,3,2,1,0:T(8,128)(2,1)S(1)}, u32[]{:S(2)}, u32[]{:S(2)}) collective-permute-start(bf16[2,2,4,16,512]{4,3,2,1,0:T(8,128)(2,1)} %get-tuple-element.44), channel_id=1, source_target_pairs={{0,16},{16,32},{32,48},{48,64},{64,80},{80,96},{96,112},{1,17},{17... | collective-permute-start | bytes 786440 | tf_op jit(solution)/shard_map/ppermute | solution.py:369
  82.6 1.3 collective-permute-start.9
  83.9 2.3 %collective-permute-done.8.ft_ref = bf16[2,2,4,16,512]{4,3,2,1,0:T(8,128)(2,1)S(1)} collective-permute-done((bf16[2,2,4,16,512]{4,3,2,1,0:T(8,128)(2,1)}, bf16[2,2,4,16,512]{4,3,2,1,0:T(8,128)(2,1)S(1)}, u32[]{:S(2)}, u32[]{:S(2)}) %collective-permute-start.8) | collective-permute-done | bytes 262176 | tf_op jit(solution)/shard_map/ppermute | solution.py:369
  86.2 3.7 %collective-permute-done.9.fb_ref = bf16[2,2,4,16,512]{4,3,2,1,0:T(8,128)(2,1)S(1)} collective-permute-done((bf16[2,2,4,16,512]{4,3,2,1,0:T(8,128)(2,1)}, bf16[2,2,4,16,512]{4,3,2,1,0:T(8,128)(2,1)S(1)}, u32[]{:S(2)}, u32[]{:S(2)}) %collective-permute-start.9) | collective-permute-done | bytes 262176 | tf_op jit(solution)/shard_map/ppermute | solution.py:369
  89.9 0.7 copy-done.7
  90.7 7.1 %shard_map.126 = (bf16[2,24,16,512]{3,2,1,0:T(8,128)(2,1)}, bf16[8,8,64,128]{3,2,1,0:T(8,128)(2,1)}, bf16[8,8,64,128]{3,2,1,0:T(8,128)(2,1)}) custom-call(s32[1]{0:T(128)} %bitcast.core_ref, f32[2,24,16,512]{3,2,1,0:T(8,128)} %get-tuple-element.42.dk_ref, f32[2,24,16,512]{3,2,1,0:T(8,128)} %get-tuple-element.43.dv_ref, ...), custom_call_target="tpu_custom_call" | custom-call | bytes 11796484 | tf_op jit(solution)/shard_map/pallas_call | solution.py:26
  97.8 2.9 %collective-permute-done.10 = bf16[8,8,64,128]{3,2,1,0:T(8,128)(2,1)S(1)} collective-permute-done((bf16[8,8,64,128]{3,2,1,0:T(8,128)(2,1)}, bf16[8,8,64,128]{3,2,1,0:T(8,128)(2,1)S(1)}, u32[]{:S(2)}, u32[]{:S(2)}) %collective-permute-start.10) | collective-permute-done | bytes 1048608 | tf_op jit(solution)/shard_map/ppermute | solution.py:459
  100.7 1.6 %add_convert_fusion = bf16[8,8,64,128]{3,2,1,0:T(8,128)(2,1)S(1)} fusion(bf16[8,8,64,128]{3,2,1,0:T(8,128)(2,1)S(1)} %collective-permute-done.10, bf16[8,8,64,128]{3,2,1,0:T(8,128)(2,1)} %get-tuple-element.49), kind=kLoop, calls=%fused_computation | loop fusion | flops 2097152 | bytes 3145728 | tf_op jit(solution)/shard_map/convert_element_type | solution.py:460
  102.3 37.8 %all_to_all.16.x_ref = bf16[64,64,128]{2,1,0:T(8,128)(2,1)} all-to-all(bf16[64,64,128]{2,1,0:T(8,128)(2,1)S(1)} %bitcast.10), channel_id=1, replica_groups=mesh['row'=8,'pair'=8,'core'=2] {'row','pair'}, dimensions={0} | all-to-all | bytes 2097152 | tf_op jit(solution)/shard_map/all_to_all | solution.py:461
  140.0 2.0 %shard_map.127 = (f32[64,128]{1,0:T(8,128)}, f32[128,128]{1,0:T(8,128)}) custom-call(bf16[64,64,128]{2,1,0:T(8,128)(2,1)} %all_to_all.16.x_ref), custom_call_target="tpu_custom_call" | custom-call | bytes 1146880 | tf_op jit(solution)/shard_map/pallas_call | solution.py:26
  142.1 16.6 %all_to_all.17 = f32[128,1,128]{2,1,0:T(1,128)} all-to-all(f32[128,1,128]{2,1,0:T(1,128)} %bitcast.12), channel_id=1, replica_groups=mesh['row'=8,'pair'=8,'core'=2] {'row','pair','core'}, dimensions={0} | all-to-all | bytes 131072 | tf_op jit(solution)/shard_map/all_to_all | solution.py:467
  158.7 1.7 %shard_map.128 = (f32[64,96]{1,0:T(8,128)}, f32[64,32]{1,0:T(8,128)}) custom-call(f32[64,128]{1,0:T(8,128)} %get-tuple-element.51.x_ref, f32[128,128]{1,0:T(8,128)} %bitcast.11), custom_call_target="tpu_custom_call" | custom-call | bytes 131072 | tf_op jit(solution)/shard_map/pallas_call | solution.py:26
  160.4 1.4 copy.15
  (31 shorter events, 2.5 us)
Async XLA Ops:
  0.6 27.1 %copy-start.10 = (s32[2]{0:T(128)S(1)}, s32[2]{0:T(128)}, u32[]{:S(2)}) copy-start(s32[2]{0:T(128)} %constant.22.clone) | copy-start | bytes 28
  0.6 27.0 %copy-start.11 = (s32[2,2]{1,0:T(2,128)S(1)}, s32[2,2]{1,0:T(2,128)}, u32[]{:S(2)}) copy-start(s32[2,2]{1,0:T(2,128)} %param.18) | copy-start | bytes 52
  4.8 11.6 %collective-permute-start = (bf16[2,2,4,16,512]{4,3,2,1,0:T(8,128)(2,1)}, bf16[2,2,4,16,512]{4,3,2,1,0:T(8,128)(2,1)S(1)}, u32[]{:S(2)}, u32[]{:S(2)}) collective-permute-start(bf16[2,2,4,16,512]{4,3,2,1,0:T(8,128)(2,1)} %get-tuple-element.32), channel_id=1, source_target_pairs={{0,16},{16,32},{32,48},{48,64},{64,80},{80,96},{96,112},{1,17},{17... | collective-permute-start | bytes 786440 | tf_op jit(solution)/shard_map/ppermute | solution.py:369
  9.2 9.3 %collective-permute-start.1 = (bf16[2,2,4,16,512]{4,3,2,1,0:T(8,128)(2,1)}, bf16[2,2,4,16,512]{4,3,2,1,0:T(8,128)(2,1)S(1)}, u32[]{:S(2)}, u32[]{:S(2)}) collective-permute-start(bf16[2,2,4,16,512]{4,3,2,1,0:T(8,128)(2,1)} %get-tuple-element.33), channel_id=1, source_target_pairs={{16,0},{32,16},{48,32},{64,48},{80,64},{96,80},{112,96},{17,1},{33... | collective-permute-start | bytes 786440 | tf_op jit(solution)/shard_map/ppermute | solution.py:369
  10.5 21.8 %collective-permute-start.2 = (bf16[2,24,8,512]{3,2,1,0:T(8,128)(2,1)}, bf16[2,24,8,512]{3,2,1,0:T(8,128)(2,1)S(1)}, u32[]{:S(2)}, u32[]{:S(2)}) collective-permute-start(bf16[2,24,8,512]{3,2,1,0:T(8,128)(2,1)} %get-tuple-element.34), channel_id=1, source_target_pairs={{0,1},{1,2},{2,3},{3,4},{4,5},{5,6},{6,7},{7,8},{8,9},{9,10},{10,1... | collective-permute-start | bytes 1179656 | tf_op jit(solution)/shard_map/ppermute | solution.py:369
  14.5 17.8 %collective-permute-start.3 = (bf16[2,24,8,512]{3,2,1,0:T(8,128)(2,1)}, bf16[2,24,8,512]{3,2,1,0:T(8,128)(2,1)S(1)}, u32[]{:S(2)}, u32[]{:S(2)}) collective-permute-start(bf16[2,24,8,512]{3,2,1,0:T(8,128)(2,1)} %get-tuple-element.35), channel_id=1, source_target_pairs={{1,0},{2,1},{3,2},{4,3},{5,4},{6,5},{7,6},{8,7},{9,8},{10,9},{11,1... | collective-permute-start | bytes 1179656 | tf_op jit(solution)/shard_map/ppermute | solution.py:369
  16.4 2.1 %copy-start = (bf16[2,2,4,16,512]{4,3,2,1,0:T(8,128)(2,1)}, bf16[2,2,4,16,512]{4,3,2,1,0:T(8,128)(2,1)S(1)}, u32[]{:S(2)}) copy-start(bf16[2,2,4,16,512]{4,3,2,1,0:T(8,128)(2,1)S(1)} %collective-permute-done.top_ref) | copy-start | bytes 786436
  18.5 0.7 copy-start.1
  21.1 11.2 %collective-permute-start.4 = (bf16[2,8,8,512]{3,2,1,0:T(8,128)(2,1)}, bf16[2,8,8,512]{3,2,1,0:T(8,128)(2,1)S(1)}, u32[]{:S(2)}, u32[]{:S(2)}) collective-permute-start(bf16[2,8,8,512]{3,2,1,0:T(8,128)(2,1)} %get-tuple-element.36), channel_id=1, source_target_pairs={{0,1},{1,2},{2,3},{3,4},{4,5},{5,6},{6,7},{7,8},{8,9},{9,10},{10,1... | collective-permute-start | bytes 393224 | tf_op jit(solution)/shard_map/ppermute | solution.py:369
  25.7 6.5 %collective-permute-start.5 = (bf16[2,8,8,512]{3,2,1,0:T(8,128)(2,1)}, bf16[2,8,8,512]{3,2,1,0:T(8,128)(2,1)S(1)}, u32[]{:S(2)}, u32[]{:S(2)}) collective-permute-start(bf16[2,8,8,512]{3,2,1,0:T(8,128)(2,1)} %get-tuple-element.37), channel_id=1, source_target_pairs={{1,0},{2,1},{3,2},{4,3},{5,4},{6,5},{7,6},{8,7},{9,8},{10,9},{11,1... | collective-permute-start | bytes 393224 | tf_op jit(solution)/shard_map/ppermute | solution.py:369
  32.3 0.7 copy-start.8
  32.3 0.7 copy-start.9
  32.3 0.8 copy-start.4
  32.3 0.9 copy-start.5
  59.6 10.1 %collective-permute-start.6 = (bf16[2,32,8,512]{3,2,1,0:T(8,128)(2,1)}, bf16[2,32,8,512]{3,2,1,0:T(8,128)(2,1)S(1)}, u32[]{:S(2)}, u32[]{:S(2)}) collective-permute-start(bf16[2,32,8,512]{3,2,1,0:T(8,128)(2,1)} %get-tuple-element.40), channel_id=1, source_target_pairs={{0,1},{1,2},{2,3},{3,4},{4,5},{5,6},{6,7},{7,8},{8,9},{9,10},{10,1... | collective-permute-start | bytes 1572872 | tf_op jit(solution)/shard_map/ppermute | solution.py:369
  63.2 10.7 %collective-permute-start.7 = (bf16[2,32,8,512]{3,2,1,0:T(8,128)(2,1)}, bf16[2,32,8,512]{3,2,1,0:T(8,128)(2,1)S(1)}, u32[]{:S(2)}, u32[]{:S(2)}) collective-permute-start(bf16[2,32,8,512]{3,2,1,0:T(8,128)(2,1)} %get-tuple-element.41), channel_id=1, source_target_pairs={{1,0},{2,1},{3,2},{4,3},{5,4},{6,5},{7,6},{8,7},{9,8},{10,9},{11,1... | collective-permute-start | bytes 1572872 | tf_op jit(solution)/shard_map/ppermute | solution.py:369
  69.6 4.3 %copy-start.2 = (bf16[2,32,8,512]{3,2,1,0:T(8,128)(2,1)}, bf16[2,32,8,512]{3,2,1,0:T(8,128)(2,1)S(1)}, u32[]{:S(2)}) copy-start(bf16[2,32,8,512]{3,2,1,0:T(8,128)(2,1)S(1)} %collective-permute-done.6.fl_ref) | copy-start | bytes 1572868
  73.9 0.8 copy-start.3
  79.2 7.0 %collective-permute-start.8 = (bf16[2,2,4,16,512]{4,3,2,1,0:T(8,128)(2,1)}, bf16[2,2,4,16,512]{4,3,2,1,0:T(8,128)(2,1)S(1)}, u32[]{:S(2)}, u32[]{:S(2)}) collective-permute-start(bf16[2,2,4,16,512]{4,3,2,1,0:T(8,128)(2,1)} %get-tuple-element.44), channel_id=1, source_target_pairs={{0,16},{16,32},{32,48},{48,64},{64,80},{80,96},{96,112},{1,17},{17... | collective-permute-start | bytes 786440 | tf_op jit(solution)/shard_map/ppermute | solution.py:369
  82.6 7.3 %collective-permute-start.9 = (bf16[2,2,4,16,512]{4,3,2,1,0:T(8,128)(2,1)}, bf16[2,2,4,16,512]{4,3,2,1,0:T(8,128)(2,1)S(1)}, u32[]{:S(2)}, u32[]{:S(2)}) collective-permute-start(bf16[2,2,4,16,512]{4,3,2,1,0:T(8,128)(2,1)} %get-tuple-element.45), channel_id=1, source_target_pairs={{16,0},{32,16},{48,32},{64,48},{80,64},{96,80},{112,96},{17,1},{33... | collective-permute-start | bytes 786440 | tf_op jit(solution)/shard_map/ppermute | solution.py:369
  86.2 3.7 %copy-start.6 = (bf16[2,2,4,16,512]{4,3,2,1,0:T(8,128)(2,1)}, bf16[2,2,4,16,512]{4,3,2,1,0:T(8,128)(2,1)S(1)}, u32[]{:S(2)}) copy-start(bf16[2,2,4,16,512]{4,3,2,1,0:T(8,128)(2,1)S(1)} %collective-permute-done.8.ft_ref) | copy-start | bytes 786436
  89.9 0.7 copy-start.7
  97.8 2.9 %collective-permute-start.10 = (bf16[8,8,64,128]{3,2,1,0:T(8,128)(2,1)}, bf16[8,8,64,128]{3,2,1,0:T(8,128)(2,1)S(1)}, u32[]{:S(2)}, u32[]{:S(2)}) collective-permute-start(bf16[8,8,64,128]{3,2,1,0:T(8,128)(2,1)} %get-tuple-element.50), channel_id=1, source_target_pairs={{0,1},{1,0},{2,3},{3,2},{4,5},{5,4},{6,7},{7,6},{8,9},{9,8},{10,11... | collective-permute-start | bytes 3145736 | tf_op jit(solution)/shard_map/ppermute | solution.py:459

commit v2 on v1

v2 whole, which is shorter than its diff:
```python
import jax
import jax.numpy as jnp
from jax import lax
from jax.experimental import pallas as pl
from jax.experimental.pallas import tpu as pltpu
from jax.sharding import PartitionSpec as P

HEADS = 8
RADIUS = 4
BLOCK = 8
GROUP = 4

max_norm = 1000.0
masked_score = -1e30
tiny_square = 1e-06

f32 = jnp.float32
bf16 = jnp.bfloat16
VMEM = pl.BlockSpec(memory_space=pltpu.VMEM)
COLS = ("pair", "core")
ANY = pl.BlockSpec(memory_space=pl.ANY)
SMEM = pl.BlockSpec(memory_space=pltpu.SMEM)


def call(kernel, outs, ins, scratch=(), smem=(), far=(), flops=0, limit=16 << 20):
    moved = sum(a.size * a.dtype.itemsize for a in list(ins) + jax.tree.leaves(outs))
    return pl.pallas_call(
        kernel,
        out_shape=outs,
        in_specs=[SMEM if n in smem else ANY if n in far else VMEM for n in range(len(ins))],
        out_specs=jax.tree.map(lambda _: VMEM, outs),
        scratch_shapes=list(scratch),
        compiler_params=pltpu.CompilerParams(vmem_limit_bytes=limit),
        cost_estimate=pl.CostEstimate(
            flops=flops, bytes_accessed=moved, transcendentals=0
        ),
    )(*ins)


def shape(*dims, dtype=bf16):
    return jax.ShapeDtypeStruct(dims, dtype)


def turn(x):
    return pltpu.roll(x, 4, 1)


def lower(x):
    return lax.broadcasted_iota(jnp.int32, x.shape, 1) < 4


def fetch(copies, sem):
    started = [pltpu.make_async_copy(src, dst, sem.at[n]) for n, (src, dst) in enumerate(copies)]
    for c in started:
        c.start()
    for c in started:
        c.wait()


def block_of(ref, fac_ref, part, b, i, j, rows, features):
    factor = fac_ref[b, i, j : j + 1, part * features : (part + 1) * features]
    return ref[b, rows, 8 * j : 8 * j + 8, :].astype(f32) * factor[None]


def edge_kernel(scale_ref, k_ref, v_ref, tok_ref, fac_ref, left_ref, right_ref):
    members, height, breadth, features = k_ref.shape
    last = breadth // 8 - 1
    count = scale_ref.shape[3]
    per = 3 * features // count
    hot = (
        lax.broadcasted_iota(jnp.int32, (count, 3 * features), 0)
        == lax.broadcasted_iota(jnp.int32, (count, 3 * features), 1) // per
    ).astype(f32).astype(bf16)
    for b in range(members):
        for i in range(height // 8):
            factor = jnp.exp2(scale_ref[b, i].astype(f32)).astype(bf16)
            fac_ref[b, i] = jnp.dot(factor, hot, preferred_element_type=f32)
    half = height // 2
    for b in range(members):
        for i in range(height // 8):
            rows = slice(8 * i, 8 * i + 8)
            k0 = block_of(k_ref, fac_ref, 1, b, i, 0, rows, features)
            v0 = block_of(v_ref, fac_ref, 2, b, i, 0, rows, features)
            k1 = block_of(k_ref, fac_ref, 1, b, i, last, rows, features)
            v1 = block_of(v_ref, fac_ref, 2, b, i, last, rows, features)
            low = lower(k0)
            left_ref[b, rows] = jnp.where(low, k0, turn(v0)).astype(bf16)
            right_ref[b, rows] = jnp.where(low, turn(v1), k1).astype(bf16)
        for r in range(0, half, 4):
            here, there = slice(r, r + 4), slice(half + r, half + r + 4)
            out = slice(height + r, height + r + 4)
            x0 = tok_ref[b, here, 0:8].astype(f32)
            y0 = tok_ref[b, there, 0:8].astype(f32)
            x1 = tok_ref[b, here, breadth - 8 :].astype(f32)
            y1 = tok_ref[b, there, breadth - 8 :].astype(f32)
            low = lower(x0)
            left_ref[b, out] = jnp.where(low, x0, turn(y0)).astype(bf16)
            right_ref[b, out] = jnp.where(low, turn(y1), x1).astype(bf16)


def rims_of(left, right):
    low = lower(left)
    return jnp.where(low, right, left), turn(jnp.where(low, left, right))


def token_rims(left, right):
    low = lower(left)
    return jnp.where(low, right, left), turn(jnp.where(low, left, right))


def strip_kernel(k_ref, v_ref, tok_ref, fac_ref, fl_ref, fr_ref, up_ref, down_ref, k_buf, v_buf, t_buf, sem):
    members, height, breadth, features = k_ref.shape
    tiles, half = breadth // 8, height // 2
    copies = []
    for ref, buf in ((k_ref, k_buf), (v_ref, v_buf), (tok_ref, t_buf)):
        copies.append((ref.at[:, 0:4], buf.at[0]))
        copies.append((ref.at[:, height - 4 : height], buf.at[1]))
    fetch(copies, sem)
    for n, out in enumerate((up_ref, down_ref)):
        row = 0 if n == 0 else height - 4
        i = row // 8
        for b in range(members):
            rim_k, rim_v = rims_of(
                fl_ref[b, row : row + 4].astype(f32), fr_ref[b, row : row + 4].astype(f32)
            )
            packed = height + (row if n == 0 else row - half)
            rim_t = token_rims(
                fl_ref[b, packed : packed + 4].astype(f32), fr_ref[b, packed : packed + 4].astype(f32)
            )[n]
            for m, (buf, rim) in enumerate(((k_buf, rim_k), (v_buf, rim_v))):
                parts = [
                    buf[n, b, :, 8 * j : 8 * j + 8].astype(f32)
                    * fac_ref[b, i, j : j + 1, (m + 1) * features : (m + 2) * features][None]
                    for j in range(tiles)
                ]
                out[m, b] = jnp.concatenate(parts + [rim], 1).astype(bf16)
            out[2, b] = jnp.concatenate([t_buf[n, b].astype(f32), rim_t], 1).astype(bf16)


def prepare_kernel(crop_ref, q_ref, g_ref, fac_ref, w_ref, qs_ref, gm_ref, do_ref):
    members, height, breadth, features = q_ref.shape
    tiles = breadth // 8
    row0 = lax.axis_index("row") * height
    col0 = (lax.axis_index("pair") * 2 + lax.axis_index("core")) * breadth
    for b in range(members):
        for i in range(height // 8):
            rows = slice(8 * i, 8 * i + 8)
            parts = [block_of(q_ref, fac_ref, 0, b, i, j, rows, features) for j in range(tiles)]
            qs_ref[b, rows] = (jnp.concatenate(parts, 1) * 0.125).astype(bf16)
            g = g_ref[b, rows].astype(f32)
            r = lax.broadcasted_iota(jnp.int32, g.shape, 0) + (8 * i + row0)
            c = lax.broadcasted_iota(jnp.int32, g.shape, 1) + col0
            keep = (r >= crop_ref[b, 0]) & (c >= crop_ref[b, 1])
            gm = jnp.where(keep, g, 0.0).astype(bf16)
            gm_ref[b, rows] = gm
            do = lax.dot_general(
                gm.reshape(8 * breadth, features), w_ref[...], (((1,), (1,)), ((), ())),
                preferred_element_type=f32,
            )
            do_ref[b, rows] = do.astype(bf16).reshape(8, breadth, features)


def main_kernel(
    qs_ref, do_ref, k_ref, v_ref, fac_ref, gm_ref, tok_ref,
    fl_ref, fr_ref, top_ref, bottom_ref,
    keep_ref, send_ref, dq_ref, kv_ref,
    kt_ref, vt_ref, dkt_ref, dvt_ref, o_ref, tp_ref, all_ref,
):
    members, height, breadth, features = qs_ref.shape
    tall = height + 8
    strips, tiles = height // 8, breadth // 8
    heads_lanes = features // HEADS
    wide = GROUP * heads_lanes
    groups = HEADS // GROUP
    row0 = lax.axis_index("row") * height
    col0 = (lax.axis_index("pair") * 2 + lax.axis_index("core")) * breadth
    frame_rows = height * lax.axis_size("row")
    frame_cols = breadth * lax.axis_size("pair") * 2

    def put(ref, b, rows, blocks, rim):
        low = lower(rim)
        for t in range(tiles):
            before = rim if t == 0 else blocks[t - 1]
            after = rim if t == tiles - 1 else blocks[t + 1]
            ref[b, t, rows] = jnp.concatenate([blocks[t], jnp.where(low, after, before)], 1).astype(bf16)

    for b in range(members):
        for n, ref in enumerate((top_ref, bottom_ref)):
            halo = slice(0, 4) if n == 0 else slice(height + 4, height + 8)
            for m, out in enumerate((kt_ref, vt_ref)):
                parts = [ref[m, b, :, 8 * j : 8 * j + 8].astype(f32) for j in range(tiles + 1)]
                put(out, b, halo, parts[:tiles], parts[tiles])
            tp_ref[b, halo] = ref[2, b]
        for i in range(strips):
            rows = slice(8 * i, 8 * i + 8)
            rim_k, rim_v = rims_of(fl_ref[b, rows].astype(f32), fr_ref[b, rows].astype(f32))
            for m, (ref, out, rim) in enumerate(((k_ref, kt_ref, rim_k), (v_ref, vt_ref, rim_v))):
                blocks = [block_of(ref, fac_ref, m + 1, b, i, j, rows, features) for j in range(tiles)]
                put(out, b, slice(8 * i + 4, 8 * i + 12), blocks, rim)
        half = height // 2
        for r in range(0, half, 4):
            packed = slice(height + r, height + r + 4)
            pair = token_rims(fl_ref[b, packed].astype(f32), fr_ref[b, packed].astype(f32))
            for rim, row in zip(pair, (r, half + r)):
                own = tok_ref[b, row : row + 4].astype(f32)
                tp_ref[b, row + 4 : row + 8] = jnp.concatenate([own, rim], 1).astype(bf16)
        for t in range(tiles):
            dkt_ref[b, t, 0:8] = jnp.zeros((8, 16, features), f32)
            dvt_ref[b, t, 0:8] = jnp.zeros((8, 16, features), f32)
        dq_ref[b, 0:4] = jnp.zeros((4, breadth, features), bf16)
        dq_ref[b, tall - 4 : tall] = jnp.zeros((4, breadth, features), bf16)

    lane = lax.broadcasted_iota(jnp.int32, (1, wide), 1) // heads_lanes
    head_mask = [(lane == h).astype(f32).astype(bf16) for h in range(GROUP)]
    first = lax.broadcasted_iota(jnp.int32, (64, 2 * heads_lanes), 1) < heads_lanes

    def spread(x):
        return jnp.concatenate([x * m for m in head_mask], 0)

    def gather(x):
        parts = []
        for n in range(GROUP // 2):
            lanes = slice(128 * n, 128 * n + 128)
            parts.append(jnp.where(first, x[128 * n : 128 * n + 64, lanes], x[128 * n + 64 : 128 * n + 128, lanes]))
        return jnp.concatenate(parts, 1)

    def bias_of(i, t):
        qn = lax.broadcasted_iota(jnp.int32, (64, 256), 0)
        kn = lax.broadcasted_iota(jnp.int32, (64, 256), 1)
        qr, qc = qn // 8, qn % 8
        kr, ks = kn // 16, kn % 16
        kc = jnp.where(ks < 12, ks, ks - 16)
        row = row0 + 8 * i - 4 + kr
        col = col0 + 8 * t + kc
        ok = (kr >= qr) & (kr <= qr + 8) & (kc >= qc - 4) & (kc <= qc + 4)
        ok &= (row >= 0) & (row < frame_rows) & (col >= 0) & (col < frame_cols)
        return jnp.where(ok, 0.0, masked_score)

    across = (((1,), (1,)), ((), ()))
    down = (((0,), (0,)), ((), ()))

    def step(n, _):
        b, i = n // strips, n % strips
        rows = pl.ds(8 * i, 8)
        q8 = qs_ref[b, rows].astype(f32)
        g8 = do_ref[b, rows].astype(f32)
        outs, grads = [], []
        for t in range(tiles):
            bias4 = jnp.concatenate([bias_of(i, t)] * GROUP, 0)
            q64 = q8[:, 8 * t : 8 * t + 8].reshape(64, features).astype(bf16)
            g64 = g8[:, 8 * t : 8 * t + 8].reshape(64, features).astype(bf16)
            keys = pl.ds(8 * i, 16)
            ot, dqt = [], []
            for g in range(groups):
                lanes = slice(g * wide, (g + 1) * wide)
                qx, gx = spread(q64[:, lanes]), spread(g64[:, lanes])
                k = kt_ref[b, t, keys, :, lanes].reshape(256, wide)
                v = vt_ref[b, t, keys, :, lanes].reshape(256, wide)
                s = lax.dot_general(qx, k, across, preferred_element_type=f32) + bias4
                w = jnp.exp(s - jnp.max(s, 1, keepdims=True))
                p = w * (1.0 / jnp.sum(w, 1, keepdims=True))
                ph = p.astype(bf16)
                o = jnp.dot(ph, v, preferred_element_type=f32).astype(bf16).astype(f32)
                delta = jnp.sum(o * gx.astype(f32), 1, keepdims=True)
                dp = lax.dot_general(gx, v, across, preferred_element_type=f32)
                ds = (p * (dp - delta)).astype(bf16)
                dq = jnp.dot(ds, k, preferred_element_type=f32)
                dk = lax.dot_general(ds, qx, down, preferred_element_type=f32).reshape(16, 16, wide)
                dv = lax.dot_general(ph, gx, down, preferred_element_type=f32).reshape(16, 16, wide)
                ot.append(gather(o))
                dqt.append(gather(dq) * 0.125)
                for ref, x in ((dkt_ref, dk), (dvt_ref, dv)):
                    ref[b, t, rows, :, lanes] = ref[b, t, rows, :, lanes] + x[0:8]
                    ref[b, t, pl.ds(8 * i + 8, 8), :, lanes] = x[8:16]
            outs.append(jnp.concatenate(ot, 1).reshape(8, 8, features))
            grads.append(jnp.concatenate(dqt, 1).reshape(8, 8, features))
        o_ref[b, rows] = jnp.concatenate(outs, 1).astype(bf16)
        dq_ref[b, pl.ds(8 * i + 4, 8)] = jnp.concatenate(grads, 1).astype(bf16)
        return 0

    lax.fori_loop(0, members * strips, step, 0)

    for b in range(members):
        for r in range(0, tall, 8):
            rows = slice(r, r + 8)
            for m, ref in enumerate((dkt_ref, dvt_ref)):
                rim = [ref[b, t, rows, 8:16] for t in range(tiles)]
                low = lower(rim[0])
                own = []
                for t in range(tiles):
                    x = ref[b, t, rows, 0:8]
                    if t > 0:
                        x = x + jnp.where(low, rim[t - 1], 0.0)
                    if t < tiles - 1:
                        x = x + jnp.where(low, 0.0, rim[t + 1])
                    own.append(x)
                own.append(jnp.where(low, rim[tiles - 1], rim[0]))
                kv_ref[b, rows, :, m * features : (m + 1) * features] = jnp.concatenate(own, 1).astype(bf16)

    cells = members * height * breadth
    padded = members * tall * (breadth + 8)
    for b in range(members):
        x = lax.dot_general(
            tok_ref[b].reshape(cells // members, features),
            dq_ref[b, 4 : tall - 4].reshape(cells // members, features), down,
            preferred_element_type=f32,
        )
        y = lax.dot_general(
            o_ref[b].reshape(cells // members, features), gm_ref[b].reshape(cells // members, features), down,
            preferred_element_type=f32,
        )
        if b:
            x, y = x + all_ref[:, 0:features], y + all_ref[:, 3 * features :]
        all_ref[:, 0:features] = x
        all_ref[:, 3 * features :] = y
    kv = kv_ref[...].reshape(padded, 2 * features)
    all_ref[:, features : 3 * features] = lax.dot_general(
        tp_ref[...].reshape(padded, features), kv, down, preferred_element_type=f32
    )

    deep_rows, pairs, deep, broad = keep_ref.shape
    count = 2 * pairs
    main, rest = 3 * features // count, features // count
    lanes = lax.broadcasted_iota(jnp.int32, (features, broad), 1)

    def window(start, end):
        base, off = start // broad * broad, start % broad
        x = all_ref[:, base : base + broad]
        if off:
            x = pltpu.roll(x, broad - off, 1)
        if end > base + broad:
            y = pltpu.roll(all_ref[:, base + broad : base + 2 * broad], broad - off, 1)
            x = jnp.where(lanes < broad - off, x, y)
        return x

    def block(c):
        x = window(main * c, main * (c + 1))
        base, off = 3 * features + rest * c // broad * broad, rest * c % broad
        y = all_ref[:, base : base + broad]
        if off != main:
            y = pltpu.roll(y, (main - off) % broad, 1)
        return jnp.where(lanes < main, x, y).astype(bf16).reshape(deep_rows, deep, broad)

    mine = lax.axis_index("core") == 0
    for p in range(pairs):
        even, odd = block(2 * p), block(2 * p + 1)
        keep_ref[:, p] = jnp.where(mine, even, odd)
        send_ref[:, p] = jnp.where(mine, odd, even)


def token_kernel(kv_ref, dq_ref, w_ref, gt_ref, left_ref, right_ref):
    members, tall, breadth, features = dq_ref.shape
    across = (((1,), (1,)), ((), ()))
    middle = tall // 2
    for b in range(members):
        y = lax.dot_general(
            kv_ref[b].reshape(tall * (breadth + 8), 2 * features), w_ref[:, features:], across,
            preferred_element_type=f32,
        ).reshape(tall, breadth + 8, features)
        z = lax.dot_general(
            dq_ref[b].reshape(tall * breadth, features), w_ref[:, 0:features], across,
            preferred_element_type=f32,
        ).reshape(tall, breadth, features)
        gt_ref[b] = (y[:, 0:breadth] + z).astype(bf16)
        here, there = y[0:middle, breadth:], turn(y[middle:, breadth:])
        low = lower(here)
        right_ref[b] = jnp.where(low, here, there).astype(bf16)
        left_ref[b] = jnp.where(low, there, here).astype(bf16)


def back_rims(fl, fr):
    low = lower(fl)
    here = (jnp.where(low, fl, 0.0), jnp.where(low, 0.0, fr))
    there = (jnp.where(low, turn(fl), 0.0), jnp.where(low, 0.0, turn(fr)))
    return here, there


def plus_rims(x, rims):
    last = x.shape[1] - 8
    return jnp.concatenate([x[:, 0:8] + rims[0], x[:, 8:last], x[:, last:] + rims[1]], 1) if last > 8 else (
        jnp.concatenate([x[:, 0:8] + rims[0], x[:, 8:] + rims[1]], 1)
    )


def total_kernel(x_ref, sum_ref, square_ref):
    x = jnp.sum(x_ref[...].astype(f32), 0)
    sum_ref[...] = x
    square = jnp.sum(x * x, 0, keepdims=True)
    square_ref[...] = jnp.broadcast_to(square, square_ref.shape)


def halo_kernel(gt_ref, fl_ref, fr_ref, up_ref, down_ref):
    members, tall = gt_ref.shape[:2]
    half = tall // 2
    for b in range(members):
        here, _ = back_rims(fl_ref[b, 0:4].astype(f32), fr_ref[b, 0:4].astype(f32))
        _, there = back_rims(fl_ref[b, half - 4 : half].astype(f32), fr_ref[b, half - 4 : half].astype(f32))
        up_ref[b] = plus_rims(gt_ref[b, 0:4].astype(f32), here).astype(bf16)
        down_ref[b] = plus_rims(gt_ref[b, tall - 4 : tall].astype(f32), there).astype(bf16)


def join_kernel(gt_ref, fl_ref, fr_ref, ft_ref, fb_ref, tok_ref):
    members, height = tok_ref.shape[:2]
    half = (height + 8) // 2
    for b in range(members):
        for r in range(0, half, 4):
            pair = back_rims(fl_ref[b, r : r + 4].astype(f32), fr_ref[b, r : r + 4].astype(f32))
            for rims, row in zip(pair, (r, half + r)):
                if row == 0 or row == height + 4:
                    continue
                y = plus_rims(gt_ref[b, row : row + 4].astype(f32), rims)
                if row == 4:
                    y = y + ft_ref[b].astype(f32)
                if row == height:
                    y = y + fb_ref[b].astype(f32)
                tok_ref[b, row - 4 : row] = y.astype(bf16)


def clip_kernel(x_ref, square_ref, qkv_ref, out_ref):
    total = jnp.sum(jnp.sum(square_ref[...], 0, keepdims=True), 1, keepdims=True)
    clip = jnp.minimum(1.0, max_norm / jnp.sqrt(total + tiny_square))
    x = x_ref[...] * clip
    main = qkv_ref.shape[1]
    qkv_ref[...] = x[:, 0:main]
    out_ref[...] = x.T[main:]


def shift(x, axes, by):
    size = lax.axis_size(axes)
    return lax.ppermute(x, axes, [(i, i + by) for i in range(size) if 0 <= i + by < size])


def body(tokens, w_qkv, w_out, q_saved, k_saved, v_saved, scale_exp, grad_out, crop_start):
    members, height, breadth, features = tokens.shape
    tall = height + 8
    packed = height + height // 2
    factor, left, right = call(
        edge_kernel,
        (
            shape(*scale_exp.shape[:3], 3 * features, dtype=f32),
            shape(members, packed, 8, features),
            shape(members, packed, 8, features),
        ),
        (scale_exp, k_saved, v_saved, tokens),
    )
    from_left, from_right = shift(right, COLS, 1), shift(left, COLS, -1)
    strip = shape(3, members, 4, breadth + 8, features)
    edge_rows = pltpu.VMEM((2, members, 4, breadth, features), bf16)
    up, down = call(
        strip_kernel,
        (strip, strip),
        (k_saved, v_saved, tokens, factor, from_left, from_right),
        scratch=(edge_rows,) * 3 + (pltpu.SemaphoreType.DMA((6,)),),
        far=(0, 1, 2),
    )
    top, bottom = shift(down, "row", 1), shift(up, "row", -1)
    cells = members * height * breadth
    qs, gm, do = call(
        prepare_kernel,
        (shape(*tokens.shape),) * 3,
        (crop_start, q_saved, grad_out, factor, w_out),
        smem=(0,),
        flops=2 * cells * features * features,
    )
    rows, pairs = lax.axis_size("row"), lax.axis_size("pair")
    deep, wide = features // rows, 4 * features // (2 * pairs)
    tile_shape = (members, breadth // 8, tall, 16, features)
    keep, send, dq, kv = call(
        main_kernel,
        (
            shape(rows, pairs, deep, wide),
            shape(rows, pairs, deep, wide),
            shape(members, tall, breadth, features),
            shape(members, tall, breadth + 8, 2 * features),
        ),
        (qs, do, k_saved, v_saved, factor, gm, tokens, from_left, from_right, top, bottom),
        scratch=(
            pltpu.VMEM(tile_shape, bf16),
            pltpu.VMEM(tile_shape, bf16),
            pltpu.VMEM(tile_shape, f32),
            pltpu.VMEM(tile_shape, f32),
            pltpu.VMEM(tokens.shape, bf16),
            pltpu.VMEM((members, tall, breadth + 8, features), bf16),
            pltpu.VMEM((features, 4 * features), f32),
        ),
        flops=12 * cells * features * features,
        limit=44 << 20,
    )
    other = lax.ppermute(send, "core", [(0, 1), (1, 0)])
    both = (keep.astype(f32) + other.astype(f32)).astype(bf16).reshape(rows * pairs, deep, wide)
    parts = lax.all_to_all(both, ("row", "pair"), 0, 0, tiled=True)
    gt, left, right = call(
        token_kernel,
        (
            shape(members, tall, breadth, features),
            shape(members, tall // 2, 8, features),
            shape(members, tall // 2, 8, features),
        ),
        (kv, dq, w_qkv),
        flops=6 * cells * features * features,
        limit=24 << 20,
    )
    back_left, back_right = shift(right, COLS, 1), shift(left, COLS, -1)
    halo = shape(members, 4, breadth, features)
    up, down = call(halo_kernel, (halo, halo), (gt, back_left, back_right))
    back_top, back_bottom = shift(down, "row", 1), shift(up, "row", -1)
    grad_tokens = call(
        join_kernel, shape(*tokens.shape), (gt, back_left, back_right, back_top, back_bottom)
    )
    total, square = call(
        total_kernel,
        (shape(deep, wide, dtype=f32), shape(2 * rows * pairs, wide, dtype=f32)),
        (parts,),
    )
    squares = lax.all_to_all(square, ("row", "pair", "core"), 0, 0, tiled=True)
    main = 3 * features // (2 * pairs)
    grad_qkv, grad_w_out = call(
        clip_kernel,
        (shape(deep, main, dtype=f32), shape(wide - main, deep, dtype=f32)),
        (total, squares),
    )
    return grad_tokens, grad_qkv, grad_w_out.T


def solution(mesh):
    rows, cols = mesh.devices.shape
    split = jax.sharding.Mesh(mesh.devices.reshape(rows, cols // 2, 2), ("row",) + COLS)
    cells = P(None, "row", COLS, None)
    return jax.shard_map(
        body,
        mesh=split,
        in_specs=(cells, P(), P(), cells, cells, cells, cells, cells, P()),
        out_specs=(cells, P("row", COLS), P("row", COLS)),
        check_vma=False,
    )
```

time: 163 us -> 127 us (0.78)
  blocking collectives: 54.4 us -> 0 us
  starting transfers between devices: 28.3 us -> 50.3 us
  Pallas kernels: 50 us -> 32.2 us
  waiting for transfers between devices: 19.8 us -> 34 us
  local copies, waits for them, and re-layouts: 5.52 us -> 7.41 us
    all_to_all x2 -> x0, blocking collectives: 54.4 us -> none  [the longest x1 37.8 us: body(): parts = lax.all_to_all(both, ('row', 'pair'), 0, 0, tiled=True)]
    all_to_all x0 -> x2, starting transfers between devices: none -> 28.8 us  [the longest x1 16.8 us: body(): parts = lax.all_to_all(both, ('row', 'pair'), 0, 0, tiled=True)]
    pallas_call x8 -> x9, Pallas kernels: 50 us -> 32.2 us  [call(): pl.pallas_call(kernel, out_shape=outs, in_specs=[SMEM if n in smem else A...]
    all_to_all x0 -> x2, waiting for transfers between devices: none -> 8.31 us  [the longest x1 8.31 us: body(): squares = lax.all_to_all(square, ('row', 'pair', 'core'), 0, 0, tiled=True)]
    ppermute x10 -> x8, starting transfers between devices: 28.3 us -> 21.5 us  [shift(): lax.ppermute(x, axes, [(i, i + by) for i in range(size) if 0 <= i + by <...]
    ppermute x10 -> x8, waiting for transfers between devices: 16.9 us -> 23 us  [shift(): lax.ppermute(x, axes, [(i, i + by) for i in range(size) if 0 <= i + by <...]
    unnamed x25 -> x26, local copies, waits for them, and re-layouts: 4.61 us -> 7.41 us
  transfers between devices with their start and end apart: 11 -> 11, of which waited for: 6 -> 8; matrix products, arithmetic and copies ran while one was open for 0% -> 0% of each run, Pallas kernels for 4% -> 5%
where the time goes in v2:
time: 127 us; the launch traced here: 126 us
  starting transfers between devices  50.3 us (40%)
  waiting for transfers between devices  34 us (27%)
  Pallas kernels  32.2 us (25%)
  local copies, waits for them, and re-layouts  7.41 us (6%)
  other arithmetic  1.36 us (1%)
    pallas_call x9, Pallas kernels, call(): pl.pallas_call(kernel, out_shape=outs, in_specs=[SMEM if n in smem else A...  32.2 us
    ppermute x8, waiting for transfers between devices, shift(): lax.ppermute(x, axes, [(i, i + by) for i in range(size) if 0 <= i + by <...  23 us
    ppermute x8, starting transfers between devices, shift(): lax.ppermute(x, axes, [(i, i + by) for i in range(size) if 0 <= i + by <...  21.5 us
    all_to_all x1, starting transfers between devices, body(): parts = lax.all_to_all(both, ('row', 'pair'), 0, 0, tiled=True)  16.8 us
    all_to_all x1, starting transfers between devices, body(): squares = lax.all_to_all(square, ('row', 'pair', 'core'), 0, 0, tiled=True)  12 us
    all_to_all x1, waiting for transfers between devices, body(): squares = lax.all_to_all(square, ('row', 'pair', 'core'), 0, 0, tiled=True)  8.31 us
    unnamed x26, local copies, waits for them, and re-layouts  7.41 us
    ppermute x1, waiting for transfers between devices, body(): other = lax.ppermute(send, 'core', [(0, 1), (1, 0)])  2.66 us
  transfers between devices with their start and end apart: 11, of which 8 were waited for; matrix products, arithmetic and copies ran while one was open for 0% of the time, Pallas kernels for 5%

profile of v2, /device:TPU:1, one launch (start us, length us, event | category | flops | bytes accessed | tf_op | source)
XLA Modules:
  0.0 126.1 jit_solution(16022134588259600435)
XLA Ops:
  0.6 1.1 copy-done
  1.8 1.1 copy-done.2
  2.9 1.1 copy-done.4
  4.0 0.7 copy-done.11
  5.5 4.6 %collective-permute-start = (bf16[2,36,8,512]{3,2,1,0:T(8,128)(2,1)S(1)}, bf16[2,36,8,512]{3,2,1,0:T(8,128)(2,1)S(1)}, u32[]{:S(2)}, u32[]{:S(2)}) collective-permute-start(bf16[2,36,8,512]{3,2,1,0:T(8,128)(2,1)S(1)} %get-tuple-element.28), channel_id=1, source_target_pairs={{0,1},{1,2},{2,3},{3,4},{4,5},{5,6},{6,7},{7,8},{8,9},{9,10},{10,1... | collective-permute-start | bytes 1769480 | tf_op jit(solution)/shard_map/ppermute | solution.py:430
  10.1 1.9 %collective-permute-start.1 = (bf16[2,36,8,512]{3,2,1,0:T(8,128)(2,1)S(1)}, bf16[2,36,8,512]{3,2,1,0:T(8,128)(2,1)S(1)}, u32[]{:S(2)}, u32[]{:S(2)}) collective-permute-start(bf16[2,36,8,512]{3,2,1,0:T(8,128)(2,1)S(1)} %get-tuple-element.29), channel_id=1, source_target_pairs={{1,0},{2,1},{3,2},{4,3},{5,4},{6,5},{7,6},{8,7},{9,8},{10,9},{11,1... | collective-permute-start | bytes 1769480 | tf_op jit(solution)/shard_map/ppermute | solution.py:430
  12.0 4.9 %collective-permute-done.fl_ref = bf16[2,36,8,512]{3,2,1,0:T(8,128)(2,1)S(1)} collective-permute-done((bf16[2,36,8,512]{3,2,1,0:T(8,128)(2,1)S(1)}, bf16[2,36,8,512]{3,2,1,0:T(8,128)(2,1)S(1)}, u32[]{:S(2)}, u32[]{:S(2)}) %collective-permute-start) | collective-permute-done | bytes 589856 | tf_op jit(solution)/shard_map/ppermute | solution.py:430
  16.9 4.4 %collective-permute-done.1.fr_ref = bf16[2,36,8,512]{3,2,1,0:T(8,128)(2,1)S(1)} collective-permute-done((bf16[2,36,8,512]{3,2,1,0:T(8,128)(2,1)S(1)}, bf16[2,36,8,512]{3,2,1,0:T(8,128)(2,1)S(1)}, u32[]{:S(2)}, u32[]{:S(2)}) %collective-permute-start.1) | collective-permute-done | bytes 589856 | tf_op jit(solution)/shard_map/ppermute | solution.py:430
  21.3 0.8 shard_map.114
  22.1 3.9 %collective-permute-start.2 = (bf16[3,2,4,24,512]{4,3,2,1,0:T(8,128)(2,1)S(1)}, bf16[3,2,4,24,512]{4,3,2,1,0:T(8,128)(2,1)S(1)}, u32[]{:S(2)}, u32[]{:S(2)}) collective-permute-start(bf16[3,2,4,24,512]{4,3,2,1,0:T(8,128)(2,1)S(1)} %get-tuple-element.30), channel_id=1, source_target_pairs={{0,16},{16,32},{32,48},{48,64},{64,80},{80,96},{96,112},{1,17},{17... | collective-permute-start | bytes 1769480 | tf_op jit(solution)/shard_map/ppermute | solution.py:430
  26.0 1.3 %collective-permute-start.3 = (bf16[3,2,4,24,512]{4,3,2,1,0:T(8,128)(2,1)S(1)}, bf16[3,2,4,24,512]{4,3,2,1,0:T(8,128)(2,1)S(1)}, u32[]{:S(2)}, u32[]{:S(2)}) collective-permute-start(bf16[3,2,4,24,512]{4,3,2,1,0:T(8,128)(2,1)S(1)} %get-tuple-element.31), channel_id=1, source_target_pairs={{16,0},{32,16},{48,32},{64,48},{80,64},{96,80},{112,96},{17,1},{33... | collective-permute-start | bytes 1769480 | tf_op jit(solution)/shard_map/ppermute | solution.py:430
  27.3 1.7 %shard_map.113 = (bf16[2,24,16,512]{3,2,1,0:T(8,128)(2,1)S(1)}, bf16[2,24,16,512]{3,2,1,0:T(8,128)(2,1)S(1)}, bf16[2,24,16,512]{3,2,1,0:T(8,128)(2,1)S(1)}) custom-call(s32[2,2]{1,0:T(2,128)S(1)} %copy-done.12, bf16[2,24,16,512]{3,2,1,0:T(8,128)(2,1)S(1)} %copy-done.8, bf16[2,24,16,512]{3,2,1,0:T(8,128)(2,1)S(1)} %copy-done.9, ...), custom_call_target="tpu_custom_call" | custom-call | flops 402653184 | bytes 4530192 | tf_op jit(solution)/shard_map/pallas_call | solution.py:27
  29.1 3.7 %collective-permute-done.2.top_ref = bf16[3,2,4,24,512]{4,3,2,1,0:T(8,128)(2,1)S(1)} collective-permute-done((bf16[3,2,4,24,512]{4,3,2,1,0:T(8,128)(2,1)S(1)}, bf16[3,2,4,24,512]{4,3,2,1,0:T(8,128)(2,1)S(1)}, u32[]{:S(2)}, u32[]{:S(2)}) %collective-permute-start.2) | collective-permute-done | bytes 589856 | tf_op jit(solution)/shard_map/ppermute | solution.py:430
  32.7 4.0 %collective-permute-done.3.bottom_ref = bf16[3,2,4,24,512]{4,3,2,1,0:T(8,128)(2,1)S(1)} collective-permute-done((bf16[3,2,4,24,512]{4,3,2,1,0:T(8,128)(2,1)S(1)}, bf16[3,2,4,24,512]{4,3,2,1,0:T(8,128)(2,1)S(1)}, u32[]{:S(2)}, u32[]{:S(2)}) %collective-permute-start.3) | collective-permute-done | bytes 589856 | tf_op jit(solution)/shard_map/ppermute | solution.py:430
  36.7 23.7 %shard_map.115 = (bf16[8,8,64,128]{3,2,1,0:T(8,128)(2,1)S(1)}, bf16[8,8,64,128]{3,2,1,0:T(8,128)(2,1)S(1)}, bf16[2,32,16,512]{3,2,1,0:T(8,128)(2,1)S(1)}, bf16[2,32,24,1024]{3,2,1,0:T(8,128)(2,1)}) custom-call(bf16[2,24,16,512]{3,2,1,0:T(8,128)(2,1)S(1)} %get-tuple-element.25.qs_ref, bf16[2,24,16,512]{3,2,1,0:T(8,128)(2,1)S(1)} %get-tuple-element.26.do_ref, ...), custom_call_target="tpu_custom_call" | custom-call | flops 2415919104 | bytes 13443072 | tf_op jit(solution)/shard_map/pallas_call | solution.py:27
  60.5 2.7 %collective-permute-done.8 = bf16[8,8,64,128]{3,2,1,0:T(8,128)(2,1)S(1)} collective-permute-done((bf16[8,8,64,128]{3,2,1,0:T(8,128)(2,1)S(1)}, bf16[8,8,64,128]{3,2,1,0:T(8,128)(2,1)S(1)}, u32[]{:S(2)}, u32[]{:S(2)}) %collective-permute-start.8) | collective-permute-done | bytes 1048608 | tf_op jit(solution)/shard_map/ppermute | solution.py:489
  63.1 1.4 %add_convert_fusion = bf16[8,8,64,128]{3,2,1,0:T(8,128)(2,1)} fusion(bf16[8,8,64,128]{3,2,1,0:T(8,128)(2,1)S(1)} %collective-permute-done.8, bf16[8,8,64,128]{3,2,1,0:T(8,128)(2,1)S(1)} %get-tuple-element.39), kind=kLoop, calls=%fused_computation | loop fusion | flops 2097152 | bytes 3145728 | tf_op jit(solution)/shard_map/convert_element_type | solution.py:490
  64.5 16.8 %all-to-all-start = ((bf16[64,64,128]{2,1,0:T(8,128)(2,1)}), bf16[64,64,128]{2,1,0:T(8,128)(2,1)S(1)}, u32[]{:S(2)}, u32[]{:S(2)}) async-start(bf16[64,64,128]{2,1,0:T(8,128)(2,1)} %bitcast), calls=%async_computation | async-start | bytes 2097152 | tf_op jit(solution)/shard_map/all_to_all | solution.py:491
  81.3 1.9 %copy-done.6 = bf16[2,32,24,1024]{3,2,1,0:T(8,128)(2,1)S(1)} copy-done((bf16[2,32,24,1024]{3,2,1,0:T(8,128)(2,1)S(1)}, bf16[2,32,24,1024]{3,2,1,0:T(8,128)(2,1)}, u32[]{:S(2)}) %copy-start.6) | copy-done | bytes 3145752
  83.2 1.4 %copy-done.7 = bf16[512,1536]{1,0:T(8,128)(2,1)S(1)} copy-done((bf16[512,1536]{1,0:T(8,128)(2,1)S(1)}, bf16[512,1536]{1,0:T(8,128)(2,1)}, u32[]{:S(2)}) %copy-start.7) | copy-done | bytes 1572888
  84.6 2.4 %shard_map.116 = (bf16[2,32,16,512]{3,2,1,0:T(8,128)(2,1)S(1)}, bf16[2,16,8,512]{3,2,1,0:T(8,128)(2,1)S(1)}, bf16[2,16,8,512]{3,2,1,0:T(8,128)(2,1)S(1)}) custom-call(bf16[2,32,24,1024]{3,2,1,0:T(8,128)(2,1)S(1)} %copy-done.6, bf16[2,32,16,512]{3,2,1,0:T(8,128)(2,1)S(1)} %get-tuple-element.33.dq_ref, bf16[512,1536]{1,0:T(8,128)(2,1)S(1)} %copy-done.7), custom_call_target="tpu_custom_call" | custom-call | flops 1207959552 | bytes 7340032 | tf_op jit(solution)/shard_map/pallas_call | solution.py:27
  87.0 3.4 %collective-permute-start.4 = (bf16[2,16,8,512]{3,2,1,0:T(8,128)(2,1)S(1)}, bf16[2,16,8,512]{3,2,1,0:T(8,128)(2,1)S(1)}, u32[]{:S(2)}, u32[]{:S(2)}) collective-permute-start(bf16[2,16,8,512]{3,2,1,0:T(8,128)(2,1)S(1)} %get-tuple-element.35), channel_id=1, source_target_pairs={{0,1},{1,2},{2,3},{3,4},{4,5},{5,6},{6,7},{7,8},{8,9},{9,10},{10,1... | collective-permute-start | bytes 786440 | tf_op jit(solution)/shard_map/ppermute | solution.py:430
  90.4 1.9 %collective-permute-start.5 = (bf16[2,16,8,512]{3,2,1,0:T(8,128)(2,1)S(1)}, bf16[2,16,8,512]{3,2,1,0:T(8,128)(2,1)S(1)}, u32[]{:S(2)}, u32[]{:S(2)}) collective-permute-start(bf16[2,16,8,512]{3,2,1,0:T(8,128)(2,1)S(1)} %get-tuple-element.36), channel_id=1, source_target_pairs={{1,0},{2,1},{3,2},{4,3},{5,4},{6,5},{7,6},{8,7},{9,8},{10,9},{11,1... | collective-permute-start | bytes 786440 | tf_op jit(solution)/shard_map/ppermute | solution.py:430
  92.4 3.2 %collective-permute-done.4.fl_ref = bf16[2,16,8,512]{3,2,1,0:T(8,128)(2,1)S(1)} collective-permute-done((bf16[2,16,8,512]{3,2,1,0:T(8,128)(2,1)S(1)}, bf16[2,16,8,512]{3,2,1,0:T(8,128)(2,1)S(1)}, u32[]{:S(2)}, u32[]{:S(2)}) %collective-permute-start.4) | collective-permute-done | bytes 262176 | tf_op jit(solution)/shard_map/ppermute | solution.py:430
  95.6 2.8 %collective-permute-done.5.fr_ref = bf16[2,16,8,512]{3,2,1,0:T(8,128)(2,1)S(1)} collective-permute-done((bf16[2,16,8,512]{3,2,1,0:T(8,128)(2,1)S(1)}, bf16[2,16,8,512]{3,2,1,0:T(8,128)(2,1)S(1)}, u32[]{:S(2)}, u32[]{:S(2)}) %collective-permute-start.5) | collective-permute-done | bytes 262176 | tf_op jit(solution)/shard_map/ppermute | solution.py:430
  98.5 3.1 %collective-permute-start.6 = (bf16[2,4,16,512]{3,2,1,0:T(8,128)(2,1)S(1)}, bf16[2,4,16,512]{3,2,1,0:T(8,128)(2,1)S(1)}, u32[]{:S(2)}, u32[]{:S(2)}) collective-permute-start(bf16[2,4,16,512]{3,2,1,0:T(8,128)(2,1)S(1)} %get-tuple-element.37), channel_id=1, source_target_pairs={{0,16},{16,32},{32,48},{48,64},{64,80},{80,96},{96,112},{1,17},{17... | collective-permute-start | bytes 393224 | tf_op jit(solution)/shard_map/ppermute | solution.py:430
  101.6 1.3 %collective-permute-start.7 = (bf16[2,4,16,512]{3,2,1,0:T(8,128)(2,1)S(1)}, bf16[2,4,16,512]{3,2,1,0:T(8,128)(2,1)S(1)}, u32[]{:S(2)}, u32[]{:S(2)}) collective-permute-start(bf16[2,4,16,512]{3,2,1,0:T(8,128)(2,1)S(1)} %get-tuple-element.38), channel_id=1, source_target_pairs={{16,0},{32,16},{48,32},{64,48},{80,64},{96,80},{112,96},{17,1},{33... | collective-permute-start | bytes 393224 | tf_op jit(solution)/shard_map/ppermute | solution.py:430
  102.9 0.8 shard_map.119
  103.8 12.0 %all-to-all-start.1 = ((f32[128,1,128]{2,1,0:T(1,128)}), f32[128,1,128]{2,1,0:T(1,128)S(1)}, u32[]{:S(2)}, u32[]{:S(2)}) async-start(f32[128,1,128]{2,1,0:T(1,128)} %bitcast.2), calls=%async_computation.1 | async-start | bytes 131072 | tf_op jit(solution)/shard_map/all_to_all | solution.py:515
  115.8 1.2 shard_map.118
  117.0 8.3 %all-to-all-done.1 = f32[128,1,128]{2,1,0:T(1,128)S(1)} async-done(((f32[128,1,128]{2,1,0:T(1,128)}), f32[128,1,128]{2,1,0:T(1,128)S(1)}, u32[]{:S(2)}, u32[]{:S(2)}) %all-to-all-start.1) | async-done | bytes 65568 | tf_op jit(solution)/shard_map/all_to_all | solution.py:515
  125.3 0.8 shard_map.120
  (26 shorter events, 0.8 us)
Async XLA Ops:
  0.6 1.1 copy-start
  1.8 1.1 copy-start.2
  2.9 1.1 copy-start.4
  4.0 0.7 copy-start.11
  4.7 16.6 %copy-start.1 = (bf16[2,24,16,512]{3,2,1,0:T(8,128)(2,1)S(1)}, bf16[2,24,16,512]{3,2,1,0:T(8,128)(2,1)}, u32[]{:S(2)}) copy-start(bf16[2,24,16,512]{3,2,1,0:T(8,128)(2,1)} %k_ref.5) | copy-start | bytes 2359300
  4.7 16.6 %copy-start.3 = (bf16[2,24,16,512]{3,2,1,0:T(8,128)(2,1)S(1)}, bf16[2,24,16,512]{3,2,1,0:T(8,128)(2,1)}, u32[]{:S(2)}) copy-start(bf16[2,24,16,512]{3,2,1,0:T(8,128)(2,1)} %v_ref.5) | copy-start | bytes 2359300
  4.7 16.6 %copy-start.5 = (bf16[2,24,16,512]{3,2,1,0:T(8,128)(2,1)S(1)}, bf16[2,24,16,512]{3,2,1,0:T(8,128)(2,1)}, u32[]{:S(2)}) copy-start(bf16[2,24,16,512]{3,2,1,0:T(8,128)(2,1)} %tok_ref.5) | copy-start | bytes 2359300
  5.4 21.9 %copy-start.8 = (bf16[2,24,16,512]{3,2,1,0:T(8,128)(2,1)S(1)}, bf16[2,24,16,512]{3,2,1,0:T(8,128)(2,1)}, u32[]{:S(2)}) copy-start(bf16[2,24,16,512]{3,2,1,0:T(8,128)(2,1)} %q_ref.1) | copy-start | bytes 2359300
  5.4 21.9 %copy-start.9 = (bf16[2,24,16,512]{3,2,1,0:T(8,128)(2,1)S(1)}, bf16[2,24,16,512]{3,2,1,0:T(8,128)(2,1)}, u32[]{:S(2)}) copy-start(bf16[2,24,16,512]{3,2,1,0:T(8,128)(2,1)} %g_ref.1) | copy-start | bytes 2359300
  5.4 21.8 %copy-start.10 = (bf16[512,512]{1,0:T(8,128)(2,1)S(1)}, bf16[512,512]{1,0:T(8,128)(2,1)}, u32[]{:S(2)}) copy-start(bf16[512,512]{1,0:T(8,128)(2,1)} %w_ref.2) | copy-start | bytes 1572868
  5.4 21.8 %copy-start.12 = (s32[2,2]{1,0:T(2,128)S(1)}, s32[2,2]{1,0:T(2,128)}, u32[]{:S(2)}) copy-start(s32[2,2]{1,0:T(2,128)} %crop_ref.1) | copy-start | bytes 52
  5.5 11.5 %collective-permute-start = (bf16[2,36,8,512]{3,2,1,0:T(8,128)(2,1)S(1)}, bf16[2,36,8,512]{3,2,1,0:T(8,128)(2,1)S(1)}, u32[]{:S(2)}, u32[]{:S(2)}) collective-permute-start(bf16[2,36,8,512]{3,2,1,0:T(8,128)(2,1)S(1)} %get-tuple-element.28), channel_id=1, source_target_pairs={{0,1},{1,2},{2,3},{3,4},{4,5},{5,6},{6,7},{7,8},{8,9},{9,10},{10,1... | collective-permute-start | bytes 1769480 | tf_op jit(solution)/shard_map/ppermute | solution.py:430
  10.1 11.2 %collective-permute-start.1 = (bf16[2,36,8,512]{3,2,1,0:T(8,128)(2,1)S(1)}, bf16[2,36,8,512]{3,2,1,0:T(8,128)(2,1)S(1)}, u32[]{:S(2)}, u32[]{:S(2)}) collective-permute-start(bf16[2,36,8,512]{3,2,1,0:T(8,128)(2,1)S(1)} %get-tuple-element.29), channel_id=1, source_target_pairs={{1,0},{2,1},{3,2},{4,3},{5,4},{6,5},{7,6},{8,7},{9,8},{10,9},{11,1... | collective-permute-start | bytes 1769480 | tf_op jit(solution)/shard_map/ppermute | solution.py:430
  22.1 10.7 %collective-permute-start.2 = (bf16[3,2,4,24,512]{4,3,2,1,0:T(8,128)(2,1)S(1)}, bf16[3,2,4,24,512]{4,3,2,1,0:T(8,128)(2,1)S(1)}, u32[]{:S(2)}, u32[]{:S(2)}) collective-permute-start(bf16[3,2,4,24,512]{4,3,2,1,0:T(8,128)(2,1)S(1)} %get-tuple-element.30), channel_id=1, source_target_pairs={{0,16},{16,32},{32,48},{48,64},{64,80},{80,96},{96,112},{1,17},{17... | collective-permute-start | bytes 1769480 | tf_op jit(solution)/shard_map/ppermute | solution.py:430
  26.0 10.8 %collective-permute-start.3 = (bf16[3,2,4,24,512]{4,3,2,1,0:T(8,128)(2,1)S(1)}, bf16[3,2,4,24,512]{4,3,2,1,0:T(8,128)(2,1)S(1)}, u32[]{:S(2)}, u32[]{:S(2)}) collective-permute-start(bf16[3,2,4,24,512]{4,3,2,1,0:T(8,128)(2,1)S(1)} %get-tuple-element.31), channel_id=1, source_target_pairs={{16,0},{32,16},{48,32},{64,48},{80,64},{96,80},{112,96},{17,1},{33... | collective-permute-start | bytes 1769480 | tf_op jit(solution)/shard_map/ppermute | solution.py:430
  60.5 2.7 %collective-permute-start.8 = (bf16[8,8,64,128]{3,2,1,0:T(8,128)(2,1)S(1)}, bf16[8,8,64,128]{3,2,1,0:T(8,128)(2,1)S(1)}, u32[]{:S(2)}, u32[]{:S(2)}) collective-permute-start(bf16[8,8,64,128]{3,2,1,0:T(8,128)(2,1)S(1)} %get-tuple-element.40), channel_id=1, source_target_pairs={{0,1},{1,0},{2,3},{3,2},{4,5},{5,4},{6,7},{7,6},{8,9},{9,8},{10,11... | collective-permute-start | bytes 3145736 | tf_op jit(solution)/shard_map/ppermute | solution.py:489
  64.5 38.4 %all-to-all-start = ((bf16[64,64,128]{2,1,0:T(8,128)(2,1)}), bf16[64,64,128]{2,1,0:T(8,128)(2,1)S(1)}, u32[]{:S(2)}, u32[]{:S(2)}) async-start(bf16[64,64,128]{2,1,0:T(8,128)(2,1)} %bitcast), calls=%async_computation | async-start | bytes 2097152 | tf_op jit(solution)/shard_map/all_to_all | solution.py:491
  81.3 1.9 %copy-start.6 = (bf16[2,32,24,1024]{3,2,1,0:T(8,128)(2,1)S(1)}, bf16[2,32,24,1024]{3,2,1,0:T(8,128)(2,1)}, u32[]{:S(2)}) copy-start(bf16[2,32,24,1024]{3,2,1,0:T(8,128)(2,1)} %get-tuple-element.32.kv_ref) | copy-start | bytes 9437188
  83.2 1.4 %copy-start.7 = (bf16[512,1536]{1,0:T(8,128)(2,1)S(1)}, bf16[512,1536]{1,0:T(8,128)(2,1)}, u32[]{:S(2)}) copy-start(bf16[512,1536]{1,0:T(8,128)(2,1)} %w_ref.3) | copy-start | bytes 4718596
  87.0 8.6 %collective-permute-start.4 = (bf16[2,16,8,512]{3,2,1,0:T(8,128)(2,1)S(1)}, bf16[2,16,8,512]{3,2,1,0:T(8,128)(2,1)S(1)}, u32[]{:S(2)}, u32[]{:S(2)}) collective-permute-start(bf16[2,16,8,512]{3,2,1,0:T(8,128)(2,1)S(1)} %get-tuple-element.35), channel_id=1, source_target_pairs={{0,1},{1,2},{2,3},{3,4},{4,5},{5,6},{6,7},{7,8},{8,9},{9,10},{10,1... | collective-permute-start | bytes 786440 | tf_op jit(solution)/shard_map/ppermute | solution.py:430
  90.4 8.0 %collective-permute-start.5 = (bf16[2,16,8,512]{3,2,1,0:T(8,128)(2,1)S(1)}, bf16[2,16,8,512]{3,2,1,0:T(8,128)(2,1)S(1)}, u32[]{:S(2)}, u32[]{:S(2)}) collective-permute-start(bf16[2,16,8,512]{3,2,1,0:T(8,128)(2,1)S(1)} %get-tuple-element.36), channel_id=1, source_target_pairs={{1,0},{2,1},{3,2},{4,3},{5,4},{6,5},{7,6},{8,7},{9,8},{10,9},{11,1... | collective-permute-start | bytes 786440 | tf_op jit(solution)/shard_map/ppermute | solution.py:430
  98.5 17.3 %collective-permute-start.6 = (bf16[2,4,16,512]{3,2,1,0:T(8,128)(2,1)S(1)}, bf16[2,4,16,512]{3,2,1,0:T(8,128)(2,1)S(1)}, u32[]{:S(2)}, u32[]{:S(2)}) collective-permute-start(bf16[2,4,16,512]{3,2,1,0:T(8,128)(2,1)S(1)} %get-tuple-element.37), channel_id=1, source_target_pairs={{0,16},{16,32},{32,48},{48,64},{64,80},{80,96},{96,112},{1,17},{17... | collective-permute-start | bytes 393224 | tf_op jit(solution)/shard_map/ppermute | solution.py:430
  101.6 14.2 %collective-permute-start.7 = (bf16[2,4,16,512]{3,2,1,0:T(8,128)(2,1)S(1)}, bf16[2,4,16,512]{3,2,1,0:T(8,128)(2,1)S(1)}, u32[]{:S(2)}, u32[]{:S(2)}) collective-permute-start(bf16[2,4,16,512]{3,2,1,0:T(8,128)(2,1)S(1)} %get-tuple-element.38), channel_id=1, source_target_pairs={{16,0},{32,16},{48,32},{64,48},{80,64},{96,80},{112,96},{17,1},{33... | collective-permute-start | bytes 393224 | tf_op jit(solution)/shard_map/ppermute | solution.py:430
  103.8 21.5 %all-to-all-start.1 = ((f32[128,1,128]{2,1,0:T(1,128)}), f32[128,1,128]{2,1,0:T(1,128)S(1)}, u32[]{:S(2)}, u32[]{:S(2)}) async-start(f32[128,1,128]{2,1,0:T(1,128)} %bitcast.2), calls=%async_computation.1 | async-start | bytes 131072 | tf_op jit(solution)/shard_map/all_to_all | solution.py:515

commit v3 on v2

v3 whole, which is shorter than its diff:
```python
import jax
import jax.numpy as jnp
from jax import lax
from jax.experimental import pallas as pl
from jax.experimental.pallas import tpu as pltpu
from jax.sharding import PartitionSpec as P

HEADS = 8
RADIUS = 4
BLOCK = 8
GROUP = 4

max_norm = 1000.0
masked_score = -1e30
tiny_square = 1e-06

f32 = jnp.float32
bf16 = jnp.bfloat16
VMEM = pl.BlockSpec(memory_space=pltpu.VMEM)
COLS = ("pair", "core")
ANY = pl.BlockSpec(memory_space=pltpu.HBM)
SMEM = pl.BlockSpec(memory_space=pltpu.SMEM)


def call(kernel, outs, ins, scratch=(), smem=(), far=(), far_outs=(), flops=0, limit=16 << 20):
    moved = sum(a.size * a.dtype.itemsize for a in list(ins) + jax.tree.leaves(outs))
    return pl.pallas_call(
        kernel,
        out_shape=outs,
        in_specs=[SMEM if n in smem else ANY if n in far else VMEM for n in range(len(ins))],
        out_specs=tuple(ANY if n in far_outs else VMEM for n in range(len(outs))) if isinstance(outs, tuple) else VMEM,
        scratch_shapes=list(scratch),
        compiler_params=pltpu.CompilerParams(vmem_limit_bytes=limit),
        cost_estimate=pl.CostEstimate(
            flops=flops, bytes_accessed=moved, transcendentals=0
        ),
    )(*ins)


def shape(*dims, dtype=bf16):
    return jax.ShapeDtypeStruct(dims, dtype)


def turn(x):
    return pltpu.roll(x, 4, 1)


def lower(x):
    return lax.broadcasted_iota(jnp.int32, x.shape, 1) < 4


def block_of(ref, fac_ref, part, b, i, j, rows, features):
    factor = fac_ref[b, i, j : j + 1, part * features : (part + 1) * features]
    return ref[b, rows, 8 * j : 8 * j + 8, :].astype(f32) * factor[None]


def edge_kernel(
    scale_ref, k_ref, v_ref, tok_ref, fac_ref, left_ref, right_ref, up_ref, down_ref, k_buf, v_buf, t_buf, sem
):
    members, height, breadth, features = k_ref.shape
    tiles = breadth // 8
    copies = [
        pltpu.make_async_copy(src, dst, sem.at[n])
        for n, (src, dst) in enumerate(((k_ref, k_buf), (v_ref, v_buf), (tok_ref, t_buf)))
    ]
    for c in copies:
        c.start()
    count = scale_ref.shape[3]
    per = 3 * features // count
    hot = (
        lax.broadcasted_iota(jnp.int32, (count, 3 * features), 0)
        == lax.broadcasted_iota(jnp.int32, (count, 3 * features), 1) // per
    ).astype(f32).astype(bf16)
    for b in range(members):
        for i in range(height // 8):
            factor = jnp.exp2(scale_ref[b, i].astype(f32)).astype(bf16)
            fac_ref[b, i] = jnp.dot(factor, hot, preferred_element_type=f32)
    for c in copies:
        c.wait()
    half = height // 2
    for b in range(members):
        for i in range(height // 8):
            rows = slice(8 * i, 8 * i + 8)
            k = [block_of(k_buf, fac_ref, 1, b, i, j, rows, features) for j in range(tiles)]
            v = [block_of(v_buf, fac_ref, 2, b, i, j, rows, features) for j in range(tiles)]
            low = lower(k[0])
            left_ref[b, rows] = jnp.where(low, k[0], turn(v[0])).astype(bf16)
            right_ref[b, rows] = jnp.where(low, turn(v[-1]), k[-1]).astype(bf16)
            for m, parts in enumerate((k, v)):
                x = jnp.concatenate(parts, 1).astype(bf16)
                if i == 0:
                    up_ref[m, b] = x[0:4]
                if i == height // 8 - 1:
                    down_ref[m, b] = x[4:8]
        up_ref[2, b] = t_buf[b, 0:4]
        down_ref[2, b] = t_buf[b, height - 4 : height]
        for r in range(0, half, 4):
            here, there = slice(r, r + 4), slice(half + r, half + r + 4)
            out = slice(height + r, height + r + 4)
            pack_columns(t_buf.at[b, here], t_buf.at[b, there], left_ref.at[b, out], right_ref.at[b, out])


def pack_columns(one_ref, two_ref, left_ref, right_ref):
    last = one_ref.shape[1] - 8
    x0, y0 = one_ref[:, 0:8].astype(f32), two_ref[:, 0:8].astype(f32)
    x1, y1 = one_ref[:, last:].astype(f32), two_ref[:, last:].astype(f32)
    low = lower(x0)
    left_ref[...] = jnp.where(low, x0, turn(y0)).astype(bf16)
    right_ref[...] = jnp.where(low, turn(y1), x1).astype(bf16)


def corner_kernel(top_ref, bottom_ref, left_ref, right_ref):
    for b in range(top_ref.shape[1]):
        for n, (one, two) in enumerate(
            (
                (top_ref.at[0, b], top_ref.at[1, b]),
                (bottom_ref.at[0, b], bottom_ref.at[1, b]),
                (top_ref.at[2, b], bottom_ref.at[2, b]),
            )
        ):
            out = slice(4 * n, 4 * n + 4)
            pack_columns(one, two, left_ref.at[b, out], right_ref.at[b, out])


def rims_of(left_ref, right_ref, b, rows):
    left, right = left_ref[b, rows].astype(f32), right_ref[b, rows].astype(f32)
    low = lower(left)
    return jnp.where(low, right, left), turn(jnp.where(low, left, right))


def prepare_kernel(crop_ref, q_ref, g_ref, fac_ref, w_ref, qs_ref, gm_ref, do_ref):
    members, height, breadth, features = q_ref.shape
    tiles = breadth // 8
    row0 = lax.axis_index("row") * height
    col0 = (lax.axis_index("pair") * 2 + lax.axis_index("core")) * breadth
    for b in range(members):
        for i in range(height // 8):
            rows = slice(8 * i, 8 * i + 8)
            parts = [block_of(q_ref, fac_ref, 0, b, i, j, rows, features) for j in range(tiles)]
            qs_ref[b, rows] = (jnp.concatenate(parts, 1) * 0.125).astype(bf16)
            g = g_ref[b, rows].astype(f32)
            r = lax.broadcasted_iota(jnp.int32, g.shape, 0) + (8 * i + row0)
            c = lax.broadcasted_iota(jnp.int32, g.shape, 1) + col0
            keep = (r >= crop_ref[b, 0]) & (c >= crop_ref[b, 1])
            gm = jnp.where(keep, g, 0.0).astype(bf16)
            gm_ref[b, rows] = gm
            do = lax.dot_general(
                gm.reshape(8 * breadth, features), w_ref[...], (((1,), (1,)), ((), ())),
                preferred_element_type=f32,
            )
            do_ref[b, rows] = do.astype(bf16).reshape(8, breadth, features)


def key_tile(blocks, rim, t):
    low = lower(rim)
    before = rim if t == 0 else blocks[t - 1]
    after = rim if t == len(blocks) - 1 else blocks[t + 1]
    return jnp.concatenate([blocks[t], jnp.where(low, after, before)], 1).astype(bf16)


def place_of(height, breadth):
    row0 = lax.axis_index("row") * height
    col0 = (lax.axis_index("pair") * 2 + lax.axis_index("core")) * breadth
    return row0, col0, height * lax.axis_size("row"), breadth * lax.axis_size("pair") * 2


def attend(q, g, keys_of, i, place, emit):
    features = q.shape[2]
    head_lanes = features // HEADS
    wide = GROUP * head_lanes
    row0, col0, frame_rows, frame_cols = place
    lane = lax.broadcasted_iota(jnp.int32, (1, wide), 1) // head_lanes
    head_mask = [(lane == h).astype(f32).astype(bf16) for h in range(GROUP)]
    first = lax.broadcasted_iota(jnp.int32, (64, 2 * head_lanes), 1) < head_lanes
    across = (((1,), (1,)), ((), ()))
    down = (((0,), (0,)), ((), ()))

    def spread(x):
        return jnp.concatenate([x * m for m in head_mask], 0)

    def gather(x):
        parts = []
        for n in range(GROUP // 2):
            lanes = slice(128 * n, 128 * n + 128)
            parts.append(jnp.where(first, x[128 * n : 128 * n + 64, lanes], x[128 * n + 64 : 128 * n + 128, lanes]))
        return jnp.concatenate(parts, 1)

    outs, grads = [], []
    for t in range(q.shape[1] // 8):
        qn = lax.broadcasted_iota(jnp.int32, (64, 256), 0)
        kn = lax.broadcasted_iota(jnp.int32, (64, 256), 1)
        qr, qc = qn // 8, qn % 8
        kr, ks = kn // 16, kn % 16
        kc = jnp.where(ks < 12, ks, ks - 16)
        row = row0 + 8 * i - 4 + kr
        col = col0 + 8 * t + kc
        ok = (kr >= qr) & (kr <= qr + 8) & (kc >= qc - 4) & (kc <= qc + 4)
        ok &= (row >= 0) & (row < frame_rows) & (col >= 0) & (col < frame_cols)
        bias = jnp.concatenate([jnp.where(ok, 0.0, masked_score)] * GROUP, 0)
        q64 = q[:, 8 * t : 8 * t + 8].reshape(64, features).astype(bf16)
        g64 = g[:, 8 * t : 8 * t + 8].reshape(64, features).astype(bf16)
        ot, dqt = [], []
        for lanes in [slice(n * wide, (n + 1) * wide) for n in range(HEADS // GROUP)]:
            qx, gx = spread(q64[:, lanes]), spread(g64[:, lanes])
            k, v = keys_of(t, lanes)
            s = lax.dot_general(qx, k, across, preferred_element_type=f32) + bias
            w = jnp.exp(s - jnp.max(s, 1, keepdims=True))
            p = w * (1.0 / jnp.sum(w, 1, keepdims=True))
            ph = p.astype(bf16)
            o = jnp.dot(ph, v, preferred_element_type=f32).astype(bf16).astype(f32)
            delta = jnp.sum(o * gx.astype(f32), 1, keepdims=True)
            dp = lax.dot_general(gx, v, across, preferred_element_type=f32)
            ds = (p * (dp - delta)).astype(bf16)
            dq = jnp.dot(ds, k, preferred_element_type=f32)
            dk = lax.dot_general(ds, qx, down, preferred_element_type=f32).reshape(16, 16, wide)
            dv = lax.dot_general(ph, gx, down, preferred_element_type=f32).reshape(16, 16, wide)
            ot.append(gather(o))
            dqt.append(gather(dq) * 0.125)
            emit(t, lanes, dk, dv)
        outs.append(jnp.concatenate(ot, 1).reshape(8, 8, features))
        grads.append(jnp.concatenate(dqt, 1).reshape(8, 8, features))
    return jnp.concatenate(outs, 1), jnp.concatenate(grads, 1)


def middle_kernel(
    qs_ref, do_ref, k_ref, v_ref, fac_ref, fl_ref, fr_ref, kt_ref, vt_ref, dk_ref, dv_ref, o_ref, dq_ref
):
    members, height, breadth, features = qs_ref.shape
    strips, tiles = height // 8, breadth // 8
    place = place_of(height, breadth)
    for b in range(members):
        for i in range(strips):
            rows = slice(8 * i, 8 * i + 8)
            rims = rims_of(fl_ref, fr_ref, b, rows)
            for m, (ref, out) in enumerate(((k_ref, kt_ref), (v_ref, vt_ref))):
                blocks = [block_of(ref, fac_ref, m + 1, b, i, j, rows, features) for j in range(tiles)]
                for t in range(tiles):
                    out[b, t, rows] = key_tile(blocks, rims[m], t)

    def step(b, _):
        def keys_of(t, lanes):
            return tuple(ref[b, t, 4:20, :, lanes].reshape(256, -1) for ref in (kt_ref, vt_ref))

        def emit(t, lanes, dk, dv):
            dk_ref[b, t, :, :, lanes] = dk
            dv_ref[b, t, :, :, lanes] = dv

        o, dq = attend(qs_ref[b, 8:16].astype(f32), do_ref[b, 8:16].astype(f32), keys_of, 1, place, emit)
        o_ref[b] = o.astype(bf16)
        dq_ref[b] = dq.astype(bf16)
        return 0

    lax.fori_loop(0, members, step, 0)


def main_kernel(
    qs_ref, do_ref, kt_ref, vt_ref, dkm_ref, dvm_ref, om_ref, dqm_ref, gm_ref, tok_ref,
    fl_ref, fr_ref, top_ref, bottom_ref, cl_ref, cr_ref,
    keep_ref, send_ref, dq_out, kv_out,
    kh_ref, vh_ref, dkt_ref, dvt_ref, o_ref, tp_ref, all_ref, dq_ref, kv_ref, sem,
):
    members, height, breadth, features = qs_ref.shape
    tall = height + 8
    tiles = breadth // 8
    place = place_of(height, breadth)
    for b in range(members):
        token_rims = rims_of(cl_ref, cr_ref, b, slice(8, 12))
        for n, ref in enumerate((top_ref, bottom_ref)):
            rims = rims_of(cl_ref, cr_ref, b, slice(4 * n, 4 * n + 4))
            for m, out in enumerate((kh_ref, vh_ref)):
                blocks = [ref[m, b, :, 8 * j : 8 * j + 8].astype(f32) for j in range(tiles)]
                for t in range(tiles):
                    out[n, b, t] = key_tile(blocks, rims[m], t)
            halo = slice(0, 4) if n == 0 else slice(tall - 4, tall)
            tp_ref[b, halo] = jnp.concatenate([ref[2, b].astype(f32), token_rims[n]], 1).astype(bf16)
            dq_ref[b, halo] = jnp.zeros((4, breadth, features), bf16)
        half = height // 2
        for r in range(0, half, 4):
            pair = rims_of(fl_ref, fr_ref, b, slice(height + r, height + r + 4))
            for rim, row in zip(pair, (r, half + r)):
                own = tok_ref[b, row : row + 4].astype(f32)
                tp_ref[b, row + 4 : row + 8] = jnp.concatenate([own, rim], 1).astype(bf16)
        o_ref[b, 8:16] = om_ref[b]
        dq_ref[b, 12:20] = dqm_ref[b]

    def step(b, _):
        for n, i in enumerate((0, height // 8 - 1)):
            def keys_of(t, lanes):
                parts = []
                for ref, halo in ((kt_ref, kh_ref), (vt_ref, vh_ref)):
                    rim = halo[n, b, t, :, :, lanes]
                    own = ref[b, t, slice(0, 12) if n == 0 else slice(height - 12, height), :, lanes]
                    both = [rim, own] if n == 0 else [own, rim]
                    parts.append(jnp.concatenate(both, 0).reshape(256, -1))
                return tuple(parts)

            def emit(t, lanes, dk, dv):
                for ref, mid, x in ((dkt_ref, dkm_ref, dk), (dvt_ref, dvm_ref, dv)):
                    if n == 0:
                        ref[b, t, 0:8, :, lanes] = x[0:8]
                        ref[b, t, 8:16, :, lanes] = x[8:16] + mid[b, t, 0:8, :, lanes]
                    else:
                        ref[b, t, 16:24, :, lanes] = x[0:8] + mid[b, t, 8:16, :, lanes]
                        ref[b, t, 24:32, :, lanes] = x[8:16]

            rows = slice(8 * i, 8 * i + 8)
            o, dq = attend(qs_ref[b, rows].astype(f32), do_ref[b, rows].astype(f32), keys_of, i, place, emit)
            o_ref[b, rows] = o.astype(bf16)
            dq_ref[b, 8 * i + 4 : 8 * i + 12] = dq.astype(bf16)
        return 0

    lax.fori_loop(0, members, step, 0)

    for b in range(members):
        for r in range(0, tall, 8):
            rows = slice(r, r + 8)
            for m, ref in enumerate((dkt_ref, dvt_ref)):
                rim = [ref[b, t, rows, 8:16] for t in range(tiles)]
                low = lower(rim[0])
                own = []
                for t in range(tiles):
                    x = ref[b, t, rows, 0:8]
                    if t > 0:
                        x = x + jnp.where(low, rim[t - 1], 0.0)
                    if t < tiles - 1:
                        x = x + jnp.where(low, 0.0, rim[t + 1])
                    own.append(x)
                own.append(jnp.where(low, rim[tiles - 1], rim[0]))
                kv_ref[b, rows, :, m * features : (m + 1) * features] = jnp.concatenate(own, 1).astype(bf16)

    copies = [
        pltpu.make_async_copy(src, dst, sem.at[n])
        for n, (src, dst) in enumerate(((dq_ref, dq_out), (kv_ref, kv_out)))
    ]
    for c in copies:
        c.start()
    down = (((0,), (0,)), ((), ()))
    cells = members * height * breadth
    padded = members * tall * (breadth + 8)
    for b in range(members):
        x = lax.dot_general(
            tok_ref[b].reshape(cells // members, features),
            dq_ref[b, 4 : tall - 4].reshape(cells // members, features), down,
            preferred_element_type=f32,
        )
        y = lax.dot_general(
            o_ref[b].reshape(cells // members, features), gm_ref[b].reshape(cells // members, features), down,
            preferred_element_type=f32,
        )
        if b:
            x, y = x + all_ref[:, 0:features], y + all_ref[:, 3 * features :]
        all_ref[:, 0:features] = x
        all_ref[:, 3 * features :] = y
    kv = kv_ref[...].reshape(padded, 2 * features)
    all_ref[:, features : 3 * features] = lax.dot_general(
        tp_ref[...].reshape(padded, features), kv, down, preferred_element_type=f32
    )

    deep_rows, pairs, deep, broad = keep_ref.shape
    count = 2 * pairs
    main, rest = 3 * features // count, features // count
    lanes = lax.broadcasted_iota(jnp.int32, (features, broad), 1)

    def window(start, end):
        base, off = start // broad * broad, start % broad
        x = all_ref[:, base : base + broad]
        if off:
            x = pltpu.roll(x, broad - off, 1)
        if end > base + broad:
            y = pltpu.roll(all_ref[:, base + broad : base + 2 * broad], broad - off, 1)
            x = jnp.where(lanes < broad - off, x, y)
        return x

    def block(c):
        x = window(main * c, main * (c + 1))
        base, off = 3 * features + rest * c // broad * broad, rest * c % broad
        y = all_ref[:, base : base + broad]
        if off != main:
            y = pltpu.roll(y, (main - off) % broad, 1)
        return jnp.where(lanes < main, x, y).astype(bf16).reshape(deep_rows, deep, broad)

    mine = lax.axis_index("core") == 0
    for p in range(pairs):
        even, odd = block(2 * p), block(2 * p + 1)
        keep_ref[:, p] = jnp.where(mine, even, odd)
        send_ref[:, p] = jnp.where(mine, odd, even)
    for c in copies:
        c.wait()


def token_kernel(kv_ref, dq_ref, w_ref, gt_ref, left_ref, right_ref):
    members, tall, breadth, features = dq_ref.shape
    across = (((1,), (1,)), ((), ()))
    middle = tall // 2
    for b in range(members):
        y = lax.dot_general(
            kv_ref[b].reshape(tall * (breadth + 8), 2 * features), w_ref[:, features:], across,
            preferred_element_type=f32,
        ).reshape(tall, breadth + 8, features)
        z = lax.dot_general(
            dq_ref[b].reshape(tall * breadth, features), w_ref[:, 0:features], across,
            preferred_element_type=f32,
        ).reshape(tall, breadth, features)
        gt_ref[b] = (y[:, 0:breadth] + z).astype(bf16)
        here, there = y[0:middle, breadth:], turn(y[middle:, breadth:])
        low = lower(here)
        right_ref[b] = jnp.where(low, here, there).astype(bf16)
        left_ref[b] = jnp.where(low, there, here).astype(bf16)


def back_rims(fl, fr):
    low = lower(fl)
    here = (jnp.where(low, fl, 0.0), jnp.where(low, 0.0, fr))
    there = (jnp.where(low, turn(fl), 0.0), jnp.where(low, 0.0, turn(fr)))
    return here, there


def plus_rims(x, rims):
    last = x.shape[1] - 8
    return jnp.concatenate([x[:, 0:8] + rims[0], x[:, 8:last], x[:, last:] + rims[1]], 1) if last > 8 else (
        jnp.concatenate([x[:, 0:8] + rims[0], x[:, 8:] + rims[1]], 1)
    )


def add_kernel(x_ref, y_ref, sum_ref):
    sum_ref[...] = (x_ref[...].astype(f32) + y_ref[...].astype(f32)).astype(bf16)


def total_kernel(x_ref, sum_ref, square_ref):
    x = jnp.sum(x_ref[...].astype(f32), 0)
    sum_ref[...] = x
    square = jnp.sum(x * x, 0, keepdims=True)
    square_ref[...] = jnp.broadcast_to(square, square_ref.shape)


def halo_kernel(gt_ref, fl_ref, fr_ref, up_ref, down_ref):
    members, tall = gt_ref.shape[:2]
    half = tall // 2
    for b in range(members):
        here, _ = back_rims(fl_ref[b, 0:4].astype(f32), fr_ref[b, 0:4].astype(f32))
        _, there = back_rims(fl_ref[b, half - 4 : half].astype(f32), fr_ref[b, half - 4 : half].astype(f32))
        up_ref[b] = plus_rims(gt_ref[b, 0:4].astype(f32), here).astype(bf16)
        down_ref[b] = plus_rims(gt_ref[b, tall - 4 : tall].astype(f32), there).astype(bf16)


def join_kernel(gt_ref, fl_ref, fr_ref, ft_ref, fb_ref, tok_ref):
    members, height = tok_ref.shape[:2]
    half = (height + 8) // 2
    for b in range(members):
        for r in range(0, half, 4):
            pair = back_rims(fl_ref[b, r : r + 4].astype(f32), fr_ref[b, r : r + 4].astype(f32))
            for rims, row in zip(pair, (r, half + r)):
                if row == 0 or row == height + 4:
                    continue
                y = plus_rims(gt_ref[b, row : row + 4].astype(f32), rims)
                if row == 4:
                    y = y + ft_ref[b].astype(f32)
                if row == height:
                    y = y + fb_ref[b].astype(f32)
                tok_ref[b, row - 4 : row] = y.astype(bf16)


def clip_kernel(x_ref, square_ref, qkv_ref, out_ref):
    total = jnp.sum(jnp.sum(square_ref[...], 0, keepdims=True), 1, keepdims=True)
    clip = jnp.minimum(1.0, max_norm / jnp.sqrt(total + tiny_square))
    x = x_ref[...] * clip
    main = qkv_ref.shape[1]
    qkv_ref[...] = x[:, 0:main]
    out_ref[...] = x.T[main:]


def shift(x, axes, by):
    size = lax.axis_size(axes)
    return lax.ppermute(x, axes, [(i, i + by) for i in range(size) if 0 <= i + by < size])


def body(tokens, w_qkv, w_out, q_saved, k_saved, v_saved, scale_exp, grad_out, crop_start):
    members, height, breadth, features = tokens.shape
    tall = height + 8
    packed = height + height // 2
    packed_columns = shape(members, packed, 8, features)
    strip = shape(3, members, 4, breadth, features)
    factor, left, right, up, down = call(
        edge_kernel,
        (
            shape(*scale_exp.shape[:3], 3 * features, dtype=f32),
            packed_columns, packed_columns, strip, strip,
        ),
        (scale_exp, k_saved, v_saved, tokens),
        scratch=(pltpu.VMEM(tokens.shape, bf16),) * 3 + (pltpu.SemaphoreType.DMA((3,)),),
        far=(1, 2, 3),
        limit=58 << 20,
    )
    top, bottom = shift(down, "row", 1), shift(up, "row", -1)
    from_left, from_right = shift(right, COLS, 1), shift(left, COLS, -1)
    cells = members * height * breadth
    qs, gm, do = call(
        prepare_kernel,
        (shape(*tokens.shape),) * 3,
        (crop_start, q_saved, grad_out, factor, w_out),
        smem=(0,),
        flops=2 * cells * features * features,
    )
    corner = shape(members, 12, 8, features)
    top, bottom, do = lax.optimization_barrier((top, bottom, do))
    left, right = call(corner_kernel, (corner, corner), (top, bottom))
    corner_left, corner_right = shift(right, COLS, 1), shift(left, COLS, -1)
    tiles = breadth // 8
    own_tiles = shape(members, tiles, height, 16, features)
    middle_tiles = shape(members, tiles, 16, 16, features, dtype=f32)
    middle_rows = shape(members, 8, breadth, features)
    kt, vt, dk, dv, out, dq = call(
        middle_kernel,
        (own_tiles, own_tiles, middle_tiles, middle_tiles, middle_rows, middle_rows),
        (qs, do, k_saved, v_saved, factor, from_left, from_right),
        flops=4 * cells * features * features,
        limit=20 << 20,
    )
    rows, pairs = lax.axis_size("row"), lax.axis_size("pair")
    deep, wide = features // rows, 4 * features // (2 * pairs)
    halo_tiles = pltpu.VMEM((2, members, tiles, 4, 16, features), bf16)
    all_tiles = pltpu.VMEM((members, tiles, tall, 16, features), f32)
    keep, send, dq, kv = call(
        main_kernel,
        (
            shape(rows, pairs, deep, wide),
            shape(rows, pairs, deep, wide),
            shape(members, tall, breadth, features),
            shape(members, tall, breadth + 8, 2 * features),
        ),
        (
            qs, do, kt, vt, dk, dv, out, dq, gm, tokens,
            from_left, from_right, top, bottom, corner_left, corner_right,
        ),
        scratch=(
            halo_tiles, halo_tiles, all_tiles, all_tiles,
            pltpu.VMEM(tokens.shape, bf16),
            pltpu.VMEM((members, tall, breadth + 8, features), bf16),
            pltpu.VMEM((features, 4 * features), f32),
            pltpu.VMEM((members, tall, breadth, features), bf16),
            pltpu.VMEM((members, tall, breadth + 8, 2 * features), bf16),
            pltpu.SemaphoreType.DMA((2,)),
        ),
        far_outs=(2, 3),
        flops=12 * cells * features * features,
        limit=37 << 20,
    )
    other = lax.ppermute(send, "core", [(0, 1), (1, 0)])
    both = call(add_kernel, shape(rows, pairs, deep, wide), (keep, other)).reshape(rows * pairs, deep, wide)
    parts = lax.all_to_all(both, ("row", "pair"), 0, 0, tiled=True)
    gt, left, right = call(
        token_kernel,
        (
            shape(members, tall, breadth, features),
            shape(members, tall // 2, 8, features),
            shape(members, tall // 2, 8, features),
        ),
        (kv, dq, w_qkv),
        flops=6 * cells * features * features,
        limit=20 << 20,
    )
    back_left, back_right = shift(right, COLS, 1), shift(left, COLS, -1)
    halo = shape(members, 4, breadth, features)
    up, down = call(halo_kernel, (halo, halo), (gt, back_left, back_right))
    back_top, back_bottom = shift(down, "row", 1), shift(up, "row", -1)
    grad_tokens = call(
        join_kernel, shape(*tokens.shape), (gt, back_left, back_right, back_top, back_bottom)
    )
    total, square = call(
        total_kernel,
        (shape(deep, wide, dtype=f32), shape(2 * rows * pairs, wide, dtype=f32)),
        (parts,),
    )
    squares = lax.all_to_all(square, ("row", "pair", "core"), 0, 0, tiled=True)
    main = 3 * features // (2 * pairs)
    grad_qkv, grad_w_out = call(
        clip_kernel,
        (shape(deep, main, dtype=f32), shape(wide - main, deep, dtype=f32)),
        (total, squares),
    )
    return grad_tokens, grad_qkv, grad_w_out.T


def solution(mesh):
    rows, cols = mesh.devices.shape
    split = jax.sharding.Mesh(mesh.devices.reshape(rows, cols // 2, 2), ("row",) + COLS)
    cells = P(None, "row", COLS, None)
    return jax.shard_map(
        body,
        mesh=split,
        in_specs=(cells, P(), P(), cells, cells, cells, cells, cells, P()),
        out_specs=(cells, P("row", COLS), P("row", COLS)),
        check_vma=False,
    )
```

time: 127 us -> 121 us (0.953)
  waiting for transfers between devices: 34 us -> 22.8 us
  starting transfers between devices: 50.3 us -> 54.8 us
  Pallas kernels: 32.2 us -> 35.3 us
  other arithmetic: 1.36 us -> 0 us
    ppermute x8 -> x10, waiting for transfers between devices: 23 us -> 11.8 us  [shift(): lax.ppermute(x, axes, [(i, i + by) for i in range(size) if 0 <= i + by <...]
    ppermute x8 -> x10, starting transfers between devices: 21.5 us -> 28.2 us  [shift(): lax.ppermute(x, axes, [(i, i + by) for i in range(size) if 0 <= i + by <...]
    pallas_call x9 -> x11, Pallas kernels: 32.2 us -> 35.3 us  [call(): pl.pallas_call(kernel, out_shape=outs, in_specs=[SMEM if n in smem else A...]
    all_to_all x1, starting transfers between devices: 16.8 us -> 14.5 us  [body(): parts = lax.all_to_all(both, ('row', 'pair'), 0, 0, tiled=True)]
    convert_element_type x1 -> x0, other arithmetic: 1.36 us -> none  [body(): (keep.astype(f32) + other.astype(f32)).astype(bf16)]
    unnamed x26 -> x22, local copies, waits for them, and re-layouts: 7.41 us -> 6.37 us
  transfers between devices with their start and end apart: 11 -> 13, of which waited for: 8 -> 6; matrix products, arithmetic and copies ran while one was open for 0% -> 0% of each run, Pallas kernels for 5% -> 11%
where the time goes in v3:
time: 121 us; the launch traced here: 120 us
  starting transfers between devices  54.8 us (45%)
  Pallas kernels  35.3 us (29%)
  waiting for transfers between devices  22.8 us (19%)
  local copies, waits for them, and re-layouts  6.37 us (5%)
    pallas_call x11, Pallas kernels, call(): pl.pallas_call(kernel, out_shape=outs, in_specs=[SMEM if n in smem else A...  35.3 us
    ppermute x10, starting transfers between devices, shift(): lax.ppermute(x, axes, [(i, i + by) for i in range(size) if 0 <= i + by <...  28.2 us
    all_to_all x1, starting transfers between devices, body(): parts = lax.all_to_all(both, ('row', 'pair'), 0, 0, tiled=True)  14.5 us
    all_to_all x1, starting transfers between devices, body(): squares = lax.all_to_all(square, ('row', 'pair', 'core'), 0, 0, tiled=True)  12 us
    ppermute x10, waiting for transfers between devices, shift(): lax.ppermute(x, axes, [(i, i + by) for i in range(size) if 0 <= i + by <...  11.8 us
    all_to_all x1, waiting for transfers between devices, body(): squares = lax.all_to_all(square, ('row', 'pair', 'core'), 0, 0, tiled=True)  8.41 us
    unnamed x22, local copies, waits for them, and re-layouts  6.37 us
    ppermute x1, waiting for transfers between devices, body(): other = lax.ppermute(send, 'core', [(0, 1), (1, 0)])  2.65 us
  transfers between devices with their start and end apart: 13, of which 6 were waited for; matrix products, arithmetic and copies ran while one was open for 0% of the time, Pallas kernels for 11%

profile of v3, /device:TPU:1, one launch (start us, length us, event | category | flops | bytes accessed | tf_op | source)
XLA Modules:
  0.0 120.2 jit_solution(15412493894650210192)
XLA Ops:
  0.7 3.9 %shard_map.112 = (f32[2,3,2,1536]{3,2,1,0:T(2,128)}, bf16[2,36,8,512]{3,2,1,0:T(8,128)(2,1)}, bf16[2,36,8,512]{3,2,1,0:T(8,128)(2,1)}, bf16[3,2,4,16,512]{4,3,2,1,0:T(8,128)(2,1)}, bf16[3,2,4,16,512]{4,3,2,1,0:T(8,128)(2,1)}) custom-call(s32[2,3,2,24]{3,2,1,0:T(2,128)} %scale_ref.1, bf16[2,24,16,512]{3,2,1,0:T(8,128)(2,1)} %k_ref.3, ...), custom_call_target="tpu_custom_call" | custom-call | bytes 4400256 | tf_op jit(solution)/shard_map/pallas_call | solution.py:27
  4.6 4.5 %collective-permute-start.2 = (bf16[2,36,8,512]{3,2,1,0:T(8,128)(2,1)}, bf16[2,36,8,512]{3,2,1,0:T(8,128)(2,1)S(1)}, u32[]{:S(2)}, u32[]{:S(2)}) collective-permute-start(bf16[2,36,8,512]{3,2,1,0:T(8,128)(2,1)} %get-tuple-element.41), channel_id=1, source_target_pairs={{0,1},{1,2},{2,3},{3,4},{4,5},{5,6},{6,7},{7,8},{8,9},{9,10},{10,1... | collective-permute-start | bytes 1769480 | tf_op jit(solution)/shard_map/ppermute | solution.py:474
  9.1 1.9 %collective-permute-start.3 = (bf16[2,36,8,512]{3,2,1,0:T(8,128)(2,1)}, bf16[2,36,8,512]{3,2,1,0:T(8,128)(2,1)S(1)}, u32[]{:S(2)}, u32[]{:S(2)}) collective-permute-start(bf16[2,36,8,512]{3,2,1,0:T(8,128)(2,1)} %get-tuple-element.42), channel_id=1, source_target_pairs={{1,0},{2,1},{3,2},{4,3},{5,4},{6,5},{7,6},{8,7},{9,8},{10,9},{11,1... | collective-permute-start | bytes 1769480 | tf_op jit(solution)/shard_map/ppermute | solution.py:474
  11.1 3.6 %collective-permute-start = (bf16[3,2,4,16,512]{4,3,2,1,0:T(8,128)(2,1)}, bf16[3,2,4,16,512]{4,3,2,1,0:T(8,128)(2,1)S(1)}, u32[]{:S(2)}, u32[]{:S(2)}) collective-permute-start(bf16[3,2,4,16,512]{4,3,2,1,0:T(8,128)(2,1)} %get-tuple-element.37), channel_id=1, source_target_pairs={{0,16},{16,32},{32,48},{48,64},{64,80},{80,96},{96,112},{1,17},{17... | collective-permute-start | bytes 1179656 | tf_op jit(solution)/shard_map/ppermute | solution.py:474
  14.6 1.3 %collective-permute-start.1 = (bf16[3,2,4,16,512]{4,3,2,1,0:T(8,128)(2,1)}, bf16[3,2,4,16,512]{4,3,2,1,0:T(8,128)(2,1)S(1)}, u32[]{:S(2)}, u32[]{:S(2)}) collective-permute-start(bf16[3,2,4,16,512]{4,3,2,1,0:T(8,128)(2,1)} %get-tuple-element.38), channel_id=1, source_target_pairs={{16,0},{32,16},{48,32},{64,48},{80,64},{96,80},{112,96},{17,1},{33... | collective-permute-start | bytes 1179656 | tf_op jit(solution)/shard_map/ppermute | solution.py:474
  16.0 1.1 copy-done.6
  17.1 1.0 copy-done.7
  18.1 0.9 copy-done.8
  19.0 1.7 %shard_map.113 = (bf16[2,24,16,512]{3,2,1,0:T(8,128)(2,1)S(1)}, bf16[2,24,16,512]{3,2,1,0:T(8,128)(2,1)S(1)}, bf16[2,24,16,512]{3,2,1,0:T(8,128)(2,1)S(1)}) custom-call(s32[2,2]{1,0:T(2,128)S(1)} %copy-done.10, bf16[2,24,16,512]{3,2,1,0:T(8,128)(2,1)S(1)} %copy-done.5, bf16[2,24,16,512]{3,2,1,0:T(8,128)(2,1)S(1)} %copy-done.6, ...), custom_call_target="tpu_custom_call" | custom-call | flops 402653184 | bytes 4530192 | tf_op jit(solution)/shard_map/pallas_call | solution.py:27
  20.8 1.7 %collective-permute-done.top_ref = bf16[3,2,4,16,512]{4,3,2,1,0:T(8,128)(2,1)S(1)} collective-permute-done((bf16[3,2,4,16,512]{4,3,2,1,0:T(8,128)(2,1)}, bf16[3,2,4,16,512]{4,3,2,1,0:T(8,128)(2,1)S(1)}, u32[]{:S(2)}, u32[]{:S(2)}) %collective-permute-start) | collective-permute-done | bytes 393248 | tf_op jit(solution)/shard_map/ppermute | solution.py:474
  22.5 4.0 %collective-permute-done.1.bottom_ref = bf16[3,2,4,16,512]{4,3,2,1,0:T(8,128)(2,1)S(1)} collective-permute-done((bf16[3,2,4,16,512]{4,3,2,1,0:T(8,128)(2,1)}, bf16[3,2,4,16,512]{4,3,2,1,0:T(8,128)(2,1)S(1)}, u32[]{:S(2)}, u32[]{:S(2)}) %collective-permute-start.1) | collective-permute-done | bytes 393248 | tf_op jit(solution)/shard_map/ppermute | solution.py:474
  26.6 5.0 %collective-permute-start.4 = (bf16[2,12,8,512]{3,2,1,0:T(8,128)(2,1)S(1)}, bf16[2,12,8,512]{3,2,1,0:T(8,128)(2,1)S(1)}, u32[]{:S(2)}, u32[]{:S(2)}) collective-permute-start(bf16[2,12,8,512]{3,2,1,0:T(8,128)(2,1)S(1)} %get-tuple-element.52), channel_id=1, source_target_pairs={{0,1},{1,2},{2,3},{3,4},{4,5},{5,6},{6,7},{7,8},{8,9},{9,10},{10,1... | collective-permute-start | bytes 589832 | tf_op jit(solution)/shard_map/ppermute | solution.py:474
  31.6 1.9 %collective-permute-start.5 = (bf16[2,12,8,512]{3,2,1,0:T(8,128)(2,1)S(1)}, bf16[2,12,8,512]{3,2,1,0:T(8,128)(2,1)S(1)}, u32[]{:S(2)}, u32[]{:S(2)}) collective-permute-start(bf16[2,12,8,512]{3,2,1,0:T(8,128)(2,1)S(1)} %get-tuple-element.53), channel_id=1, source_target_pairs={{1,0},{2,1},{3,2},{4,3},{5,4},{6,5},{7,6},{8,7},{9,8},{10,9},{11,1... | collective-permute-start | bytes 589832 | tf_op jit(solution)/shard_map/ppermute | solution.py:474
  33.6 6.7 %shard_map.114 = (bf16[2,2,24,16,512]{4,3,2,1,0:T(8,128)(2,1)S(1)}, bf16[2,2,24,16,512]{4,3,2,1,0:T(8,128)(2,1)S(1)}, f32[2,2,16,16,512]{4,3,2,1,0:T(8,128)S(1)}...) custom-call(bf16[2,24,16,512]{3,2,1,0:T(8,128)(2,1)S(1)} %get-tuple-el, ...), custom_call_target="tpu_custom_call" | custom-call | flops 805306368 | bytes 12263424 | tf_op jit(solution)/shard_map/pallas_call | solution.py:27
  40.3 16.3 %shard_map.116 = (bf16[8,8,64,128]{3,2,1,0:T(8,128)(2,1)S(1)}, bf16[8,8,64,128]{3,2,1,0:T(8,128)(2,1)S(1)}, bf16[2,32,16,512]{3,2,1,0:T(8,128)(2,1)S(1)}, bf16[2,32,24,1024]{3,2,1,0:T(8,128)(2,1)}) custom-call(bf16[2,24,16,512]{3,2,1,0:T(8,128)(2,1)S(1)} %get-tuple-element.36.qs_ref, bf16[2,24,16,512]{3,2,1,0:T(8,128)(2,1)S(1)} %get-tuple-element.40.do_ref, ...), custom_call_target="tpu_custom_call" | custom-call | flops 2415919104 | bytes 19660800 | tf_op jit(solution)/shard_map/pallas_call | solution.py:27
  56.7 2.6 %collective-permute-done.10.y_ref = bf16[8,8,64,128]{3,2,1,0:T(8,128)(2,1)S(1)} collective-permute-done((bf16[8,8,64,128]{3,2,1,0:T(8,128)(2,1)S(1)}, bf16[8,8,64,128]{3,2,1,0:T(8,128)(2,1)S(1)}, u32[]{:S(2)}, u32[]{:S(2)}) %collective-permute-start.10) | collective-permute-done | bytes 1048608 | tf_op jit(solution)/shard_map/ppermute | solution.py:548
  59.3 1.2 %shard_map.120 = bf16[8,8,64,128]{3,2,1,0:T(8,128)(2,1)} custom-call(bf16[8,8,64,128]{3,2,1,0:T(8,128)(2,1)S(1)} %get-tuple-element.61.x_ref, bf16[8,8,64,128]{3,2,1,0:T(8,128)(2,1)S(1)} %collective-permute-done.10.y_ref), custom_call_target="tpu_custom_call" | custom-call | bytes 3145728 | tf_op jit(solution)/shard_map/pallas_call | solution.py:27
  60.6 14.5 %all-to-all-start = ((bf16[64,64,128]{2,1,0:T(8,128)(2,1)}), bf16[64,64,128]{2,1,0:T(8,128)(2,1)S(1)}, u32[]{:S(2)}, u32[]{:S(2)}) async-start(bf16[64,64,128]{2,1,0:T(8,128)(2,1)} %bitcast), calls=%async_computation | async-start | bytes 2097152 | tf_op jit(solution)/shard_map/all_to_all | solution.py:550
  75.1 1.9 %copy-done.1 = bf16[2,32,24,1024]{3,2,1,0:T(8,128)(2,1)S(1)} copy-done((bf16[2,32,24,1024]{3,2,1,0:T(8,128)(2,1)S(1)}, bf16[2,32,24,1024]{3,2,1,0:T(8,128)(2,1)}, u32[]{:S(2)}) %copy-start.1) | copy-done | bytes 3145752
  77.0 1.4 %copy-done.4 = bf16[512,1536]{1,0:T(8,128)(2,1)S(1)} copy-done((bf16[512,1536]{1,0:T(8,128)(2,1)S(1)}, bf16[512,1536]{1,0:T(8,128)(2,1)}, u32[]{:S(2)}) %copy-start.4) | copy-done | bytes 1572888
  78.4 2.4 %shard_map.117 = (bf16[2,32,16,512]{3,2,1,0:T(8,128)(2,1)S(1)}, bf16[2,16,8,512]{3,2,1,0:T(8,128)(2,1)S(1)}, bf16[2,16,8,512]{3,2,1,0:T(8,128)(2,1)S(1)}) custom-call(bf16[2,32,24,1024]{3,2,1,0:T(8,128)(2,1)S(1)} %copy-done.1, bf16[2,32,16,512]{3,2,1,0:T(8,128)(2,1)S(1)} %get-tuple-element.55.dq_ref, bf16[512,1536]{1,0:T(8,128)(2,1)S(1)} %copy-done.4), custom_call_target="tpu_custom_call" | custom-call | flops 1207959552 | bytes 7340032 | tf_op jit(solution)/shard_map/pallas_call | solution.py:27
  80.7 3.7 %collective-permute-start.6 = (bf16[2,16,8,512]{3,2,1,0:T(8,128)(2,1)S(1)}, bf16[2,16,8,512]{3,2,1,0:T(8,128)(2,1)S(1)}, u32[]{:S(2)}, u32[]{:S(2)}) collective-permute-start(bf16[2,16,8,512]{3,2,1,0:T(8,128)(2,1)S(1)} %get-tuple-element.57), channel_id=1, source_target_pairs={{0,1},{1,2},{2,3},{3,4},{4,5},{5,6},{6,7},{7,8},{8,9},{9,10},{10,1... | collective-permute-start | bytes 786440 | tf_op jit(solution)/shard_map/ppermute | solution.py:474
  84.5 1.9 %collective-permute-start.7 = (bf16[2,16,8,512]{3,2,1,0:T(8,128)(2,1)S(1)}, bf16[2,16,8,512]{3,2,1,0:T(8,128)(2,1)S(1)}, u32[]{:S(2)}, u32[]{:S(2)}) collective-permute-start(bf16[2,16,8,512]{3,2,1,0:T(8,128)(2,1)S(1)} %get-tuple-element.58), channel_id=1, source_target_pairs={{1,0},{2,1},{3,2},{4,3},{5,4},{6,5},{7,6},{8,7},{9,8},{10,9},{11,1... | collective-permute-start | bytes 786440 | tf_op jit(solution)/shard_map/ppermute | solution.py:474
  86.4 2.9 %collective-permute-done.6.fl_ref = bf16[2,16,8,512]{3,2,1,0:T(8,128)(2,1)S(1)} collective-permute-done((bf16[2,16,8,512]{3,2,1,0:T(8,128)(2,1)S(1)}, bf16[2,16,8,512]{3,2,1,0:T(8,128)(2,1)S(1)}, u32[]{:S(2)}, u32[]{:S(2)}) %collective-permute-start.6) | collective-permute-done | bytes 262176 | tf_op jit(solution)/shard_map/ppermute | solution.py:474
  89.3 3.1 %collective-permute-done.7.fr_ref = bf16[2,16,8,512]{3,2,1,0:T(8,128)(2,1)S(1)} collective-permute-done((bf16[2,16,8,512]{3,2,1,0:T(8,128)(2,1)S(1)}, bf16[2,16,8,512]{3,2,1,0:T(8,128)(2,1)S(1)}, u32[]{:S(2)}, u32[]{:S(2)}) %collective-permute-start.7) | collective-permute-done | bytes 262176 | tf_op jit(solution)/shard_map/ppermute | solution.py:474
  92.6 3.1 %collective-permute-start.8 = (bf16[2,4,16,512]{3,2,1,0:T(8,128)(2,1)S(1)}, bf16[2,4,16,512]{3,2,1,0:T(8,128)(2,1)S(1)}, u32[]{:S(2)}, u32[]{:S(2)}) collective-permute-start(bf16[2,4,16,512]{3,2,1,0:T(8,128)(2,1)S(1)} %get-tuple-element.59), channel_id=1, source_target_pairs={{0,16},{16,32},{32,48},{48,64},{64,80},{80,96},{96,112},{1,17},{17... | collective-permute-start | bytes 393224 | tf_op jit(solution)/shard_map/ppermute | solution.py:474
  95.7 1.3 %collective-permute-start.9 = (bf16[2,4,16,512]{3,2,1,0:T(8,128)(2,1)S(1)}, bf16[2,4,16,512]{3,2,1,0:T(8,128)(2,1)S(1)}, u32[]{:S(2)}, u32[]{:S(2)}) collective-permute-start(bf16[2,4,16,512]{3,2,1,0:T(8,128)(2,1)S(1)} %get-tuple-element.60), channel_id=1, source_target_pairs={{16,0},{32,16},{48,32},{64,48},{80,64},{96,80},{112,96},{17,1},{33... | collective-permute-start | bytes 393224 | tf_op jit(solution)/shard_map/ppermute | solution.py:474
  97.0 0.8 shard_map.121
  97.8 12.0 %all-to-all-start.1 = ((f32[128,1,128]{2,1,0:T(1,128)}), f32[128,1,128]{2,1,0:T(1,128)S(1)}, u32[]{:S(2)}, u32[]{:S(2)}) async-start(f32[128,1,128]{2,1,0:T(1,128)} %bitcast.2), calls=%async_computation.1 | async-start | bytes 131072 | tf_op jit(solution)/shard_map/all_to_all | solution.py:574
  109.8 1.2 shard_map.119
  111.0 8.4 %all-to-all-done.1 = f32[128,1,128]{2,1,0:T(1,128)S(1)} async-done(((f32[128,1,128]{2,1,0:T(1,128)}), f32[128,1,128]{2,1,0:T(1,128)S(1)}, u32[]{:S(2)}, u32[]{:S(2)}) %all-to-all-start.1) | async-done | bytes 65568 | tf_op jit(solution)/shard_map/all_to_all | solution.py:574
  119.4 0.8 shard_map.122
  (27 shorter events, 0.3 us)
Async XLA Ops:
  0.6 32.9 %copy-start.3 = (bf16[2,24,16,512]{3,2,1,0:T(8,128)(2,1)S(1)}, bf16[2,24,16,512]{3,2,1,0:T(8,128)(2,1)}, u32[]{:S(2)}) copy-start(bf16[2,24,16,512]{3,2,1,0:T(8,128)(2,1)} %v_ref.3) | copy-start | bytes 2359300
  0.6 32.9 %copy-start.2 = (bf16[2,24,16,512]{3,2,1,0:T(8,128)(2,1)S(1)}, bf16[2,24,16,512]{3,2,1,0:T(8,128)(2,1)}, u32[]{:S(2)}) copy-start(bf16[2,24,16,512]{3,2,1,0:T(8,128)(2,1)} %k_ref.3) | copy-start | bytes 2359300
  0.7 15.3 %copy-start.10 = (s32[2,2]{1,0:T(2,128)S(1)}, s32[2,2]{1,0:T(2,128)}, u32[]{:S(2)}) copy-start(s32[2,2]{1,0:T(2,128)} %crop_ref.1) | copy-start | bytes 52
  0.7 15.3 %copy-start.5 = (bf16[2,24,16,512]{3,2,1,0:T(8,128)(2,1)S(1)}, bf16[2,24,16,512]{3,2,1,0:T(8,128)(2,1)}, u32[]{:S(2)}) copy-start(bf16[2,24,16,512]{3,2,1,0:T(8,128)(2,1)} %q_ref.1) | copy-start | bytes 2359300
  4.6 28.9 %collective-permute-start.2 = (bf16[2,36,8,512]{3,2,1,0:T(8,128)(2,1)}, bf16[2,36,8,512]{3,2,1,0:T(8,128)(2,1)S(1)}, u32[]{:S(2)}, u32[]{:S(2)}) collective-permute-start(bf16[2,36,8,512]{3,2,1,0:T(8,128)(2,1)} %get-tuple-element.41), channel_id=1, source_target_pairs={{0,1},{1,2},{2,3},{3,4},{4,5},{5,6},{6,7},{7,8},{8,9},{9,10},{10,1... | collective-permute-start | bytes 1769480 | tf_op jit(solution)/shard_map/ppermute | solution.py:474
  9.1 24.4 %collective-permute-start.3 = (bf16[2,36,8,512]{3,2,1,0:T(8,128)(2,1)}, bf16[2,36,8,512]{3,2,1,0:T(8,128)(2,1)S(1)}, u32[]{:S(2)}, u32[]{:S(2)}) collective-permute-start(bf16[2,36,8,512]{3,2,1,0:T(8,128)(2,1)} %get-tuple-element.42), channel_id=1, source_target_pairs={{1,0},{2,1},{3,2},{4,3},{5,4},{6,5},{7,6},{8,7},{9,8},{10,9},{11,1... | collective-permute-start | bytes 1769480 | tf_op jit(solution)/shard_map/ppermute | solution.py:474
  11.1 11.4 %collective-permute-start = (bf16[3,2,4,16,512]{4,3,2,1,0:T(8,128)(2,1)}, bf16[3,2,4,16,512]{4,3,2,1,0:T(8,128)(2,1)S(1)}, u32[]{:S(2)}, u32[]{:S(2)}) collective-permute-start(bf16[3,2,4,16,512]{4,3,2,1,0:T(8,128)(2,1)} %get-tuple-element.37), channel_id=1, source_target_pairs={{0,16},{16,32},{32,48},{48,64},{64,80},{80,96},{96,112},{1,17},{17... | collective-permute-start | bytes 1179656 | tf_op jit(solution)/shard_map/ppermute | solution.py:474
  14.6 11.8 %collective-permute-start.1 = (bf16[3,2,4,16,512]{4,3,2,1,0:T(8,128)(2,1)}, bf16[3,2,4,16,512]{4,3,2,1,0:T(8,128)(2,1)S(1)}, u32[]{:S(2)}, u32[]{:S(2)}) collective-permute-start(bf16[3,2,4,16,512]{4,3,2,1,0:T(8,128)(2,1)} %get-tuple-element.38), channel_id=1, source_target_pairs={{16,0},{32,16},{48,32},{64,48},{80,64},{96,80},{112,96},{17,1},{33... | collective-permute-start | bytes 1179656 | tf_op jit(solution)/shard_map/ppermute | solution.py:474
  16.0 1.1 copy-start.6
  17.1 1.0 copy-start.7
  18.1 0.9 copy-start.8
  19.0 14.5 %copy-start.9 = (f32[2,3,2,1536]{3,2,1,0:T(2,128)S(1)}, f32[2,3,2,1536]{3,2,1,0:T(2,128)}, u32[]{:S(2)}) copy-start(f32[2,3,2,1536]{3,2,1,0:T(2,128)} %get-tuple-element.35.fac_ref) | copy-start | bytes 221188
  26.6 13.7 %collective-permute-start.4 = (bf16[2,12,8,512]{3,2,1,0:T(8,128)(2,1)S(1)}, bf16[2,12,8,512]{3,2,1,0:T(8,128)(2,1)S(1)}, u32[]{:S(2)}, u32[]{:S(2)}) collective-permute-start(bf16[2,12,8,512]{3,2,1,0:T(8,128)(2,1)S(1)} %get-tuple-element.52), channel_id=1, source_target_pairs={{0,1},{1,2},{2,3},{3,4},{4,5},{5,6},{6,7},{7,8},{8,9},{9,10},{10,1... | collective-permute-start | bytes 589832 | tf_op jit(solution)/shard_map/ppermute | solution.py:474
  31.6 8.7 %collective-permute-start.5 = (bf16[2,12,8,512]{3,2,1,0:T(8,128)(2,1)S(1)}, bf16[2,12,8,512]{3,2,1,0:T(8,128)(2,1)S(1)}, u32[]{:S(2)}, u32[]{:S(2)}) collective-permute-start(bf16[2,12,8,512]{3,2,1,0:T(8,128)(2,1)S(1)} %get-tuple-element.53), channel_id=1, source_target_pairs={{1,0},{2,1},{3,2},{4,3},{5,4},{6,5},{7,6},{8,7},{9,8},{10,9},{11,1... | collective-permute-start | bytes 589832 | tf_op jit(solution)/shard_map/ppermute | solution.py:474
  33.6 6.7 %copy-start = (bf16[2,24,16,512]{3,2,1,0:T(8,128)(2,1)S(1)}, bf16[2,24,16,512]{3,2,1,0:T(8,128)(2,1)}, u32[]{:S(2)}) copy-start(bf16[2,24,16,512]{3,2,1,0:T(8,128)(2,1)} %tok_ref.3) | copy-start | bytes 2359300
  56.6 2.7 %collective-permute-start.10 = (bf16[8,8,64,128]{3,2,1,0:T(8,128)(2,1)S(1)}, bf16[8,8,64,128]{3,2,1,0:T(8,128)(2,1)S(1)}, u32[]{:S(2)}, u32[]{:S(2)}) collective-permute-start(bf16[8,8,64,128]{3,2,1,0:T(8,128)(2,1)S(1)} %get-tuple-element.62), channel_id=1, source_target_pairs={{0,1},{1,0},{2,3},{3,2},{4,5},{5,4},{6,7},{7,6},{8,9},{9,8},{10,11... | collective-permute-start | bytes 3145736 | tf_op jit(solution)/shard_map/ppermute | solution.py:548
  60.6 36.4 %all-to-all-start = ((bf16[64,64,128]{2,1,0:T(8,128)(2,1)}), bf16[64,64,128]{2,1,0:T(8,128)(2,1)S(1)}, u32[]{:S(2)}, u32[]{:S(2)}) async-start(bf16[64,64,128]{2,1,0:T(8,128)(2,1)} %bitcast), calls=%async_computation | async-start | bytes 2097152 | tf_op jit(solution)/shard_map/all_to_all | solution.py:550
  75.1 1.9 %copy-start.1 = (bf16[2,32,24,1024]{3,2,1,0:T(8,128)(2,1)S(1)}, bf16[2,32,24,1024]{3,2,1,0:T(8,128)(2,1)}, u32[]{:S(2)}) copy-start(bf16[2,32,24,1024]{3,2,1,0:T(8,128)(2,1)} %get-tuple-element.54.kv_ref) | copy-start | bytes 9437188
  77.0 1.4 %copy-start.4 = (bf16[512,1536]{1,0:T(8,128)(2,1)S(1)}, bf16[512,1536]{1,0:T(8,128)(2,1)}, u32[]{:S(2)}) copy-start(bf16[512,1536]{1,0:T(8,128)(2,1)} %w_ref.3) | copy-start | bytes 4718596
  80.7 8.6 %collective-permute-start.6 = (bf16[2,16,8,512]{3,2,1,0:T(8,128)(2,1)S(1)}, bf16[2,16,8,512]{3,2,1,0:T(8,128)(2,1)S(1)}, u32[]{:S(2)}, u32[]{:S(2)}) collective-permute-start(bf16[2,16,8,512]{3,2,1,0:T(8,128)(2,1)S(1)} %get-tuple-element.57), channel_id=1, source_target_pairs={{0,1},{1,2},{2,3},{3,4},{4,5},{5,6},{6,7},{7,8},{8,9},{9,10},{10,1... | collective-permute-start | bytes 786440 | tf_op jit(solution)/shard_map/ppermute | solution.py:474
  84.5 8.0 %collective-permute-start.7 = (bf16[2,16,8,512]{3,2,1,0:T(8,128)(2,1)S(1)}, bf16[2,16,8,512]{3,2,1,0:T(8,128)(2,1)S(1)}, u32[]{:S(2)}, u32[]{:S(2)}) collective-permute-start(bf16[2,16,8,512]{3,2,1,0:T(8,128)(2,1)S(1)} %get-tuple-element.58), channel_id=1, source_target_pairs={{1,0},{2,1},{3,2},{4,3},{5,4},{6,5},{7,6},{8,7},{9,8},{10,9},{11,1... | collective-permute-start | bytes 786440 | tf_op jit(solution)/shard_map/ppermute | solution.py:474
  92.6 17.3 %collective-permute-start.8 = (bf16[2,4,16,512]{3,2,1,0:T(8,128)(2,1)S(1)}, bf16[2,4,16,512]{3,2,1,0:T(8,128)(2,1)S(1)}, u32[]{:S(2)}, u32[]{:S(2)}) collective-permute-start(bf16[2,4,16,512]{3,2,1,0:T(8,128)(2,1)S(1)} %get-tuple-element.59), channel_id=1, source_target_pairs={{0,16},{16,32},{32,48},{48,64},{64,80},{80,96},{96,112},{1,17},{17... | collective-permute-start | bytes 393224 | tf_op jit(solution)/shard_map/ppermute | solution.py:474
  95.7 14.2 %collective-permute-start.9 = (bf16[2,4,16,512]{3,2,1,0:T(8,128)(2,1)S(1)}, bf16[2,4,16,512]{3,2,1,0:T(8,128)(2,1)S(1)}, u32[]{:S(2)}, u32[]{:S(2)}) collective-permute-start(bf16[2,4,16,512]{3,2,1,0:T(8,128)(2,1)S(1)} %get-tuple-element.60), channel_id=1, source_target_pairs={{16,0},{32,16},{48,32},{64,48},{80,64},{96,80},{112,96},{17,1},{33... | collective-permute-start | bytes 393224 | tf_op jit(solution)/shard_map/ppermute | solution.py:474
  97.8 21.6 %all-to-all-start.1 = ((f32[128,1,128]{2,1,0:T(1,128)}), f32[128,1,128]{2,1,0:T(1,128)S(1)}, u32[]{:S(2)}, u32[]{:S(2)}) async-start(f32[128,1,128]{2,1,0:T(1,128)} %bitcast.2), calls=%async_computation.1 | async-start | bytes 131072 | tf_op jit(solution)/shard_map/all_to_all | solution.py:574

commit v4 on v3

--- a/solution.py
+++ b/solution.py
@@ -55,7 +55,7 @@
 
 
 def edge_kernel(
-    scale_ref, k_ref, v_ref, tok_ref, fac_ref, left_ref, right_ref, up_ref, down_ref, k_buf, v_buf, t_buf, sem
+    scale_ref, k_ref, v_ref, tok_ref, fac_ref, up_ref, down_ref, left_ref, right_ref, k_buf, v_buf, t_buf, sem
 ):
     members, height, breadth, features = k_ref.shape
     tiles = breadth // 8
@@ -109,17 +109,16 @@
     right_ref[...] = jnp.where(low, turn(y1), x1).astype(bf16)
 
 
-def corner_kernel(top_ref, bottom_ref, left_ref, right_ref):
-    for b in range(top_ref.shape[1]):
-        for n, (one, two) in enumerate(
-            (
-                (top_ref.at[0, b], top_ref.at[1, b]),
-                (bottom_ref.at[0, b], bottom_ref.at[1, b]),
-                (top_ref.at[2, b], bottom_ref.at[2, b]),
-            )
-        ):
-            out = slice(4 * n, 4 * n + 4)
-            pack_columns(one, two, left_ref.at[b, out], right_ref.at[b, out])
+def corner_kernel(fl_ref, fr_ref, up_ref, down_ref):
+    members, packed = fl_ref.shape[:2]
+    height = packed * 2 // 3
+    half = height // 2
+    for b in range(members):
+        for n, (out, row) in enumerate(((up_ref, 0), (down_ref, height - 4))):
+            k, v = rims_of(fl_ref, fr_ref, b, slice(row, row + 4))
+            first = height + (row if n == 0 else row - half)
+            t = rims_of(fl_ref, fr_ref, b, slice(first, first + 4))[n]
+            out[b] = jnp.concatenate([k, v, t], 0).astype(bf16)
 
 
 def rims_of(left_ref, right_ref, b, rows):
@@ -164,16 +163,37 @@
     return row0, col0, height * lax.axis_size("row"), breadth * lax.axis_size("pair") * 2
 
 
-def attend(q, g, keys_of, i, place, emit):
+def mask_biases(bias_ref, strips, tiles, place):
+    row0, col0, frame_rows, frame_cols = place
+    wide = bias_ref.shape[2]
+
+    def key_cell(n):
+        kn = lax.broadcasted_iota(jnp.int32, (256, n), 0)
+        ks = kn % 16
+        return kn // 16, jnp.where(ks < 12, ks, ks - 16)
+
+    kr, kc = key_cell(wide)
+    qn = lax.broadcasted_iota(jnp.int32, (256, wide), 1) % 64
+    qr, qc = qn // 8, qn % 8
+    seen = (kr >= qr) & (kr <= qr + 8) & (kc >= qc - 4) & (kc <= qc + 4)
+    window = jnp.where(seen, 0.0, masked_score)
+    kr, kc = key_cell(128)
+    for n, i in enumerate(strips):
+        for t in range(tiles):
+            row, col = kr + (row0 + 8 * i - 4), kc + (col0 + 8 * t)
+            inside = (row >= 0) & (row < frame_rows) & (col >= 0) & (col < frame_cols)
+            edge = jnp.where(inside, 0.0, masked_score)
+            bias_ref[n * tiles + t] = window + jnp.concatenate([edge] * (wide // 128), 1)
+
+
+def attend(q, g, keys_of, bias_of, emit):
     features = q.shape[2]
+    tiles = q.shape[1] // 8
     head_lanes = features // HEADS
     wide = GROUP * head_lanes
-    row0, col0, frame_rows, frame_cols = place
     lane = lax.broadcasted_iota(jnp.int32, (1, wide), 1) // head_lanes
     head_mask = [(lane == h).astype(f32).astype(bf16) for h in range(GROUP)]
     first = lax.broadcasted_iota(jnp.int32, (64, 2 * head_lanes), 1) < head_lanes
-    across = (((1,), (1,)), ((), ()))
-    down = (((0,), (0,)), ((), ()))
 
     def spread(x):
         return jnp.concatenate([x * m for m in head_mask], 0)
@@ -185,49 +205,43 @@
             parts.append(jnp.where(first, x[128 * n : 128 * n + 64, lanes], x[128 * n + 64 : 128 * n + 128, lanes]))
         return jnp.concatenate(parts, 1)
 
-    outs, grads = [], []
-    for t in range(q.shape[1] // 8):
-        qn = lax.broadcasted_iota(jnp.int32, (64, 256), 0)
-        kn = lax.broadcasted_iota(jnp.int32, (64, 256), 1)
-        qr, qc = qn // 8, qn % 8
-        kr, ks = kn // 16, kn % 16
-        kc = jnp.where(ks < 12, ks, ks - 16)
-        row = row0 + 8 * i - 4 + kr
-        col = col0 + 8 * t + kc
-        ok = (kr >= qr) & (kr <= qr + 8) & (kc >= qc - 4) & (kc <= qc + 4)
-        ok &= (row >= 0) & (row < frame_rows) & (col >= 0) & (col < frame_cols)
-        bias = jnp.concatenate([jnp.where(ok, 0.0, masked_score)] * GROUP, 0)
+    def dot(x, y, left, right):
+        return lax.dot_general(x, y, (((left,), (right,)), ((), ())), preferred_element_type=f32)
+
+    groups = []
+    for t in range(tiles):
         q64 = q[:, 8 * t : 8 * t + 8].reshape(64, features).astype(bf16)
         g64 = g[:, 8 * t : 8 * t + 8].reshape(64, features).astype(bf16)
-        ot, dqt = [], []
-        for lanes in [slice(n * wide, (n + 1) * wide) for n in range(HEADS // GROUP)]:
-            qx, gx = spread(q64[:, lanes]), spread(g64[:, lanes])
+        for n in range(HEADS // GROUP):
+            lanes = slice(n * wide, (n + 1) * wide)
             k, v = keys_of(t, lanes)
-            s = lax.dot_general(qx, k, across, preferred_element_type=f32) + bias
-            w = jnp.exp(s - jnp.max(s, 1, keepdims=True))
-            p = w * (1.0 / jnp.sum(w, 1, keepdims=True))
-            ph = p.astype(bf16)
-            o = jnp.dot(ph, v, preferred_element_type=f32).astype(bf16).astype(f32)
-            delta = jnp.sum(o * gx.astype(f32), 1, keepdims=True)
-            dp = lax.dot_general(gx, v, across, preferred_element_type=f32)
-            ds = (p * (dp - delta)).astype(bf16)
-            dq = jnp.dot(ds, k, preferred_element_type=f32)
-            dk = lax.dot_general(ds, qx, down, preferred_element_type=f32).reshape(16, 16, wide)
-            dv = lax.dot_general(ph, gx, down, preferred_element_type=f32).reshape(16, 16, wide)
-            ot.append(gather(o))
-            dqt.append(gather(dq) * 0.125)
-            emit(t, lanes, dk, dv)
-        outs.append(jnp.concatenate(ot, 1).reshape(8, 8, features))
-        grads.append(jnp.concatenate(dqt, 1).reshape(8, 8, features))
-    return jnp.concatenate(outs, 1), jnp.concatenate(grads, 1)
+            groups.append((t, lanes, spread(q64[:, lanes]), spread(g64[:, lanes]), k, v))
+    scores = [dot(k, qx, 1, 1) + bias_of(t) for t, _, qx, _, k, _ in groups]
+    grad_probs = [dot(v, gx, 1, 1) for _, _, _, gx, _, v in groups]
+    halves = []
+    for s, dp in zip(scores, grad_probs):
+        w = jnp.exp(s - jnp.max(s, 0, keepdims=True))
+        scale = 1.0 / jnp.sum(w, 0, keepdims=True)
+        delta = jnp.sum(w * dp, 0, keepdims=True) * scale
+        p = w * scale
+        halves.append((p.astype(bf16), (p * (dp - delta)).astype(bf16)))
+    outs, grads = [[] for _ in range(tiles)], [[] for _ in range(tiles)]
+    for (t, lanes, qx, gx, k, v), (ph, ds) in zip(groups, halves):
+        outs[t].append(gather(dot(ph, v, 0, 0)))
+        grads[t].append(gather(dot(ds, k, 0, 0)) * 0.125)
+        dk = dot(ds, qx, 1, 0).reshape(16, 16, wide)
+        dv = dot(ph, gx, 1, 0).reshape(16, 16, wide)
+        emit(t, lanes, dk, dv)
+    join = lambda x: jnp.concatenate([jnp.concatenate(y, 1).reshape(8, 8, features) for y in x], 1)
+    return join(outs), join(grads)
 
 
 def middle_kernel(
-    qs_ref, do_ref, k_ref, v_ref, fac_ref, fl_ref, fr_ref, kt_ref, vt_ref, dk_ref, dv_ref, o_ref, dq_ref
+    qs_ref, do_ref, k_ref, v_ref, fac_ref, fl_ref, fr_ref, kt_ref, vt_ref, dk_ref, dv_ref, o_ref, dq_ref, bias_ref
 ):
     members, height, breadth, features = qs_ref.shape
     strips, tiles = height // 8, breadth // 8
-    place = place_of(height, breadth)
+    mask_biases(bias_ref, (1,), tiles, place_of(height, breadth))
     for b in range(members):
         for i in range(strips):
             rows = slice(8 * i, 8 * i + 8)
@@ -245,7 +259,7 @@
             dk_ref[b, t, :, :, lanes] = dk
             dv_ref[b, t, :, :, lanes] = dv
 
-        o, dq = attend(qs_ref[b, 8:16].astype(f32), do_ref[b, 8:16].astype(f32), keys_of, 1, place, emit)
+        o, dq = attend(qs_ref[b, 8:16].astype(f32), do_ref[b, 8:16].astype(f32), keys_of, lambda t: bias_ref[t], emit)
         o_ref[b] = o.astype(bf16)
         dq_ref[b] = dq.astype(bf16)
         return 0
@@ -255,24 +269,23 @@
 
 def main_kernel(
     qs_ref, do_ref, kt_ref, vt_ref, dkm_ref, dvm_ref, om_ref, dqm_ref, gm_ref, tok_ref,
-    fl_ref, fr_ref, top_ref, bottom_ref, cl_ref, cr_ref,
+    fl_ref, fr_ref, top_ref, bottom_ref, ct_ref, cb_ref,
     keep_ref, send_ref, dq_out, kv_out,
-    kh_ref, vh_ref, dkt_ref, dvt_ref, o_ref, tp_ref, all_ref, dq_ref, kv_ref, sem,
+    kh_ref, vh_ref, dkt_ref, dvt_ref, o_ref, tp_ref, all_ref, dq_ref, kv_ref, bias_ref, sem,
 ):
     members, height, breadth, features = qs_ref.shape
     tall = height + 8
     tiles = breadth // 8
-    place = place_of(height, breadth)
-    for b in range(members):
-        token_rims = rims_of(cl_ref, cr_ref, b, slice(8, 12))
-        for n, ref in enumerate((top_ref, bottom_ref)):
-            rims = rims_of(cl_ref, cr_ref, b, slice(4 * n, 4 * n + 4))
+    mask_biases(bias_ref, (0, height // 8 - 1), tiles, place_of(height, breadth))
+    for b in range(members):
+        for n, (ref, corner) in enumerate(((top_ref, ct_ref), (bottom_ref, cb_ref))):
+            rims = [corner[b, 4 * m : 4 * m + 4].astype(f32) for m in range(3)]
             for m, out in enumerate((kh_ref, vh_ref)):
                 blocks = [ref[m, b, :, 8 * j : 8 * j + 8].astype(f32) for j in range(tiles)]
                 for t in range(tiles):
                     out[n, b, t] = key_tile(blocks, rims[m], t)
             halo = slice(0, 4) if n == 0 else slice(tall - 4, tall)
-            tp_ref[b, halo] = jnp.concatenate([ref[2, b].astype(f32), token_rims[n]], 1).astype(bf16)
+            tp_ref[b, halo] = jnp.concatenate([ref[2, b].astype(f32), rims[2]], 1).astype(bf16)
             dq_ref[b, halo] = jnp.zeros((4, breadth, features), bf16)
         half = height // 2
         for r in range(0, half, 4):
@@ -304,7 +317,7 @@
                         ref[b, t, 24:32, :, lanes] = x[8:16]
 
             rows = slice(8 * i, 8 * i + 8)
-            o, dq = attend(qs_ref[b, rows].astype(f32), do_ref[b, rows].astype(f32), keys_of, i, place, emit)
+            o, dq = attend(qs_ref[b, rows].astype(f32), do_ref[b, rows].astype(f32), keys_of, lambda t: bias_ref[n * tiles + t], emit)
             o_ref[b, rows] = o.astype(bf16)
             dq_ref[b, 8 * i + 4 : 8 * i + 12] = dq.astype(bf16)
         return 0
@@ -480,11 +493,11 @@
     packed = height + height // 2
     packed_columns = shape(members, packed, 8, features)
     strip = shape(3, members, 4, breadth, features)
-    factor, left, right, up, down = call(
+    factor, up, down, left, right = call(
         edge_kernel,
         (
             shape(*scale_exp.shape[:3], 3 * features, dtype=f32),
-            packed_columns, packed_columns, strip, strip,
+            strip, strip, packed_columns, packed_columns,
         ),
         (scale_exp, k_saved, v_saved, tokens),
         scratch=(pltpu.VMEM(tokens.shape, bf16),) * 3 + (pltpu.SemaphoreType.DMA((3,)),),
@@ -492,7 +505,6 @@
         limit=58 << 20,
     )
     top, bottom = shift(down, "row", 1), shift(up, "row", -1)
-    from_left, from_right = shift(right, COLS, 1), shift(left, COLS, -1)
     cells = members * height * breadth
     qs, gm, do = call(
         prepare_kernel,
@@ -501,10 +513,10 @@
         smem=(0,),
         flops=2 * cells * features * features,
     )
+    from_left, from_right = shift(right, COLS, 1), shift(left, COLS, -1)
     corner = shape(members, 12, 8, features)
-    top, bottom, do = lax.optimization_barrier((top, bottom, do))
-    left, right = call(corner_kernel, (corner, corner), (top, bottom))
-    corner_left, corner_right = shift(right, COLS, 1), shift(left, COLS, -1)
+    up, down = call(corner_kernel, (corner, corner), (from_left, from_right))
+    corner_top, corner_bottom = shift(down, "row", 1), shift(up, "row", -1)
     tiles = breadth // 8
     own_tiles = shape(members, tiles, height, 16, features)
     middle_tiles = shape(members, tiles, 16, 16, features, dtype=f32)
@@ -513,6 +525,7 @@
         middle_kernel,
         (own_tiles, own_tiles, middle_tiles, middle_tiles, middle_rows, middle_rows),
         (qs, do, k_saved, v_saved, factor, from_left, from_right),
+        scratch=(pltpu.VMEM((tiles, 256, features // 2), f32),),
         flops=4 * cells * features * features,
         limit=20 << 20,
     )
@@ -530,7 +543,7 @@
         ),
         (
             qs, do, kt, vt, dk, dv, out, dq, gm, tokens,
-            from_left, from_right, top, bottom, corner_left, corner_right,
+            from_left, from_right, top, bottom, corner_top, corner_bottom,
         ),
         scratch=(
             halo_tiles, halo_tiles, all_tiles, all_tiles,
@@ -539,6 +552,7 @@
             pltpu.VMEM((features, 4 * features), f32),
             pltpu.VMEM((members, tall, breadth, features), bf16),
             pltpu.VMEM((members, tall, breadth + 8, 2 * features), bf16),
+            pltpu.VMEM((2 * tiles, 256, features // 2), f32),
             pltpu.SemaphoreType.DMA((2,)),
         ),
         far_outs=(2, 3),

time: 121 us -> 106 us (0.88)
  Pallas kernels: 35.3 us -> 25.4 us
  starting transfers between devices: 54.8 us -> 52.5 us
  local copies, waits for them, and re-layouts: 6.37 us -> 4.21 us
    pallas_call x11, Pallas kernels: 35.3 us -> 25.4 us  [call(): pl.pallas_call(kernel, out_shape=outs, in_specs=[SMEM if n in smem else A...]
    unnamed x22, local copies, waits for them, and re-layouts: 6.37 us -> 4.21 us
    ppermute x10, starting transfers between devices: 28.2 us -> 26.3 us  [shift(): lax.ppermute(x, axes, [(i, i + by) for i in range(size) if 0 <= i + by <...]
  transfers between devices with their start and end apart: 13 -> 13, of which waited for: 6 -> 6; matrix products, arithmetic and copies ran while one was open for 0% -> 0% of each run, Pallas kernels for 11% -> 9%
where the time goes in v4:
time: 106 us; the launch traced here: 105 us
  starting transfers between devices  52.5 us (50%)
  Pallas kernels  25.4 us (24%)
  waiting for transfers between devices  22 us (21%)
  local copies, waits for them, and re-layouts  4.21 us (4%)
    ppermute x10, starting transfers between devices, shift(): lax.ppermute(x, axes, [(i, i + by) for i in range(size) if 0 <= i + by <...  26.3 us
    pallas_call x11, Pallas kernels, call(): pl.pallas_call(kernel, out_shape=outs, in_specs=[SMEM if n in smem else A...  25.4 us
    all_to_all x1, starting transfers between devices, body(): parts = lax.all_to_all(both, ('row', 'pair'), 0, 0, tiled=True)  14.1 us
    all_to_all x1, starting transfers between devices, body(): squares = lax.all_to_all(square, ('row', 'pair', 'core'), 0, 0, tiled=True)  12 us
    ppermute x10, waiting for transfers between devices, shift(): lax.ppermute(x, axes, [(i, i + by) for i in range(size) if 0 <= i + by <...  11 us
    all_to_all x1, waiting for transfers between devices, body(): squares = lax.all_to_all(square, ('row', 'pair', 'core'), 0, 0, tiled=True)  8.41 us
    unnamed x22, local copies, waits for them, and re-layouts  4.21 us
    ppermute x1, waiting for transfers between devices, body(): other = lax.ppermute(send, 'core', [(0, 1), (1, 0)])  2.65 us
  transfers between devices with their start and end apart: 13, of which 6 were waited for; matrix products, arithmetic and copies ran while one was open for 0% of the time, Pallas kernels for 9%

profile of v4, /device:TPU:1, one launch (start us, length us, event | category | flops | bytes accessed | tf_op | source)
XLA Modules:
  0.0 105.1 jit_solution(1654692670871566516)
XLA Ops:
  0.7 3.9 %shard_map.112 = (f32[2,3,2,1536]{3,2,1,0:T(2,128)}, bf16[3,2,4,16,512]{4,3,2,1,0:T(8,128)(2,1)}, bf16[3,2,4,16,512]{4,3,2,1,0:T(8,128)(2,1)}, bf16[2,36,8,512]{3,2,1,0:T(8,128)(2,1)}, bf16[2,36,8,512]{3,2,1,0:T(8,128)(2,1)}) custom-call(s32[2,3,2,24]{3,2,1,0:T(2,128)} %scale_ref.1, bf16[2,24,16,512]{3,2,1,0:T(8,128)(2,1)} %k_ref.3, ...), custom_call_target="tpu_custom_call" | custom-call | bytes 4400256 | tf_op jit(solution)/shard_map/pallas_call | solution.py:27
  4.6 4.6 %collective-permute-start = (bf16[2,36,8,512]{3,2,1,0:T(8,128)(2,1)}, bf16[2,36,8,512]{3,2,1,0:T(8,128)(2,1)S(1)}, u32[]{:S(2)}, u32[]{:S(2)}) collective-permute-start(bf16[2,36,8,512]{3,2,1,0:T(8,128)(2,1)} %get-tuple-element.35), channel_id=1, source_target_pairs={{0,1},{1,2},{2,3},{3,4},{4,5},{5,6},{6,7},{7,8},{8,9},{9,10},{10,1... | collective-permute-start | bytes 1769480 | tf_op jit(solution)/shard_map/ppermute | solution.py:487
  9.3 1.9 %collective-permute-start.1 = (bf16[2,36,8,512]{3,2,1,0:T(8,128)(2,1)}, bf16[2,36,8,512]{3,2,1,0:T(8,128)(2,1)S(1)}, u32[]{:S(2)}, u32[]{:S(2)}) collective-permute-start(bf16[2,36,8,512]{3,2,1,0:T(8,128)(2,1)} %get-tuple-element.36), channel_id=1, source_target_pairs={{1,0},{2,1},{3,2},{4,3},{5,4},{6,5},{7,6},{8,7},{9,8},{10,9},{11,1... | collective-permute-start | bytes 1769480 | tf_op jit(solution)/shard_map/ppermute | solution.py:487
  11.2 3.6 %collective-permute-start.2 = (bf16[3,2,4,16,512]{4,3,2,1,0:T(8,128)(2,1)}, bf16[3,2,4,16,512]{4,3,2,1,0:T(8,128)(2,1)S(1)}, u32[]{:S(2)}, u32[]{:S(2)}) collective-permute-start(bf16[3,2,4,16,512]{4,3,2,1,0:T(8,128)(2,1)} %get-tuple-element.44), channel_id=1, source_target_pairs={{0,16},{16,32},{32,48},{48,64},{64,80},{80,96},{96,112},{1,17},{17... | collective-permute-start | bytes 1179656 | tf_op jit(solution)/shard_map/ppermute | solution.py:487
  14.8 1.3 %collective-permute-start.3 = (bf16[3,2,4,16,512]{4,3,2,1,0:T(8,128)(2,1)}, bf16[3,2,4,16,512]{4,3,2,1,0:T(8,128)(2,1)S(1)}, u32[]{:S(2)}, u32[]{:S(2)}) collective-permute-start(bf16[3,2,4,16,512]{4,3,2,1,0:T(8,128)(2,1)} %get-tuple-element.45), channel_id=1, source_target_pairs={{16,0},{32,16},{48,32},{64,48},{80,64},{96,80},{112,96},{17,1},{33... | collective-permute-start | bytes 1179656 | tf_op jit(solution)/shard_map/ppermute | solution.py:487
  16.1 0.3 collective-permute-done.fl_ref
  16.4 4.6 %collective-permute-done.1.fr_ref = bf16[2,36,8,512]{3,2,1,0:T(8,128)(2,1)S(1)} collective-permute-done((bf16[2,36,8,512]{3,2,1,0:T(8,128)(2,1)}, bf16[2,36,8,512]{3,2,1,0:T(8,128)(2,1)S(1)}, u32[]{:S(2)}, u32[]{:S(2)}) %collective-permute-start.1) | collective-permute-done | bytes 589856 | tf_op jit(solution)/shard_map/ppermute | solution.py:487
  21.0 0.1 shard_map.115
  21.1 3.6 %collective-permute-start.4 = (bf16[2,12,8,512]{3,2,1,0:T(8,128)(2,1)S(1)}, bf16[2,12,8,512]{3,2,1,0:T(8,128)(2,1)S(1)}, u32[]{:S(2)}, u32[]{:S(2)}) collective-permute-start(bf16[2,12,8,512]{3,2,1,0:T(8,128)(2,1)S(1)} %get-tuple-element.46), channel_id=1, source_target_pairs={{0,16},{16,32},{32,48},{48,64},{64,80},{80,96},{96,112},{1,17},{17... | collective-permute-start | bytes 589832 | tf_op jit(solution)/shard_map/ppermute | solution.py:487
  24.7 1.3 %collective-permute-start.5 = (bf16[2,12,8,512]{3,2,1,0:T(8,128)(2,1)S(1)}, bf16[2,12,8,512]{3,2,1,0:T(8,128)(2,1)S(1)}, u32[]{:S(2)}, u32[]{:S(2)}) collective-permute-start(bf16[2,12,8,512]{3,2,1,0:T(8,128)(2,1)S(1)} %get-tuple-element.47), channel_id=1, source_target_pairs={{16,0},{32,16},{48,32},{64,48},{80,64},{96,80},{112,96},{17,1},{33... | collective-permute-start | bytes 589832 | tf_op jit(solution)/shard_map/ppermute | solution.py:487
  26.0 0.9 copy-done.8
  26.9 1.7 %shard_map.113 = (bf16[2,24,16,512]{3,2,1,0:T(8,128)(2,1)S(1)}, bf16[2,24,16,512]{3,2,1,0:T(8,128)(2,1)S(1)}, bf16[2,24,16,512]{3,2,1,0:T(8,128)(2,1)S(1)}) custom-call(s32[2,2]{1,0:T(2,128)S(1)} %copy-done.10, bf16[2,24,16,512]{3,2,1,0:T(8,128)(2,1)S(1)} %copy-done.5, bf16[2,24,16,512]{3,2,1,0:T(8,128)(2,1)S(1)} %copy-done.6, ...), custom_call_target="tpu_custom_call" | custom-call | flops 402653184 | bytes 4530192 | tf_op jit(solution)/shard_map/pallas_call | solution.py:27
  28.7 3.7 %shard_map.114 = (bf16[2,2,24,16,512]{4,3,2,1,0:T(8,128)(2,1)S(1)}, bf16[2,2,24,16,512]{4,3,2,1,0:T(8,128)(2,1)S(1)}, f32[2,2,16,16,512]{4,3,2,1,0:T(8,128)S(1)}...) custom-call(bf16[2,24,16,512]{3,2,1,0:T(8,128)(2,1)S(1)} %get-tuple-el, ...), custom_call_target="tpu_custom_call" | custom-call | flops 805306368 | bytes 12263424 | tf_op jit(solution)/shard_map/pallas_call | solution.py:27
  32.4 9.4 %shard_map.116 = (bf16[8,8,64,128]{3,2,1,0:T(8,128)(2,1)S(1)}, bf16[8,8,64,128]{3,2,1,0:T(8,128)(2,1)S(1)}, bf16[2,32,16,512]{3,2,1,0:T(8,128)(2,1)S(1)}, bf16[2,32,24,1024]{3,2,1,0:T(8,128)(2,1)}) custom-call(bf16[2,24,16,512]{3,2,1,0:T(8,128)(2,1)S(1)} %get-tuple-element.33.qs_ref, bf16[2,24,16,512]{3,2,1,0:T(8,128)(2,1)S(1)} %get-tuple-element.34.do_ref, ...), custom_call_target="tpu_custom_call" | custom-call | flops 2415919104 | bytes 19660800 | tf_op jit(solution)/shard_map/pallas_call | solution.py:27
  42.0 2.6 %collective-permute-done.10.y_ref = bf16[8,8,64,128]{3,2,1,0:T(8,128)(2,1)S(1)} collective-permute-done((bf16[8,8,64,128]{3,2,1,0:T(8,128)(2,1)S(1)}, bf16[8,8,64,128]{3,2,1,0:T(8,128)(2,1)S(1)}, u32[]{:S(2)}, u32[]{:S(2)}) %collective-permute-start.10) | collective-permute-done | bytes 1048608 | tf_op jit(solution)/shard_map/ppermute | solution.py:562
  44.6 1.2 %shard_map.120 = bf16[8,8,64,128]{3,2,1,0:T(8,128)(2,1)} custom-call(bf16[8,8,64,128]{3,2,1,0:T(8,128)(2,1)S(1)} %get-tuple-element.55.x_ref, bf16[8,8,64,128]{3,2,1,0:T(8,128)(2,1)S(1)} %collective-permute-done.10.y_ref), custom_call_target="tpu_custom_call" | custom-call | bytes 3145728 | tf_op jit(solution)/shard_map/pallas_call | solution.py:27
  45.8 14.1 %all-to-all-start = ((bf16[64,64,128]{2,1,0:T(8,128)(2,1)}), bf16[64,64,128]{2,1,0:T(8,128)(2,1)S(1)}, u32[]{:S(2)}, u32[]{:S(2)}) async-start(bf16[64,64,128]{2,1,0:T(8,128)(2,1)} %bitcast), calls=%async_computation | async-start | bytes 2097152 | tf_op jit(solution)/shard_map/all_to_all | solution.py:564
  59.9 1.9 %copy-done.1 = bf16[2,32,24,1024]{3,2,1,0:T(8,128)(2,1)S(1)} copy-done((bf16[2,32,24,1024]{3,2,1,0:T(8,128)(2,1)S(1)}, bf16[2,32,24,1024]{3,2,1,0:T(8,128)(2,1)}, u32[]{:S(2)}) %copy-start.1) | copy-done | bytes 3145752
  61.8 1.4 %copy-done.4 = bf16[512,1536]{1,0:T(8,128)(2,1)S(1)} copy-done((bf16[512,1536]{1,0:T(8,128)(2,1)S(1)}, bf16[512,1536]{1,0:T(8,128)(2,1)}, u32[]{:S(2)}) %copy-start.4) | copy-done | bytes 1572888
  63.2 2.4 %shard_map.117 = (bf16[2,32,16,512]{3,2,1,0:T(8,128)(2,1)S(1)}, bf16[2,16,8,512]{3,2,1,0:T(8,128)(2,1)S(1)}, bf16[2,16,8,512]{3,2,1,0:T(8,128)(2,1)S(1)}) custom-call(bf16[2,32,24,1024]{3,2,1,0:T(8,128)(2,1)S(1)} %copy-done.1, bf16[2,32,16,512]{3,2,1,0:T(8,128)(2,1)S(1)} %get-tuple-element.49.dq_ref, bf16[512,1536]{1,0:T(8,128)(2,1)S(1)} %copy-done.4), custom_call_target="tpu_custom_call" | custom-call | flops 1207959552 | bytes 7340032 | tf_op jit(solution)/shard_map/pallas_call | solution.py:27
  65.6 3.7 %collective-permute-start.6 = (bf16[2,16,8,512]{3,2,1,0:T(8,128)(2,1)S(1)}, bf16[2,16,8,512]{3,2,1,0:T(8,128)(2,1)S(1)}, u32[]{:S(2)}, u32[]{:S(2)}) collective-permute-start(bf16[2,16,8,512]{3,2,1,0:T(8,128)(2,1)S(1)} %get-tuple-element.51), channel_id=1, source_target_pairs={{0,1},{1,2},{2,3},{3,4},{4,5},{5,6},{6,7},{7,8},{8,9},{9,10},{10,1... | collective-permute-start | bytes 786440 | tf_op jit(solution)/shard_map/ppermute | solution.py:487
  69.3 1.9 %collective-permute-start.7 = (bf16[2,16,8,512]{3,2,1,0:T(8,128)(2,1)S(1)}, bf16[2,16,8,512]{3,2,1,0:T(8,128)(2,1)S(1)}, u32[]{:S(2)}, u32[]{:S(2)}) collective-permute-start(bf16[2,16,8,512]{3,2,1,0:T(8,128)(2,1)S(1)} %get-tuple-element.52), channel_id=1, source_target_pairs={{1,0},{2,1},{3,2},{4,3},{5,4},{6,5},{7,6},{8,7},{9,8},{10,9},{11,1... | collective-permute-start | bytes 786440 | tf_op jit(solution)/shard_map/ppermute | solution.py:487
  71.2 2.9 %collective-permute-done.6.fl_ref = bf16[2,16,8,512]{3,2,1,0:T(8,128)(2,1)S(1)} collective-permute-done((bf16[2,16,8,512]{3,2,1,0:T(8,128)(2,1)S(1)}, bf16[2,16,8,512]{3,2,1,0:T(8,128)(2,1)S(1)}, u32[]{:S(2)}, u32[]{:S(2)}) %collective-permute-start.6) | collective-permute-done | bytes 262176 | tf_op jit(solution)/shard_map/ppermute | solution.py:487
  74.2 3.1 %collective-permute-done.7.fr_ref = bf16[2,16,8,512]{3,2,1,0:T(8,128)(2,1)S(1)} collective-permute-done((bf16[2,16,8,512]{3,2,1,0:T(8,128)(2,1)S(1)}, bf16[2,16,8,512]{3,2,1,0:T(8,128)(2,1)S(1)}, u32[]{:S(2)}, u32[]{:S(2)}) %collective-permute-start.7) | collective-permute-done | bytes 262176 | tf_op jit(solution)/shard_map/ppermute | solution.py:487
  77.3 0.1 shard_map.118
  77.4 3.1 %collective-permute-start.8 = (bf16[2,4,16,512]{3,2,1,0:T(8,128)(2,1)S(1)}, bf16[2,4,16,512]{3,2,1,0:T(8,128)(2,1)S(1)}, u32[]{:S(2)}, u32[]{:S(2)}) collective-permute-start(bf16[2,4,16,512]{3,2,1,0:T(8,128)(2,1)S(1)} %get-tuple-element.53), channel_id=1, source_target_pairs={{0,16},{16,32},{32,48},{48,64},{64,80},{80,96},{96,112},{1,17},{17... | collective-permute-start | bytes 393224 | tf_op jit(solution)/shard_map/ppermute | solution.py:487
  80.5 1.3 %collective-permute-start.9 = (bf16[2,4,16,512]{3,2,1,0:T(8,128)(2,1)S(1)}, bf16[2,4,16,512]{3,2,1,0:T(8,128)(2,1)S(1)}, u32[]{:S(2)}, u32[]{:S(2)}) collective-permute-start(bf16[2,4,16,512]{3,2,1,0:T(8,128)(2,1)S(1)} %get-tuple-element.54), channel_id=1, source_target_pairs={{16,0},{32,16},{48,32},{64,48},{80,64},{96,80},{112,96},{17,1},{33... | collective-permute-start | bytes 393224 | tf_op jit(solution)/shard_map/ppermute | solution.py:487
  81.8 0.8 shard_map.121
  82.7 12.0 %all-to-all-start.1 = ((f32[128,1,128]{2,1,0:T(1,128)}), f32[128,1,128]{2,1,0:T(1,128)S(1)}, u32[]{:S(2)}, u32[]{:S(2)}) async-start(f32[128,1,128]{2,1,0:T(1,128)} %bitcast.2), calls=%async_computation.1 | async-start | bytes 131072 | tf_op jit(solution)/shard_map/all_to_all | solution.py:588
  94.7 1.2 %shard_map.119 = bf16[2,24,16,512]{3,2,1,0:T(8,128)(2,1)} custom-call(bf16[2,32,16,512]{3,2,1,0:T(8,128)(2,1)S(1)} %get-tuple-element.50.gt_ref, bf16[2,16,8,512]{3,2,1,0:T(8,128)(2,1)S(1)} %collective-permute-done.6.fl_ref, bf16[2,16,8,512]{3,2,1,0:T(8,128)(2,1)S(1)} %collective-permute-done.7.fr_ref, ...), custom_call_target="tpu_custom_call" | custom-call | bytes 2621440 | tf_op jit(solution)/shard_map/pallas_call | solution.py:27
  95.8 8.4 %all-to-all-done.1 = f32[128,1,128]{2,1,0:T(1,128)S(1)} async-done(((f32[128,1,128]{2,1,0:T(1,128)}), f32[128,1,128]{2,1,0:T(1,128)S(1)}, u32[]{:S(2)}, u32[]{:S(2)}) %all-to-all-start.1) | async-done | bytes 65568 | tf_op jit(solution)/shard_map/all_to_all | solution.py:588
  104.3 0.8 shard_map.122
  (27 shorter events, 0.1 us)
Async XLA Ops:
  0.6 25.3 %copy-start.10 = (s32[2,2]{1,0:T(2,128)S(1)}, s32[2,2]{1,0:T(2,128)}, u32[]{:S(2)}) copy-start(s32[2,2]{1,0:T(2,128)} %crop_ref.1) | copy-start | bytes 52
  0.6 25.3 %copy-start.6 = (bf16[2,24,16,512]{3,2,1,0:T(8,128)(2,1)S(1)}, bf16[2,24,16,512]{3,2,1,0:T(8,128)(2,1)}, u32[]{:S(2)}) copy-start(bf16[2,24,16,512]{3,2,1,0:T(8,128)(2,1)} %g_ref.1) | copy-start | bytes 2359300
  0.7 25.3 %copy-start.5 = (bf16[2,24,16,512]{3,2,1,0:T(8,128)(2,1)S(1)}, bf16[2,24,16,512]{3,2,1,0:T(8,128)(2,1)}, u32[]{:S(2)}) copy-start(bf16[2,24,16,512]{3,2,1,0:T(8,128)(2,1)} %q_ref.1) | copy-start | bytes 2359300
  0.7 25.3 %copy-start.7 = (bf16[512,512]{1,0:T(8,128)(2,1)S(1)}, bf16[512,512]{1,0:T(8,128)(2,1)}, u32[]{:S(2)}) copy-start(bf16[512,512]{1,0:T(8,128)(2,1)} %w_ref.2) | copy-start | bytes 1572868
  4.6 24.0 %copy-start.2 = (bf16[2,24,16,512]{3,2,1,0:T(8,128)(2,1)S(1)}, bf16[2,24,16,512]{3,2,1,0:T(8,128)(2,1)}, u32[]{:S(2)}) copy-start(bf16[2,24,16,512]{3,2,1,0:T(8,128)(2,1)} %k_ref.3) | copy-start | bytes 2359300
  4.6 24.0 %copy-start.3 = (bf16[2,24,16,512]{3,2,1,0:T(8,128)(2,1)S(1)}, bf16[2,24,16,512]{3,2,1,0:T(8,128)(2,1)}, u32[]{:S(2)}) copy-start(bf16[2,24,16,512]{3,2,1,0:T(8,128)(2,1)} %v_ref.3) | copy-start | bytes 2359300
  4.6 11.8 %collective-permute-start = (bf16[2,36,8,512]{3,2,1,0:T(8,128)(2,1)}, bf16[2,36,8,512]{3,2,1,0:T(8,128)(2,1)S(1)}, u32[]{:S(2)}, u32[]{:S(2)}) collective-permute-start(bf16[2,36,8,512]{3,2,1,0:T(8,128)(2,1)} %get-tuple-element.35), channel_id=1, source_target_pairs={{0,1},{1,2},{2,3},{3,4},{4,5},{5,6},{6,7},{7,8},{8,9},{9,10},{10,1... | collective-permute-start | bytes 1769480 | tf_op jit(solution)/shard_map/ppermute | solution.py:487
  9.3 11.7 %collective-permute-start.1 = (bf16[2,36,8,512]{3,2,1,0:T(8,128)(2,1)}, bf16[2,36,8,512]{3,2,1,0:T(8,128)(2,1)S(1)}, u32[]{:S(2)}, u32[]{:S(2)}) collective-permute-start(bf16[2,36,8,512]{3,2,1,0:T(8,128)(2,1)} %get-tuple-element.36), channel_id=1, source_target_pairs={{1,0},{2,1},{3,2},{4,3},{5,4},{6,5},{7,6},{8,7},{9,8},{10,9},{11,1... | collective-permute-start | bytes 1769480 | tf_op jit(solution)/shard_map/ppermute | solution.py:487
  11.2 21.1 %collective-permute-start.2 = (bf16[3,2,4,16,512]{4,3,2,1,0:T(8,128)(2,1)}, bf16[3,2,4,16,512]{4,3,2,1,0:T(8,128)(2,1)S(1)}, u32[]{:S(2)}, u32[]{:S(2)}) collective-permute-start(bf16[3,2,4,16,512]{4,3,2,1,0:T(8,128)(2,1)} %get-tuple-element.44), channel_id=1, source_target_pairs={{0,16},{16,32},{32,48},{48,64},{64,80},{80,96},{96,112},{1,17},{17... | collective-permute-start | bytes 1179656 | tf_op jit(solution)/shard_map/ppermute | solution.py:487
  14.8 17.6 %collective-permute-start.3 = (bf16[3,2,4,16,512]{4,3,2,1,0:T(8,128)(2,1)}, bf16[3,2,4,16,512]{4,3,2,1,0:T(8,128)(2,1)S(1)}, u32[]{:S(2)}, u32[]{:S(2)}) collective-permute-start(bf16[3,2,4,16,512]{4,3,2,1,0:T(8,128)(2,1)} %get-tuple-element.45), channel_id=1, source_target_pairs={{16,0},{32,16},{48,32},{64,48},{80,64},{96,80},{112,96},{17,1},{33... | collective-permute-start | bytes 1179656 | tf_op jit(solution)/shard_map/ppermute | solution.py:487
  21.1 11.3 %collective-permute-start.4 = (bf16[2,12,8,512]{3,2,1,0:T(8,128)(2,1)S(1)}, bf16[2,12,8,512]{3,2,1,0:T(8,128)(2,1)S(1)}, u32[]{:S(2)}, u32[]{:S(2)}) collective-permute-start(bf16[2,12,8,512]{3,2,1,0:T(8,128)(2,1)S(1)} %get-tuple-element.46), channel_id=1, source_target_pairs={{0,16},{16,32},{32,48},{48,64},{64,80},{80,96},{96,112},{1,17},{17... | collective-permute-start | bytes 589832 | tf_op jit(solution)/shard_map/ppermute | solution.py:487
  24.7 7.7 %collective-permute-start.5 = (bf16[2,12,8,512]{3,2,1,0:T(8,128)(2,1)S(1)}, bf16[2,12,8,512]{3,2,1,0:T(8,128)(2,1)S(1)}, u32[]{:S(2)}, u32[]{:S(2)}) collective-permute-start(bf16[2,12,8,512]{3,2,1,0:T(8,128)(2,1)S(1)} %get-tuple-element.47), channel_id=1, source_target_pairs={{16,0},{32,16},{48,32},{64,48},{80,64},{96,80},{112,96},{17,1},{33... | collective-permute-start | bytes 589832 | tf_op jit(solution)/shard_map/ppermute | solution.py:487
  26.0 0.9 copy-start.8
  26.9 1.8 %copy-start.9 = (f32[2,3,2,1536]{3,2,1,0:T(2,128)S(1)}, f32[2,3,2,1536]{3,2,1,0:T(2,128)}, u32[]{:S(2)}) copy-start(f32[2,3,2,1536]{3,2,1,0:T(2,128)} %get-tuple-element.32.fac_ref) | copy-start | bytes 221188
  28.6 3.8 %copy-start = (bf16[2,24,16,512]{3,2,1,0:T(8,128)(2,1)S(1)}, bf16[2,24,16,512]{3,2,1,0:T(8,128)(2,1)}, u32[]{:S(2)}) copy-start(bf16[2,24,16,512]{3,2,1,0:T(8,128)(2,1)} %tok_ref.3) | copy-start | bytes 2359300
  41.9 2.7 %collective-permute-start.10 = (bf16[8,8,64,128]{3,2,1,0:T(8,128)(2,1)S(1)}, bf16[8,8,64,128]{3,2,1,0:T(8,128)(2,1)S(1)}, u32[]{:S(2)}, u32[]{:S(2)}) collective-permute-start(bf16[8,8,64,128]{3,2,1,0:T(8,128)(2,1)S(1)} %get-tuple-element.56), channel_id=1, source_target_pairs={{0,1},{1,0},{2,3},{3,2},{4,5},{5,4},{6,7},{7,6},{8,9},{9,8},{10,11... | collective-permute-start | bytes 3145736 | tf_op jit(solution)/shard_map/ppermute | solution.py:562
  45.8 36.0 %all-to-all-start = ((bf16[64,64,128]{2,1,0:T(8,128)(2,1)}), bf16[64,64,128]{2,1,0:T(8,128)(2,1)S(1)}, u32[]{:S(2)}, u32[]{:S(2)}) async-start(bf16[64,64,128]{2,1,0:T(8,128)(2,1)} %bitcast), calls=%async_computation | async-start | bytes 2097152 | tf_op jit(solution)/shard_map/all_to_all | solution.py:564
  59.9 1.9 %copy-start.1 = (bf16[2,32,24,1024]{3,2,1,0:T(8,128)(2,1)S(1)}, bf16[2,32,24,1024]{3,2,1,0:T(8,128)(2,1)}, u32[]{:S(2)}) copy-start(bf16[2,32,24,1024]{3,2,1,0:T(8,128)(2,1)} %get-tuple-element.48.kv_ref) | copy-start | bytes 9437188
  61.8 1.4 %copy-start.4 = (bf16[512,1536]{1,0:T(8,128)(2,1)S(1)}, bf16[512,1536]{1,0:T(8,128)(2,1)}, u32[]{:S(2)}) copy-start(bf16[512,1536]{1,0:T(8,128)(2,1)} %w_ref.3) | copy-start | bytes 4718596
  65.6 8.6 %collective-permute-start.6 = (bf16[2,16,8,512]{3,2,1,0:T(8,128)(2,1)S(1)}, bf16[2,16,8,512]{3,2,1,0:T(8,128)(2,1)S(1)}, u32[]{:S(2)}, u32[]{:S(2)}) collective-permute-start(bf16[2,16,8,512]{3,2,1,0:T(8,128)(2,1)S(1)} %get-tuple-element.51), channel_id=1, source_target_pairs={{0,1},{1,2},{2,3},{3,4},{4,5},{5,6},{6,7},{7,8},{8,9},{9,10},{10,1... | collective-permute-start | bytes 786440 | tf_op jit(solution)/shard_map/ppermute | solution.py:487
  69.3 8.0 %collective-permute-start.7 = (bf16[2,16,8,512]{3,2,1,0:T(8,128)(2,1)S(1)}, bf16[2,16,8,512]{3,2,1,0:T(8,128)(2,1)S(1)}, u32[]{:S(2)}, u32[]{:S(2)}) collective-permute-start(bf16[2,16,8,512]{3,2,1,0:T(8,128)(2,1)S(1)} %get-tuple-element.52), channel_id=1, source_target_pairs={{1,0},{2,1},{3,2},{4,3},{5,4},{6,5},{7,6},{8,7},{9,8},{10,9},{11,1... | collective-permute-start | bytes 786440 | tf_op jit(solution)/shard_map/ppermute | solution.py:487
  77.4 17.3 %collective-permute-start.8 = (bf16[2,4,16,512]{3,2,1,0:T(8,128)(2,1)S(1)}, bf16[2,4,16,512]{3,2,1,0:T(8,128)(2,1)S(1)}, u32[]{:S(2)}, u32[]{:S(2)}) collective-permute-start(bf16[2,4,16,512]{3,2,1,0:T(8,128)(2,1)S(1)} %get-tuple-element.53), channel_id=1, source_target_pairs={{0,16},{16,32},{32,48},{48,64},{64,80},{80,96},{96,112},{1,17},{17... | collective-permute-start | bytes 393224 | tf_op jit(solution)/shard_map/ppermute | solution.py:487
  80.5 14.2 %collective-permute-start.9 = (bf16[2,4,16,512]{3,2,1,0:T(8,128)(2,1)S(1)}, bf16[2,4,16,512]{3,2,1,0:T(8,128)(2,1)S(1)}, u32[]{:S(2)}, u32[]{:S(2)}) collective-permute-start(bf16[2,4,16,512]{3,2,1,0:T(8,128)(2,1)S(1)} %get-tuple-element.54), channel_id=1, source_target_pairs={{16,0},{32,16},{48,32},{64,48},{80,64},{96,80},{112,96},{17,1},{33... | collective-permute-start | bytes 393224 | tf_op jit(solution)/shard_map/ppermute | solution.py:487
  82.7 21.6 %all-to-all-start.1 = ((f32[128,1,128]{2,1,0:T(1,128)}), f32[128,1,128]{2,1,0:T(1,128)S(1)}, u32[]{:S(2)}, u32[]{:S(2)}) async-start(f32[128,1,128]{2,1,0:T(1,128)} %bitcast.2), calls=%async_computation.1 | async-start | bytes 131072 | tf_op jit(solution)/shard_map/all_to_all | solution.py:588

commit v5 on v4

--- a/solution.py
+++ b/solution.py
@@ -54,75 +54,106 @@
     return ref[b, rows, 8 * j : 8 * j + 8, :].astype(f32) * factor[None]
 
 
+def even_column():
+    return lax.axis_index("core") == 0
+
+
+def even_row():
+    return lax.rem(lax.axis_index("row"), 2) == 0
+
+
+def swap(even, x, y):
+    return jnp.where(even, x, y), jnp.where(even, y, x)
+
+
 def edge_kernel(
-    scale_ref, k_ref, v_ref, tok_ref, fac_ref, up_ref, down_ref, left_ref, right_ref, k_buf, v_buf, t_buf, sem
+    scale_ref, k_ref, v_ref, tok_ref, fac_ref, re_ref, ro_ref, ce_ref, co_ref, s_buf, k_buf, v_buf, t_buf, sem
 ):
     members, height, breadth, features = k_ref.shape
     tiles = breadth // 8
-    copies = [
-        pltpu.make_async_copy(src, dst, sem.at[n])
-        for n, (src, dst) in enumerate(((k_ref, k_buf), (v_ref, v_buf), (tok_ref, t_buf)))
-    ]
-    for c in copies:
-        c.start()
+    first = pltpu.make_async_copy(scale_ref, s_buf, sem.at[0])
+    first.start()
+    copies = []
+    for b in range(members):
+        copies.append([
+            pltpu.make_async_copy(src.at[b], dst.at[b], sem.at[1 + 3 * b + n])
+            for n, (src, dst) in enumerate(((k_ref, k_buf), (v_ref, v_buf), (tok_ref, t_buf)))
+        ])
+        for c in copies[b]:
+            c.start()
     count = scale_ref.shape[3]
     per = 3 * features // count
     hot = (
         lax.broadcasted_iota(jnp.int32, (count, 3 * features), 0)
         == lax.broadcasted_iota(jnp.int32, (count, 3 * features), 1) // per
     ).astype(f32).astype(bf16)
+    first.wait()
     for b in range(members):
         for i in range(height // 8):
-            factor = jnp.exp2(scale_ref[b, i].astype(f32)).astype(bf16)
+            factor = jnp.exp2(s_buf[b, i].astype(f32)).astype(bf16)
             fac_ref[b, i] = jnp.dot(factor, hot, preferred_element_type=f32)
-    for c in copies:
-        c.wait()
-    half = height // 2
-    for b in range(members):
-        for i in range(height // 8):
+    half, last = height // 2, height // 8 - 1
+    even_c, even_r = even_column(), even_row()
+    for b in range(members):
+        for c in copies[b]:
+            c.wait()
+        ends = {}
+        for i in range(last + 1):
             rows = slice(8 * i, 8 * i + 8)
             k = [block_of(k_buf, fac_ref, 1, b, i, j, rows, features) for j in range(tiles)]
             v = [block_of(v_buf, fac_ref, 2, b, i, j, rows, features) for j in range(tiles)]
             low = lower(k[0])
-            left_ref[b, rows] = jnp.where(low, k[0], turn(v[0])).astype(bf16)
-            right_ref[b, rows] = jnp.where(low, turn(v[-1]), k[-1]).astype(bf16)
+            left, right = jnp.where(low, k[0], turn(v[0])), jnp.where(low, turn(v[-1]), k[-1])
+            x, y = swap(even_c, right, left)
+            ce_ref[b, rows], co_ref[b, rows] = x.astype(bf16), y.astype(bf16)
             for m, parts in enumerate((k, v)):
-                x = jnp.concatenate(parts, 1).astype(bf16)
                 if i == 0:
-                    up_ref[m, b] = x[0:4]
-                if i == height // 8 - 1:
-                    down_ref[m, b] = x[4:8]
-        up_ref[2, b] = t_buf[b, 0:4]
-        down_ref[2, b] = t_buf[b, height - 4 : height]
+                    ends[m, 0] = jnp.concatenate(parts, 1)[0:4]
+                if i == last:
+                    ends[m, 1] = jnp.concatenate(parts, 1)[4:8]
+        ends[2, 0], ends[2, 1] = t_buf[b, 0:4].astype(f32), t_buf[b, height - 4 : height].astype(f32)
+        for m in range(3):
+            x, y = swap(even_r, ends[m, 1], ends[m, 0])
+            re_ref[m, b], ro_ref[m, b] = x.astype(bf16), y.astype(bf16)
         for r in range(0, half, 4):
             here, there = slice(r, r + 4), slice(half + r, half + r + 4)
             out = slice(height + r, height + r + 4)
-            pack_columns(t_buf.at[b, here], t_buf.at[b, there], left_ref.at[b, out], right_ref.at[b, out])
-
-
-def pack_columns(one_ref, two_ref, left_ref, right_ref):
-    last = one_ref.shape[1] - 8
-    x0, y0 = one_ref[:, 0:8].astype(f32), two_ref[:, 0:8].astype(f32)
-    x1, y1 = one_ref[:, last:].astype(f32), two_ref[:, last:].astype(f32)
+            left, right = pack_columns(t_buf[b, here], t_buf[b, there])
+            x, y = swap(even_c, right, left)
+            ce_ref[b, out], co_ref[b, out] = x.astype(bf16), y.astype(bf16)
+
+
+def pack_columns(one, two):
+    last = one.shape[1] - 8
+    x0, y0 = one[:, 0:8].astype(f32), two[:, 0:8].astype(f32)
+    x1, y1 = one[:, last:].astype(f32), two[:, last:].astype(f32)
     low = lower(x0)
-    left_ref[...] = jnp.where(low, x0, turn(y0)).astype(bf16)
-    right_ref[...] = jnp.where(low, turn(y1), x1).astype(bf16)
-
-
-def corner_kernel(fl_ref, fr_ref, up_ref, down_ref):
-    members, packed = fl_ref.shape[:2]
+    return jnp.where(low, x0, turn(y0)), jnp.where(low, turn(y1), x1)
+
+
+def corner_kernel(fe_ref, fo_ref, re_ref, ro_ref):
+    members, packed = fe_ref.shape[:2]
     height = packed * 2 // 3
     half = height // 2
-    for b in range(members):
-        for n, (out, row) in enumerate(((up_ref, 0), (down_ref, height - 4))):
-            k, v = rims_of(fl_ref, fr_ref, b, slice(row, row + 4))
+    even = even_row()
+    for b in range(members):
+        ends = []
+        for n, row in enumerate((0, height - 4)):
+            k, v = rims_of(fe_ref, fo_ref, b, slice(row, row + 4))
             first = height + (row if n == 0 else row - half)
-            t = rims_of(fl_ref, fr_ref, b, slice(first, first + 4))[n]
-            out[b] = jnp.concatenate([k, v, t], 0).astype(bf16)
-
-
-def rims_of(left_ref, right_ref, b, rows):
-    left, right = left_ref[b, rows].astype(f32), right_ref[b, rows].astype(f32)
+            t = rims_of(fe_ref, fo_ref, b, slice(first, first + 4))[n]
+            ends.append(jnp.concatenate([k, v, t], 0))
+        x, y = swap(even, ends[1], ends[0])
+        re_ref[b], ro_ref[b] = x.astype(bf16), y.astype(bf16)
+
+
+def columns_of(fe_ref, fo_ref, b, rows):
+    right, left = swap(even_column(), fe_ref[b, rows].astype(f32), fo_ref[b, rows].astype(f32))
+    return left, right
+
+
+def rims_of(fe_ref, fo_ref, b, rows):
+    left, right = columns_of(fe_ref, fo_ref, b, rows)
     low = lower(left)
     return jnp.where(low, right, left), turn(jnp.where(low, left, right))
 
@@ -269,7 +300,7 @@
 
 def main_kernel(
     qs_ref, do_ref, kt_ref, vt_ref, dkm_ref, dvm_ref, om_ref, dqm_ref, gm_ref, tok_ref,
-    fl_ref, fr_ref, top_ref, bottom_ref, ct_ref, cb_ref,
+    fl_ref, fr_ref, he_ref, ho_ref, ke_ref, ko_ref,
     keep_ref, send_ref, dq_out, kv_out,
     kh_ref, vh_ref, dkt_ref, dvt_ref, o_ref, tp_ref, all_ref, dq_ref, kv_ref, bias_ref, sem,
 ):
@@ -277,15 +308,18 @@
     tall = height + 8
     tiles = breadth // 8
     mask_biases(bias_ref, (0, height // 8 - 1), tiles, place_of(height, breadth))
-    for b in range(members):
-        for n, (ref, corner) in enumerate(((top_ref, ct_ref), (bottom_ref, cb_ref))):
-            rims = [corner[b, 4 * m : 4 * m + 4].astype(f32) for m in range(3)]
+    even = even_row()
+    for b in range(members):
+        corners = swap(even, ke_ref[b].astype(f32), ko_ref[b].astype(f32))[::-1]
+        strips = [swap(even, he_ref[m, b].astype(f32), ho_ref[m, b].astype(f32))[::-1] for m in range(3)]
+        for n, corner in enumerate(corners):
+            rims = [corner[4 * m : 4 * m + 4] for m in range(3)]
             for m, out in enumerate((kh_ref, vh_ref)):
-                blocks = [ref[m, b, :, 8 * j : 8 * j + 8].astype(f32) for j in range(tiles)]
+                blocks = [strips[m][n][:, 8 * j : 8 * j + 8] for j in range(tiles)]
                 for t in range(tiles):
                     out[n, b, t] = key_tile(blocks, rims[m], t)
             halo = slice(0, 4) if n == 0 else slice(tall - 4, tall)
-            tp_ref[b, halo] = jnp.concatenate([ref[2, b].astype(f32), rims[2]], 1).astype(bf16)
+            tp_ref[b, halo] = jnp.concatenate([strips[2][n], rims[2]], 1).astype(bf16)
             dq_ref[b, halo] = jnp.zeros((4, breadth, features), bf16)
         half = height // 2
         for r in range(0, half, 4):
@@ -401,7 +435,7 @@
         c.wait()
 
 
-def token_kernel(kv_ref, dq_ref, w_ref, gt_ref, left_ref, right_ref):
+def token_kernel(kv_ref, dq_ref, w_ref, gt_ref, ce_ref, co_ref):
     members, tall, breadth, features = dq_ref.shape
     across = (((1,), (1,)), ((), ()))
     middle = tall // 2
@@ -417,8 +451,8 @@
         gt_ref[b] = (y[:, 0:breadth] + z).astype(bf16)
         here, there = y[0:middle, breadth:], turn(y[middle:, breadth:])
         low = lower(here)
-        right_ref[b] = jnp.where(low, here, there).astype(bf16)
-        left_ref[b] = jnp.where(low, there, here).astype(bf16)
+        x, y = swap(even_column(), jnp.where(low, here, there), jnp.where(low, there, here))
+        ce_ref[b], co_ref[b] = x.astype(bf16), y.astype(bf16)
 
 
 def back_rims(fl, fr):
@@ -446,30 +480,33 @@
     square_ref[...] = jnp.broadcast_to(square, square_ref.shape)
 
 
-def halo_kernel(gt_ref, fl_ref, fr_ref, up_ref, down_ref):
+def halo_kernel(gt_ref, fe_ref, fo_ref, re_ref, ro_ref):
     members, tall = gt_ref.shape[:2]
     half = tall // 2
     for b in range(members):
-        here, _ = back_rims(fl_ref[b, 0:4].astype(f32), fr_ref[b, 0:4].astype(f32))
-        _, there = back_rims(fl_ref[b, half - 4 : half].astype(f32), fr_ref[b, half - 4 : half].astype(f32))
-        up_ref[b] = plus_rims(gt_ref[b, 0:4].astype(f32), here).astype(bf16)
-        down_ref[b] = plus_rims(gt_ref[b, tall - 4 : tall].astype(f32), there).astype(bf16)
-
-
-def join_kernel(gt_ref, fl_ref, fr_ref, ft_ref, fb_ref, tok_ref):
+        here, _ = back_rims(*columns_of(fe_ref, fo_ref, b, slice(0, 4)))
+        _, there = back_rims(*columns_of(fe_ref, fo_ref, b, slice(half - 4, half)))
+        up = plus_rims(gt_ref[b, 0:4].astype(f32), here)
+        down = plus_rims(gt_ref[b, tall - 4 : tall].astype(f32), there)
+        x, y = swap(even_row(), down, up)
+        re_ref[b], ro_ref[b] = x.astype(bf16), y.astype(bf16)
+
+
+def join_kernel(gt_ref, fe_ref, fo_ref, he_ref, ho_ref, tok_ref):
     members, height = tok_ref.shape[:2]
     half = (height + 8) // 2
     for b in range(members):
+        bottom, top = swap(even_row(), he_ref[b].astype(f32), ho_ref[b].astype(f32))
         for r in range(0, half, 4):
-            pair = back_rims(fl_ref[b, r : r + 4].astype(f32), fr_ref[b, r : r + 4].astype(f32))
+            pair = back_rims(*columns_of(fe_ref, fo_ref, b, slice(r, r + 4)))
             for rims, row in zip(pair, (r, half + r)):
                 if row == 0 or row == height + 4:
                     continue
                 y = plus_rims(gt_ref[b, row : row + 4].astype(f32), rims)
                 if row == 4:
-                    y = y + ft_ref[b].astype(f32)
+                    y = y + top
                 if row == height:
-                    y = y + fb_ref[b].astype(f32)
+                    y = y + bottom
                 tok_ref[b, row - 4 : row] = y.astype(bf16)
 
 
@@ -482,9 +519,13 @@
     out_ref[...] = x.T[main:]
 
 
-def shift(x, axes, by):
+def exchange(even, odd, axes):
     size = lax.axis_size(axes)
-    return lax.ppermute(x, axes, [(i, i + by) for i in range(size) if 0 <= i + by < size])
+    out = []
+    for x, first in ((even, 0), (odd, 1)):
+        pairs = [(i, i + 1) for i in range(first, size - 1, 2)]
+        out.append(lax.ppermute(x, axes, pairs + [(j, i) for i, j in pairs]))
+    return out
 
 
 def body(tokens, w_qkv, w_out, q_saved, k_saved, v_saved, scale_exp, grad_out, crop_start):
@@ -493,18 +534,20 @@
     packed = height + height // 2
     packed_columns = shape(members, packed, 8, features)
     strip = shape(3, members, 4, breadth, features)
-    factor, up, down, left, right = call(
+    factor, *sides = call(
         edge_kernel,
         (
             shape(*scale_exp.shape[:3], 3 * features, dtype=f32),
             strip, strip, packed_columns, packed_columns,
         ),
         (scale_exp, k_saved, v_saved, tokens),
-        scratch=(pltpu.VMEM(tokens.shape, bf16),) * 3 + (pltpu.SemaphoreType.DMA((3,)),),
-        far=(1, 2, 3),
+        scratch=(pltpu.VMEM(scale_exp.shape, jnp.int32),)
+        + (pltpu.VMEM(tokens.shape, bf16),) * 3
+        + (pltpu.SemaphoreType.DMA((1 + 3 * members,)),),
+        far=(0, 1, 2, 3),
         limit=58 << 20,
     )
-    top, bottom = shift(down, "row", 1), shift(up, "row", -1)
+    halo_rows = exchange(*sides[0:2], "row")
     cells = members * height * breadth
     qs, gm, do = call(
         prepare_kernel,
@@ -513,10 +556,9 @@
         smem=(0,),
         flops=2 * cells * features * features,
     )
-    from_left, from_right = shift(right, COLS, 1), shift(left, COLS, -1)
+    halo_columns = exchange(*sides[2:4], COLS)
     corner = shape(members, 12, 8, features)
-    up, down = call(corner_kernel, (corner, corner), (from_left, from_right))
-    corner_top, corner_bottom = shift(down, "row", 1), shift(up, "row", -1)
+    corners = exchange(*call(corner_kernel, (corner, corner), halo_columns), "row")
     tiles = breadth // 8
     own_tiles = shape(members, tiles, height, 16, features)
     middle_tiles = shape(members, tiles, 16, 16, features, dtype=f32)
@@ -524,7 +566,7 @@
     kt, vt, dk, dv, out, dq = call(
         middle_kernel,
         (own_tiles, own_tiles, middle_tiles, middle_tiles, middle_rows, middle_rows),
-        (qs, do, k_saved, v_saved, factor, from_left, from_right),
+        (qs, do, k_saved, v_saved, factor, *halo_columns),
         scratch=(pltpu.VMEM((tiles, 256, features // 2), f32),),
         flops=4 * cells * features * features,
         limit=20 << 20,
@@ -543,7 +585,7 @@
         ),
         (
             qs, do, kt, vt, dk, dv, out, dq, gm, tokens,
-            from_left, from_right, top, bottom, corner_top, corner_bottom,
+            *halo_columns, *halo_rows, *corners,
         ),
         scratch=(
             halo_tiles, halo_tiles, all_tiles, all_tiles,
@@ -562,7 +604,7 @@
     other = lax.ppermute(send, "core", [(0, 1), (1, 0)])
     both = call(add_kernel, shape(rows, pairs, deep, wide), (keep, other)).reshape(rows * pairs, deep, wide)
     parts = lax.all_to_all(both, ("row", "pair"), 0, 0, tiled=True)
-    gt, left, right = call(
+    gt, *sides = call(
         token_kernel,
         (
             shape(members, tall, breadth, features),
@@ -573,12 +615,11 @@
         flops=6 * cells * features * features,
         limit=20 << 20,
     )
-    back_left, back_right = shift(right, COLS, 1), shift(left, COLS, -1)
+    back_columns = exchange(*sides, COLS)
     halo = shape(members, 4, breadth, features)
-    up, down = call(halo_kernel, (halo, halo), (gt, back_left, back_right))
-    back_top, back_bottom = shift(down, "row", 1), shift(up, "row", -1)
+    back_rows = exchange(*call(halo_kernel, (halo, halo), (gt, *back_columns)), "row")
     grad_tokens = call(
-        join_kernel, shape(*tokens.shape), (gt, back_left, back_right, back_top, back_bottom)
+        join_kernel, shape(*tokens.shape), (gt, *back_columns, *back_rows)
     )
     total, square = call(
         total_kernel,

time: 106 us -> 96.9 us (0.914)
  starting transfers between devices: 52.5 us -> 42.4 us
  waiting for transfers between devices: 22 us -> 23.7 us
    ppermute x10, starting transfers between devices: 26.3 us -> 15.2 us  [exchange(): out.append(lax.ppermute(x, axes, pairs + [(j, i) for i, j in pairs]))]
    all_to_all x1, starting transfers between devices: 14.1 us -> 15.8 us  [body(): parts = lax.all_to_all(both, ('row', 'pair'), 0, 0, tiled=True)]
    ppermute x10, waiting for transfers between devices: 11 us -> 12.7 us  [exchange(): out.append(lax.ppermute(x, axes, pairs + [(j, i) for i, j in pairs]))]
  transfers between devices with their start and end apart: 13 -> 13, of which waited for: 6 -> 4; matrix products, arithmetic and copies ran while one was open for 0% -> 0% of each run, Pallas kernels for 9% -> 11%
where the time goes in v5:
time: 96.9 us; the launch traced here: 96.5 us
  starting transfers between devices  42.4 us (44%)
  Pallas kernels  25.2 us (26%)
  waiting for transfers between devices  23.7 us (24%)
  local copies, waits for them, and re-layouts  4.21 us (4%)
    pallas_call x11, Pallas kernels, call(): pl.pallas_call(kernel, out_shape=outs, in_specs=[SMEM if n in smem else A...  25.2 us
    all_to_all x1, starting transfers between devices, body(): parts = lax.all_to_all(both, ('row', 'pair'), 0, 0, tiled=True)  15.8 us
    ppermute x10, starting transfers between devices, exchange(): out.append(lax.ppermute(x, axes, pairs + [(j, i) for i, j in pairs]))  15.2 us
    ppermute x10, waiting for transfers between devices, exchange(): out.append(lax.ppermute(x, axes, pairs + [(j, i) for i, j in pairs]))  12.7 us
    all_to_all x1, starting transfers between devices, body(): squares = lax.all_to_all(square, ('row', 'pair', 'core'), 0, 0, tiled=True)  11.3 us
    all_to_all x1, waiting for transfers between devices, body(): squares = lax.all_to_all(square, ('row', 'pair', 'core'), 0, 0, tiled=True)  8.33 us
    unnamed x22, local copies, waits for them, and re-layouts  4.21 us
    ppermute x1, waiting for transfers between devices, body(): other = lax.ppermute(send, 'core', [(0, 1), (1, 0)])  2.65 us
  transfers between devices with their start and end apart: 13, of which 4 were waited for; matrix products, arithmetic and copies ran while one was open for 0% of the time, Pallas kernels for 11%

profile of v5, /device:TPU:1, one launch (start us, length us, event | category | flops | bytes accessed | tf_op | source)
XLA Modules:
  0.0 96.5 jit_solution(232396966202614320)
XLA Ops:
  0.7 3.3 %shard_map.112 = (f32[2,3,2,1536]{3,2,1,0:T(2,128)}, bf16[3,2,4,16,512]{4,3,2,1,0:T(8,128)(2,1)}, bf16[3,2,4,16,512]{4,3,2,1,0:T(8,128)(2,1)}, bf16[2,36,8,512]{3,2,1,0:T(8,128)(2,1)}, bf16[2,36,8,512]{3,2,1,0:T(8,128)(2,1)}) custom-call(s32[2,3,2,24]{3,2,1,0:T(2,128)} %scale_ref.1, bf16[2,24,16,512]{3,2,1,0:T(8,128)(2,1)} %k_ref.3, ...), custom_call_target="tpu_custom_call" | custom-call | bytes 4400256 | tf_op jit(solution)/shard_map/pallas_call | solution.py:27
  4.0 0.0 copy-start.2
  4.0 1.5 %collective-permute-start = (bf16[2,36,8,512]{3,2,1,0:T(8,128)(2,1)}, bf16[2,36,8,512]{3,2,1,0:T(8,128)(2,1)S(1)}, u32[]{:S(2)}, u32[]{:S(2)}) collective-permute-start(bf16[2,36,8,512]{3,2,1,0:T(8,128)(2,1)} %get-tuple-element.35), channel_id=1, source_target_pairs={{0,1},{2,3},{4,5},{6,7},{8,9},{10,11},{12,13},{14,15},{1,0},{3,2},... | collective-permute-start | bytes 1769480 | tf_op jit(solution)/shard_map/ppermute | solution.py:527
  5.5 3.2 %collective-permute-start.1 = (bf16[2,36,8,512]{3,2,1,0:T(8,128)(2,1)}, bf16[2,36,8,512]{3,2,1,0:T(8,128)(2,1)S(1)}, u32[]{:S(2)}, u32[]{:S(2)}) collective-permute-start(bf16[2,36,8,512]{3,2,1,0:T(8,128)(2,1)} %get-tuple-element.36), channel_id=1, source_target_pairs={{1,2},{3,4},{5,6},{7,8},{9,10},{11,12},{13,14},{2,1},{4,3},{6,5},{... | collective-permute-start | bytes 1769480 | tf_op jit(solution)/shard_map/ppermute | solution.py:527
  8.8 1.7 %collective-permute-start.2 = (bf16[3,2,4,16,512]{4,3,2,1,0:T(8,128)(2,1)}, bf16[3,2,4,16,512]{4,3,2,1,0:T(8,128)(2,1)S(1)}, u32[]{:S(2)}, u32[]{:S(2)}) collective-permute-start(bf16[3,2,4,16,512]{4,3,2,1,0:T(8,128)(2,1)} %get-tuple-element.44), channel_id=1, source_target_pairs={{0,16},{32,48},{64,80},{96,112},{16,0},{48,32},{80,64},{112,96},{1... | collective-permute-start | bytes 1179656 | tf_op jit(solution)/shard_map/ppermute | solution.py:527
  10.5 0.7 collective-permute-start.3
  11.2 6.0 %collective-permute-done.1.fr_ref.fo_ref = bf16[2,36,8,512]{3,2,1,0:T(8,128)(2,1)S(1)} collective-permute-done((bf16[2,36,8,512]{3,2,1,0:T(8,128)(2,1)}, bf16[2,36,8,512]{3,2,1,0:T(8,128)(2,1)S(1)}, u32[]{:S(2)}, u32[]{:S(2)}) %collective-permute-start.1) | collective-permute-done | bytes 589856 | tf_op jit(solution)/shard_map/ppermute | solution.py:527
  17.2 0.2 shard_map.115
  17.4 1.8 %collective-permute-start.4 = (bf16[2,12,8,512]{3,2,1,0:T(8,128)(2,1)S(1)}, bf16[2,12,8,512]{3,2,1,0:T(8,128)(2,1)S(1)}, u32[]{:S(2)}, u32[]{:S(2)}) collective-permute-start(bf16[2,12,8,512]{3,2,1,0:T(8,128)(2,1)S(1)} %get-tuple-element.46), channel_id=1, source_target_pairs={{0,16},{32,48},{64,80},{96,112},{16,0},{48,32},{80,64},{112,96},{1... | collective-permute-start | bytes 589832 | tf_op jit(solution)/shard_map/ppermute | solution.py:527
  19.2 0.7 collective-permute-start.5
  19.9 0.9 copy-done.8
  20.8 1.7 %shard_map.113 = (bf16[2,24,16,512]{3,2,1,0:T(8,128)(2,1)S(1)}, bf16[2,24,16,512]{3,2,1,0:T(8,128)(2,1)S(1)}, bf16[2,24,16,512]{3,2,1,0:T(8,128)(2,1)S(1)}) custom-call(s32[2,2]{1,0:T(2,128)S(1)} %copy-done.10, bf16[2,24,16,512]{3,2,1,0:T(8,128)(2,1)S(1)} %copy-done.5, bf16[2,24,16,512]{3,2,1,0:T(8,128)(2,1)S(1)} %copy-done.6, ...), custom_call_target="tpu_custom_call" | custom-call | flops 402653184 | bytes 4530192 | tf_op jit(solution)/shard_map/pallas_call | solution.py:27
  22.6 3.8 %shard_map.114 = (bf16[2,2,24,16,512]{4,3,2,1,0:T(8,128)(2,1)S(1)}, bf16[2,2,24,16,512]{4,3,2,1,0:T(8,128)(2,1)S(1)}, f32[2,2,16,16,512]{4,3,2,1,0:T(8,128)S(1)}...) custom-call(bf16[2,24,16,512]{3,2,1,0:T(8,128)(2,1)S(1)} %get-tuple-el, ...), custom_call_target="tpu_custom_call" | custom-call | flops 805306368 | bytes 12263424 | tf_op jit(solution)/shard_map/pallas_call | solution.py:27
  26.4 9.7 %shard_map.116 = (bf16[8,8,64,128]{3,2,1,0:T(8,128)(2,1)S(1)}, bf16[8,8,64,128]{3,2,1,0:T(8,128)(2,1)S(1)}, bf16[2,32,16,512]{3,2,1,0:T(8,128)(2,1)S(1)}, bf16[2,32,24,1024]{3,2,1,0:T(8,128)(2,1)}) custom-call(bf16[2,24,16,512]{3,2,1,0:T(8,128)(2,1)S(1)} %get-tuple-element.33.qs_ref, bf16[2,24,16,512]{3,2,1,0:T(8,128)(2,1)S(1)} %get-tuple-element.34.do_ref, ...), custom_call_target="tpu_custom_call" | custom-call | flops 2415919104 | bytes 19660800 | tf_op jit(solution)/shard_map/pallas_call | solution.py:27
  36.1 0.1 collective-permute-start.10
  36.2 2.6 %collective-permute-done.10.y_ref = bf16[8,8,64,128]{3,2,1,0:T(8,128)(2,1)S(1)} collective-permute-done((bf16[8,8,64,128]{3,2,1,0:T(8,128)(2,1)S(1)}, bf16[8,8,64,128]{3,2,1,0:T(8,128)(2,1)S(1)}, u32[]{:S(2)}, u32[]{:S(2)}) %collective-permute-start.10) | collective-permute-done | bytes 1048608 | tf_op jit(solution)/shard_map/ppermute | solution.py:604
  38.8 1.2 %shard_map.120 = bf16[8,8,64,128]{3,2,1,0:T(8,128)(2,1)} custom-call(bf16[8,8,64,128]{3,2,1,0:T(8,128)(2,1)S(1)} %get-tuple-element.55.x_ref, bf16[8,8,64,128]{3,2,1,0:T(8,128)(2,1)S(1)} %collective-permute-done.10.y_ref), custom_call_target="tpu_custom_call" | custom-call | bytes 3145728 | tf_op jit(solution)/shard_map/pallas_call | solution.py:27
  40.0 15.8 %all-to-all-start = ((bf16[64,64,128]{2,1,0:T(8,128)(2,1)}), bf16[64,64,128]{2,1,0:T(8,128)(2,1)S(1)}, u32[]{:S(2)}, u32[]{:S(2)}) async-start(bf16[64,64,128]{2,1,0:T(8,128)(2,1)} %bitcast), calls=%async_computation | async-start | bytes 2097152 | tf_op jit(solution)/shard_map/all_to_all | solution.py:606
  55.9 1.9 %copy-done.1 = bf16[2,32,24,1024]{3,2,1,0:T(8,128)(2,1)S(1)} copy-done((bf16[2,32,24,1024]{3,2,1,0:T(8,128)(2,1)S(1)}, bf16[2,32,24,1024]{3,2,1,0:T(8,128)(2,1)}, u32[]{:S(2)}) %copy-start.1) | copy-done | bytes 3145752
  57.8 1.4 %copy-done.4 = bf16[512,1536]{1,0:T(8,128)(2,1)S(1)} copy-done((bf16[512,1536]{1,0:T(8,128)(2,1)S(1)}, bf16[512,1536]{1,0:T(8,128)(2,1)}, u32[]{:S(2)}) %copy-start.4) | copy-done | bytes 1572888
  59.2 2.4 %shard_map.117 = (bf16[2,32,16,512]{3,2,1,0:T(8,128)(2,1)S(1)}, bf16[2,16,8,512]{3,2,1,0:T(8,128)(2,1)S(1)}, bf16[2,16,8,512]{3,2,1,0:T(8,128)(2,1)S(1)}) custom-call(bf16[2,32,24,1024]{3,2,1,0:T(8,128)(2,1)S(1)} %copy-done.1, bf16[2,32,16,512]{3,2,1,0:T(8,128)(2,1)S(1)} %get-tuple-element.49.dq_ref, bf16[512,1536]{1,0:T(8,128)(2,1)S(1)} %copy-done.4), custom_call_target="tpu_custom_call" | custom-call | flops 1207959552 | bytes 7340032 | tf_op jit(solution)/shard_map/pallas_call | solution.py:27
  61.5 0.7 collective-permute-start.6
  62.3 2.9 %collective-permute-start.7 = (bf16[2,16,8,512]{3,2,1,0:T(8,128)(2,1)S(1)}, bf16[2,16,8,512]{3,2,1,0:T(8,128)(2,1)S(1)}, u32[]{:S(2)}, u32[]{:S(2)}) collective-permute-start(bf16[2,16,8,512]{3,2,1,0:T(8,128)(2,1)S(1)} %get-tuple-element.52), channel_id=1, source_target_pairs={{1,2},{3,4},{5,6},{7,8},{9,10},{11,12},{13,14},{2,1},{4,3},{6,5},{... | collective-permute-start | bytes 786440 | tf_op jit(solution)/shard_map/ppermute | solution.py:527
  65.2 6.6 %collective-permute-done.7.fo_ref = bf16[2,16,8,512]{3,2,1,0:T(8,128)(2,1)S(1)} collective-permute-done((bf16[2,16,8,512]{3,2,1,0:T(8,128)(2,1)S(1)}, bf16[2,16,8,512]{3,2,1,0:T(8,128)(2,1)S(1)}, u32[]{:S(2)}, u32[]{:S(2)}) %collective-permute-start.7) | collective-permute-done | bytes 262176 | tf_op jit(solution)/shard_map/ppermute | solution.py:527
  71.8 0.1 shard_map.118
  72.0 1.3 %collective-permute-start.8 = (bf16[2,4,16,512]{3,2,1,0:T(8,128)(2,1)S(1)}, bf16[2,4,16,512]{3,2,1,0:T(8,128)(2,1)S(1)}, u32[]{:S(2)}, u32[]{:S(2)}) collective-permute-start(bf16[2,4,16,512]{3,2,1,0:T(8,128)(2,1)S(1)} %get-tuple-element.53), channel_id=1, source_target_pairs={{0,16},{32,48},{64,80},{96,112},{16,0},{48,32},{80,64},{112,96},{1... | collective-permute-start | bytes 393224 | tf_op jit(solution)/shard_map/ppermute | solution.py:527
  73.2 0.7 collective-permute-start.9
  73.9 0.8 shard_map.121
  74.8 11.3 %all-to-all-start.1 = ((f32[128,1,128]{2,1,0:T(1,128)}), f32[128,1,128]{2,1,0:T(1,128)S(1)}, u32[]{:S(2)}, u32[]{:S(2)}) async-start(f32[128,1,128]{2,1,0:T(1,128)} %bitcast.2), calls=%async_computation.1 | async-start | bytes 131072 | tf_op jit(solution)/shard_map/all_to_all | solution.py:629
  86.1 1.2 %shard_map.119 = bf16[2,24,16,512]{3,2,1,0:T(8,128)(2,1)} custom-call(bf16[2,32,16,512]{3,2,1,0:T(8,128)(2,1)S(1)} %get-tuple-element.50.gt_ref, bf16[2,16,8,512]{3,2,1,0:T(8,128)(2,1)S(1)} %collective-permute-done.6.fe_ref, bf16[2,16,8,512]{3,2,1,0:T(8,128)(2,1)S(1)} %collective-permute-done.7.fo_ref, ...), custom_call_target="tpu_custom_call" | custom-call | bytes 2621440 | tf_op jit(solution)/shard_map/pallas_call | solution.py:27
  87.3 8.3 %all-to-all-done.1 = f32[128,1,128]{2,1,0:T(1,128)S(1)} async-done(((f32[128,1,128]{2,1,0:T(1,128)}), f32[128,1,128]{2,1,0:T(1,128)S(1)}, u32[]{:S(2)}, u32[]{:S(2)}) %all-to-all-start.1) | async-done | bytes 65568 | tf_op jit(solution)/shard_map/all_to_all | solution.py:629
  95.6 0.8 shard_map.122
  (27 shorter events, 0.1 us)
Async XLA Ops:
  0.6 19.2 %copy-start.10 = (s32[2,2]{1,0:T(2,128)S(1)}, s32[2,2]{1,0:T(2,128)}, u32[]{:S(2)}) copy-start(s32[2,2]{1,0:T(2,128)} %crop_ref.1) | copy-start | bytes 52
  0.6 19.2 %copy-start.6 = (bf16[2,24,16,512]{3,2,1,0:T(8,128)(2,1)S(1)}, bf16[2,24,16,512]{3,2,1,0:T(8,128)(2,1)}, u32[]{:S(2)}) copy-start(bf16[2,24,16,512]{3,2,1,0:T(8,128)(2,1)} %g_ref.1) | copy-start | bytes 2359300
  0.7 19.2 %copy-start.5 = (bf16[2,24,16,512]{3,2,1,0:T(8,128)(2,1)S(1)}, bf16[2,24,16,512]{3,2,1,0:T(8,128)(2,1)}, u32[]{:S(2)}) copy-start(bf16[2,24,16,512]{3,2,1,0:T(8,128)(2,1)} %q_ref.1) | copy-start | bytes 2359300
  0.7 19.2 %copy-start.7 = (bf16[512,512]{1,0:T(8,128)(2,1)S(1)}, bf16[512,512]{1,0:T(8,128)(2,1)}, u32[]{:S(2)}) copy-start(bf16[512,512]{1,0:T(8,128)(2,1)} %w_ref.2) | copy-start | bytes 1572868
  4.0 18.5 %copy-start.2 = (bf16[2,24,16,512]{3,2,1,0:T(8,128)(2,1)S(1)}, bf16[2,24,16,512]{3,2,1,0:T(8,128)(2,1)}, u32[]{:S(2)}) copy-start(bf16[2,24,16,512]{3,2,1,0:T(8,128)(2,1)} %k_ref.3) | copy-start | bytes 2359300
  4.0 18.5 %copy-start.3 = (bf16[2,24,16,512]{3,2,1,0:T(8,128)(2,1)S(1)}, bf16[2,24,16,512]{3,2,1,0:T(8,128)(2,1)}, u32[]{:S(2)}) copy-start(bf16[2,24,16,512]{3,2,1,0:T(8,128)(2,1)} %v_ref.3) | copy-start | bytes 2359300
  4.0 7.1 %collective-permute-start = (bf16[2,36,8,512]{3,2,1,0:T(8,128)(2,1)}, bf16[2,36,8,512]{3,2,1,0:T(8,128)(2,1)S(1)}, u32[]{:S(2)}, u32[]{:S(2)}) collective-permute-start(bf16[2,36,8,512]{3,2,1,0:T(8,128)(2,1)} %get-tuple-element.35), channel_id=1, source_target_pairs={{0,1},{2,3},{4,5},{6,7},{8,9},{10,11},{12,13},{14,15},{1,0},{3,2},... | collective-permute-start | bytes 1769480 | tf_op jit(solution)/shard_map/ppermute | solution.py:527
  5.5 11.7 %collective-permute-start.1 = (bf16[2,36,8,512]{3,2,1,0:T(8,128)(2,1)}, bf16[2,36,8,512]{3,2,1,0:T(8,128)(2,1)S(1)}, u32[]{:S(2)}, u32[]{:S(2)}) collective-permute-start(bf16[2,36,8,512]{3,2,1,0:T(8,128)(2,1)} %get-tuple-element.36), channel_id=1, source_target_pairs={{1,2},{3,4},{5,6},{7,8},{9,10},{11,12},{13,14},{2,1},{4,3},{6,5},{... | collective-permute-start | bytes 1769480 | tf_op jit(solution)/shard_map/ppermute | solution.py:527
  8.8 17.6 %collective-permute-start.2 = (bf16[3,2,4,16,512]{4,3,2,1,0:T(8,128)(2,1)}, bf16[3,2,4,16,512]{4,3,2,1,0:T(8,128)(2,1)S(1)}, u32[]{:S(2)}, u32[]{:S(2)}) collective-permute-start(bf16[3,2,4,16,512]{4,3,2,1,0:T(8,128)(2,1)} %get-tuple-element.44), channel_id=1, source_target_pairs={{0,16},{32,48},{64,80},{96,112},{16,0},{48,32},{80,64},{112,96},{1... | collective-permute-start | bytes 1179656 | tf_op jit(solution)/shard_map/ppermute | solution.py:527
  10.5 15.9 %collective-permute-start.3 = (bf16[3,2,4,16,512]{4,3,2,1,0:T(8,128)(2,1)}, bf16[3,2,4,16,512]{4,3,2,1,0:T(8,128)(2,1)S(1)}, u32[]{:S(2)}, u32[]{:S(2)}) collective-permute-start(bf16[3,2,4,16,512]{4,3,2,1,0:T(8,128)(2,1)} %get-tuple-element.45), channel_id=1, source_target_pairs={{16,32},{48,64},{80,96},{32,16},{64,48},{96,80},{17,33},{49,65},{8... | collective-permute-start | bytes 1179656 | tf_op jit(solution)/shard_map/ppermute | solution.py:527
  17.4 9.0 %collective-permute-start.4 = (bf16[2,12,8,512]{3,2,1,0:T(8,128)(2,1)S(1)}, bf16[2,12,8,512]{3,2,1,0:T(8,128)(2,1)S(1)}, u32[]{:S(2)}, u32[]{:S(2)}) collective-permute-start(bf16[2,12,8,512]{3,2,1,0:T(8,128)(2,1)S(1)} %get-tuple-element.46), channel_id=1, source_target_pairs={{0,16},{32,48},{64,80},{96,112},{16,0},{48,32},{80,64},{112,96},{1... | collective-permute-start | bytes 589832 | tf_op jit(solution)/shard_map/ppermute | solution.py:527
  19.2 7.2 %collective-permute-start.5 = (bf16[2,12,8,512]{3,2,1,0:T(8,128)(2,1)S(1)}, bf16[2,12,8,512]{3,2,1,0:T(8,128)(2,1)S(1)}, u32[]{:S(2)}, u32[]{:S(2)}) collective-permute-start(bf16[2,12,8,512]{3,2,1,0:T(8,128)(2,1)S(1)} %get-tuple-element.47), channel_id=1, source_target_pairs={{16,32},{48,64},{80,96},{32,16},{64,48},{96,80},{17,33},{49,65},{8... | collective-permute-start | bytes 589832 | tf_op jit(solution)/shard_map/ppermute | solution.py:527
  19.9 0.9 copy-start.8
  20.8 1.8 %copy-start.9 = (f32[2,3,2,1536]{3,2,1,0:T(2,128)S(1)}, f32[2,3,2,1536]{3,2,1,0:T(2,128)}, u32[]{:S(2)}) copy-start(f32[2,3,2,1536]{3,2,1,0:T(2,128)} %get-tuple-element.32.fac_ref) | copy-start | bytes 221188
  22.6 3.8 %copy-start = (bf16[2,24,16,512]{3,2,1,0:T(8,128)(2,1)S(1)}, bf16[2,24,16,512]{3,2,1,0:T(8,128)(2,1)}, u32[]{:S(2)}) copy-start(bf16[2,24,16,512]{3,2,1,0:T(8,128)(2,1)} %tok_ref.3) | copy-start | bytes 2359300
  36.1 2.7 %collective-permute-start.10 = (bf16[8,8,64,128]{3,2,1,0:T(8,128)(2,1)S(1)}, bf16[8,8,64,128]{3,2,1,0:T(8,128)(2,1)S(1)}, u32[]{:S(2)}, u32[]{:S(2)}) collective-permute-start(bf16[8,8,64,128]{3,2,1,0:T(8,128)(2,1)S(1)} %get-tuple-element.56), channel_id=1, source_target_pairs={{0,1},{1,0},{2,3},{3,2},{4,5},{5,4},{6,7},{7,6},{8,9},{9,8},{10,11... | collective-permute-start | bytes 3145736 | tf_op jit(solution)/shard_map/ppermute | solution.py:604
  40.0 33.9 %all-to-all-start = ((bf16[64,64,128]{2,1,0:T(8,128)(2,1)}), bf16[64,64,128]{2,1,0:T(8,128)(2,1)S(1)}, u32[]{:S(2)}, u32[]{:S(2)}) async-start(bf16[64,64,128]{2,1,0:T(8,128)(2,1)} %bitcast), calls=%async_computation | async-start | bytes 2097152 | tf_op jit(solution)/shard_map/all_to_all | solution.py:606
  55.9 1.9 %copy-start.1 = (bf16[2,32,24,1024]{3,2,1,0:T(8,128)(2,1)S(1)}, bf16[2,32,24,1024]{3,2,1,0:T(8,128)(2,1)}, u32[]{:S(2)}) copy-start(bf16[2,32,24,1024]{3,2,1,0:T(8,128)(2,1)} %get-tuple-element.48.kv_ref) | copy-start | bytes 9437188
  57.8 1.4 %copy-start.4 = (bf16[512,1536]{1,0:T(8,128)(2,1)S(1)}, bf16[512,1536]{1,0:T(8,128)(2,1)}, u32[]{:S(2)}) copy-start(bf16[512,1536]{1,0:T(8,128)(2,1)} %w_ref.3) | copy-start | bytes 4718596
  61.5 3.7 %collective-permute-start.6 = (bf16[2,16,8,512]{3,2,1,0:T(8,128)(2,1)S(1)}, bf16[2,16,8,512]{3,2,1,0:T(8,128)(2,1)S(1)}, u32[]{:S(2)}, u32[]{:S(2)}) collective-permute-start(bf16[2,16,8,512]{3,2,1,0:T(8,128)(2,1)S(1)} %get-tuple-element.51), channel_id=1, source_target_pairs={{0,1},{2,3},{4,5},{6,7},{8,9},{10,11},{12,13},{14,15},{1,0},{3,2},... | collective-permute-start | bytes 786440 | tf_op jit(solution)/shard_map/ppermute | solution.py:527
  62.3 9.6 %collective-permute-start.7 = (bf16[2,16,8,512]{3,2,1,0:T(8,128)(2,1)S(1)}, bf16[2,16,8,512]{3,2,1,0:T(8,128)(2,1)S(1)}, u32[]{:S(2)}, u32[]{:S(2)}) collective-permute-start(bf16[2,16,8,512]{3,2,1,0:T(8,128)(2,1)S(1)} %get-tuple-element.52), channel_id=1, source_target_pairs={{1,2},{3,4},{5,6},{7,8},{9,10},{11,12},{13,14},{2,1},{4,3},{6,5},{... | collective-permute-start | bytes 786440 | tf_op jit(solution)/shard_map/ppermute | solution.py:527
  72.0 14.1 %collective-permute-start.8 = (bf16[2,4,16,512]{3,2,1,0:T(8,128)(2,1)S(1)}, bf16[2,4,16,512]{3,2,1,0:T(8,128)(2,1)S(1)}, u32[]{:S(2)}, u32[]{:S(2)}) collective-permute-start(bf16[2,4,16,512]{3,2,1,0:T(8,128)(2,1)S(1)} %get-tuple-element.53), channel_id=1, source_target_pairs={{0,16},{32,48},{64,80},{96,112},{16,0},{48,32},{80,64},{112,96},{1... | collective-permute-start | bytes 393224 | tf_op jit(solution)/shard_map/ppermute | solution.py:527
  73.2 12.8 %collective-permute-start.9 = (bf16[2,4,16,512]{3,2,1,0:T(8,128)(2,1)S(1)}, bf16[2,4,16,512]{3,2,1,0:T(8,128)(2,1)S(1)}, u32[]{:S(2)}, u32[]{:S(2)}) collective-permute-start(bf16[2,4,16,512]{3,2,1,0:T(8,128)(2,1)S(1)} %get-tuple-element.54), channel_id=1, source_target_pairs={{16,32},{48,64},{80,96},{32,16},{64,48},{96,80},{17,33},{49,65},{8... | collective-permute-start | bytes 393224 | tf_op jit(solution)/shard_map/ppermute | solution.py:527
  74.8 20.9 %all-to-all-start.1 = ((f32[128,1,128]{2,1,0:T(1,128)}), f32[128,1,128]{2,1,0:T(1,128)S(1)}, u32[]{:S(2)}, u32[]{:S(2)}) async-start(f32[128,1,128]{2,1,0:T(1,128)} %bitcast.2), calls=%async_computation.1 | async-start | bytes 131072 | tf_op jit(solution)/shard_map/all_to_all | solution.py:629

commit v6 on v5

--- a/solution.py
+++ b/solution.py
@@ -66,21 +66,18 @@
     return jnp.where(even, x, y), jnp.where(even, y, x)
 
 
-def edge_kernel(
-    scale_ref, k_ref, v_ref, tok_ref, fac_ref, re_ref, ro_ref, ce_ref, co_ref, s_buf, k_buf, v_buf, t_buf, sem
-):
+def row_kernel(scale_ref, k_ref, v_ref, tok_ref, fac_ref, re_ref, ro_ref, s_buf, buf, sem):
     members, height, breadth, features = k_ref.shape
     tiles = breadth // 8
     first = pltpu.make_async_copy(scale_ref, s_buf, sem.at[0])
     first.start()
-    copies = []
-    for b in range(members):
-        copies.append([
-            pltpu.make_async_copy(src.at[b], dst.at[b], sem.at[1 + 3 * b + n])
-            for n, (src, dst) in enumerate(((k_ref, k_buf), (v_ref, v_buf), (tok_ref, t_buf)))
-        ])
-        for c in copies[b]:
-            c.start()
+    copies = [
+        pltpu.make_async_copy(src.at[:, rows], buf.at[m, n], sem.at[1 + 2 * m + n])
+        for m, src in enumerate((k_ref, v_ref, tok_ref))
+        for n, rows in enumerate((slice(0, 4), slice(height - 4, height)))
+    ]
+    for c in copies:
+        c.start()
     count = scale_ref.shape[3]
     per = 3 * features // count
     hot = (
@@ -92,34 +89,53 @@
         for i in range(height // 8):
             factor = jnp.exp2(s_buf[b, i].astype(f32)).astype(bf16)
             fac_ref[b, i] = jnp.dot(factor, hot, preferred_element_type=f32)
-    half, last = height // 2, height // 8 - 1
-    even_c, even_r = even_column(), even_row()
+    for c in copies:
+        c.wait()
+    even = even_row()
+    for b in range(members):
+        for m in range(3):
+            ends = []
+            for n, i in enumerate((0, height // 8 - 1)):
+                x = buf[m, n, b].astype(f32)
+                if m < 2:
+                    lanes = slice((m + 1) * features, (m + 2) * features)
+                    x = jnp.concatenate(
+                        [x[:, 8 * j : 8 * j + 8] * fac_ref[b, i, j : j + 1, lanes][None] for j in range(tiles)], 1
+                    )
+                ends.append(x)
+            x, y = swap(even, ends[1], ends[0])
+            re_ref[m, b], ro_ref[m, b] = x.astype(bf16), y.astype(bf16)
+
+
+def column_kernel(fac_ref, k_ref, v_ref, tok_ref, ce_ref, co_ref, k_buf, v_buf, t_buf, sem):
+    members, height, breadth, features = k_ref.shape
+    tiles = breadth // 8
+    copies = []
+    for b in range(members):
+        copies.append([
+            pltpu.make_async_copy(src.at[b], dst.at[b], sem.at[3 * b + n])
+            for n, (src, dst) in enumerate(((k_ref, k_buf), (v_ref, v_buf), (tok_ref, t_buf)))
+        ])
+        for c in copies[b]:
+            c.start()
+    half = height // 2
+    even = even_column()
     for b in range(members):
         for c in copies[b]:
             c.wait()
-        ends = {}
-        for i in range(last + 1):
+        for i in range(height // 8):
             rows = slice(8 * i, 8 * i + 8)
-            k = [block_of(k_buf, fac_ref, 1, b, i, j, rows, features) for j in range(tiles)]
-            v = [block_of(v_buf, fac_ref, 2, b, i, j, rows, features) for j in range(tiles)]
+            k = [block_of(k_buf, fac_ref, 1, b, i, j, rows, features) for j in (0, tiles - 1)]
+            v = [block_of(v_buf, fac_ref, 2, b, i, j, rows, features) for j in (0, tiles - 1)]
             low = lower(k[0])
-            left, right = jnp.where(low, k[0], turn(v[0])), jnp.where(low, turn(v[-1]), k[-1])
-            x, y = swap(even_c, right, left)
+            left, right = jnp.where(low, k[0], turn(v[0])), jnp.where(low, turn(v[1]), k[1])
+            x, y = swap(even, right, left)
             ce_ref[b, rows], co_ref[b, rows] = x.astype(bf16), y.astype(bf16)
-            for m, parts in enumerate((k, v)):
-                if i == 0:
-                    ends[m, 0] = jnp.concatenate(parts, 1)[0:4]
-                if i == last:
-                    ends[m, 1] = jnp.concatenate(parts, 1)[4:8]
-        ends[2, 0], ends[2, 1] = t_buf[b, 0:4].astype(f32), t_buf[b, height - 4 : height].astype(f32)
-        for m in range(3):
-            x, y = swap(even_r, ends[m, 1], ends[m, 0])
-            re_ref[m, b], ro_ref[m, b] = x.astype(bf16), y.astype(bf16)
         for r in range(0, half, 4):
             here, there = slice(r, r + 4), slice(half + r, half + r + 4)
             out = slice(height + r, height + r + 4)
             left, right = pack_columns(t_buf[b, here], t_buf[b, there])
-            x, y = swap(even_c, right, left)
+            x, y = swap(even, right, left)
             ce_ref[b, out], co_ref[b, out] = x.astype(bf16), y.astype(bf16)
 
 
@@ -377,7 +393,9 @@
 
     copies = [
         pltpu.make_async_copy(src, dst, sem.at[n])
-        for n, (src, dst) in enumerate(((dq_ref, dq_out), (kv_ref, kv_out)))
+        for n, (src, dst) in enumerate(
+            (x.at[b], y.at[b]) for x, y in ((dq_ref, dq_out), (kv_ref, kv_out)) for b in range(members)
+        )
     ]
     for c in copies:
         c.start()
@@ -535,28 +553,35 @@
     packed_columns = shape(members, packed, 8, features)
     strip = shape(3, members, 4, breadth, features)
     factor, *sides = call(
-        edge_kernel,
-        (
-            shape(*scale_exp.shape[:3], 3 * features, dtype=f32),
-            strip, strip, packed_columns, packed_columns,
+        row_kernel,
+        (shape(*scale_exp.shape[:3], 3 * features, dtype=f32), strip, strip),
+        (scale_exp, k_saved, v_saved, tokens),
+        scratch=(
+            pltpu.VMEM(scale_exp.shape, jnp.int32),
+            pltpu.VMEM((3, 2, members, 4, breadth, features), bf16),
+            pltpu.SemaphoreType.DMA((7,)),
         ),
-        (scale_exp, k_saved, v_saved, tokens),
-        scratch=(pltpu.VMEM(scale_exp.shape, jnp.int32),)
-        + (pltpu.VMEM(tokens.shape, bf16),) * 3
-        + (pltpu.SemaphoreType.DMA((1 + 3 * members,)),),
         far=(0, 1, 2, 3),
         limit=58 << 20,
     )
-    halo_rows = exchange(*sides[0:2], "row")
+    halo_rows = exchange(*sides, "row")
+    sides = call(
+        column_kernel,
+        (packed_columns, packed_columns),
+        (factor, k_saved, v_saved, tokens),
+        scratch=(pltpu.VMEM(tokens.shape, bf16),) * 3 + (pltpu.SemaphoreType.DMA((3 * members,)),),
+        far=(1, 2, 3),
+        limit=58 << 20,
+    )
     cells = members * height * breadth
     qs, gm, do = call(
         prepare_kernel,
         (shape(*tokens.shape),) * 3,
         (crop_start, q_saved, grad_out, factor, w_out),
         smem=(0,),
-        flops=2 * cells * features * features,
-    )
-    halo_columns = exchange(*sides[2:4], COLS)
+        flops=200 * cells * features * features,
+    )
+    *halo_columns, do = lax.optimization_barrier((*exchange(*sides, COLS), do))
     corner = shape(members, 12, 8, features)
     corners = exchange(*call(corner_kernel, (corner, corner), halo_columns), "row")
     tiles = breadth // 8
@@ -595,7 +620,7 @@
             pltpu.VMEM((members, tall, breadth, features), bf16),
             pltpu.VMEM((members, tall, breadth + 8, 2 * features), bf16),
             pltpu.VMEM((2 * tiles, 256, features // 2), f32),
-            pltpu.SemaphoreType.DMA((2,)),
+            pltpu.SemaphoreType.DMA((2 * members,)),
         ),
         far_outs=(2, 3),
         flops=12 * cells * features * features,

time: 96.9 us -> 101 us (1.042)
  Pallas kernels: 25.2 us -> 28.2 us
  starting transfers between devices: 42.4 us -> 44 us
    ppermute x10, starting transfers between devices: 15.2 us -> 18.4 us  [exchange(): out.append(lax.ppermute(x, axes, pairs + [(j, i) for i, j in pairs]))]
    pallas_call x11 -> x12, Pallas kernels: 25.2 us -> 28.2 us  [call(): pl.pallas_call(kernel, out_shape=outs, in_specs=[SMEM if n in smem else A...]
    all_to_all x1, starting transfers between devices: 15.8 us -> 14.3 us  [body(): parts = lax.all_to_all(both, ('row', 'pair'), 0, 0, tiled=True)]
    unnamed x22 -> x20, local copies, waits for them, and re-layouts: 4.21 us -> 3.32 us
  transfers between devices with their start and end apart: 13 -> 13, of which waited for: 4 -> 4; matrix products, arithmetic and copies ran while one was open for 0% -> 0% of each run, Pallas kernels for 11% -> 14%
where the time goes in v6:
time: 101 us
  starting transfers between devices  44 us (44%)
  Pallas kernels  28.2 us (28%)
  waiting for transfers between devices  24.2 us (24%)
  local copies, waits for them, and re-layouts  3.32 us (3%)
    pallas_call x12, Pallas kernels, call(): pl.pallas_call(kernel, out_shape=outs, in_specs=[SMEM if n in smem else A...  28.2 us
    ppermute x10, starting transfers between devices, exchange(): out.append(lax.ppermute(x, axes, pairs + [(j, i) for i, j in pairs]))  18.4 us
    all_to_all x1, starting transfers between devices, body(): parts = lax.all_to_all(both, ('row', 'pair'), 0, 0, tiled=True)  14.3 us
    ppermute x10, waiting for transfers between devices, exchange(): out.append(lax.ppermute(x, axes, pairs + [(j, i) for i, j in pairs]))  13.2 us
    all_to_all x1, starting transfers between devices, body(): squares = lax.all_to_all(square, ('row', 'pair', 'core'), 0, 0, tiled=True)  11.3 us
    all_to_all x1, waiting for transfers between devices, body(): squares = lax.all_to_all(square, ('row', 'pair', 'core'), 0, 0, tiled=True)  8.33 us
    unnamed x20, local copies, waits for them, and re-layouts  3.32 us
    ppermute x1, waiting for transfers between devices, body(): other = lax.ppermute(send, 'core', [(0, 1), (1, 0)])  2.65 us
  transfers between devices with their start and end apart: 13, of which 4 were waited for; matrix products, arithmetic and copies ran while one was open for 0% of the time, Pallas kernels for 14%

profile of v6, /device:TPU:1, one launch (start us, length us, event | category | flops | bytes accessed | tf_op | source)
XLA Modules:
  0.0 100.7 jit_solution(14057413116076507251)
XLA Ops:
  0.7 2.5 %shard_map.112 = (f32[2,3,2,1536]{3,2,1,0:T(2,128)}, bf16[3,2,4,16,512]{4,3,2,1,0:T(8,128)(2,1)}, bf16[3,2,4,16,512]{4,3,2,1,0:T(8,128)(2,1)}) custom-call(s32[2,3,2,24]{3,2,1,0:T(2,128)} %scale_ref.1, bf16[2,24,16,512]{3,2,1,0:T(8,128)(2,1)} %k_ref.5, bf16[2,24,16,512]{3,2,1,0:T(8,128)(2,1)} %v_ref.5, bf16[2,24,16,512]{3,2,1,0:T(8,128)(2,1)} %tok_ref.5), custom_call_target="tpu_custom_call" | custom-call | bytes 3220608 | tf_op jit(solution)/shard_map/pallas_call | solution.py:27
  3.2 2.5 %collective-permute-start.2 = (bf16[3,2,4,16,512]{4,3,2,1,0:T(8,128)(2,1)}, bf16[3,2,4,16,512]{4,3,2,1,0:T(8,128)(2,1)S(1)}, u32[]{:S(2)}, u32[]{:S(2)}) collective-permute-start(bf16[3,2,4,16,512]{4,3,2,1,0:T(8,128)(2,1)} %get-tuple-element.50), channel_id=1, source_target_pairs={{0,16},{32,48},{64,80},{96,112},{16,0},{48,32},{80,64},{112,96},{1... | collective-permute-start | bytes 1179656 | tf_op jit(solution)/shard_map/ppermute | solution.py:545
  5.7 0.7 collective-permute-start.3
  6.4 3.8 %shard_map.114 = (bf16[2,36,8,512]{3,2,1,0:T(8,128)(2,1)}, bf16[2,36,8,512]{3,2,1,0:T(8,128)(2,1)}) custom-call(f32[2,3,2,1536]{3,2,1,0:T(2,128)} %get-tuple-element.35.fac_ref, bf16[2,24,16,512]{3,2,1,0:T(8,128)(2,1)} %k_ref.5, bf16[2,24,16,512]{3,2,1,0:T(8,128)(2,1)} %v_ref.5, bf16[2,24,16,512]{3,2,1,0:T(8,128)(2,1)} %tok_ref.5), custom_call_target="tpu_custom_call" | custom-call | bytes 3612672 | tf_op jit(solution)/shard_map/pallas_call | solution.py:27
  10.2 1.0 %collective-permute-start = (bf16[2,36,8,512]{3,2,1,0:T(8,128)(2,1)}, bf16[2,36,8,512]{3,2,1,0:T(8,128)(2,1)S(1)}, u32[]{:S(2)}, u32[]{:S(2)}) collective-permute-start(bf16[2,36,8,512]{3,2,1,0:T(8,128)(2,1)} %get-tuple-element.37), channel_id=1, source_target_pairs={{0,1},{2,3},{4,5},{6,7},{8,9},{10,11},{12,13},{14,15},{1,0},{3,2},... | collective-permute-start | bytes 1769480 | tf_op jit(solution)/shard_map/ppermute | solution.py:545
  11.2 3.2 %collective-permute-start.1 = (bf16[2,36,8,512]{3,2,1,0:T(8,128)(2,1)}, bf16[2,36,8,512]{3,2,1,0:T(8,128)(2,1)S(1)}, u32[]{:S(2)}, u32[]{:S(2)}) collective-permute-start(bf16[2,36,8,512]{3,2,1,0:T(8,128)(2,1)} %get-tuple-element.38), channel_id=1, source_target_pairs={{1,2},{3,4},{5,6},{7,8},{9,10},{11,12},{13,14},{2,1},{4,3},{6,5},{... | collective-permute-start | bytes 1769480 | tf_op jit(solution)/shard_map/ppermute | solution.py:545
  14.5 1.7 %shard_map.113 = (bf16[2,24,16,512]{3,2,1,0:T(8,128)(2,1)S(1)}, bf16[2,24,16,512]{3,2,1,0:T(8,128)(2,1)S(1)}, bf16[2,24,16,512]{3,2,1,0:T(8,128)(2,1)S(1)}) custom-call(s32[2,2]{1,0:T(2,128)S(1)} %copy-done.9, bf16[2,24,16,512]{3,2,1,0:T(8,128)(2,1)S(1)} %copy-done.6, bf16[2,24,16,512]{3,2,1,0:T(8,128)(2,1)S(1)} %copy-done.7, ...), custom_call_target="tpu_custom_call" | custom-call | flops 40265318400 | bytes 4530192 | tf_op jit(solution)/shard_map/pallas_call | solution.py:27
  16.2 6.5 %collective-permute-done.1.fr_ref.fo_ref = bf16[2,36,8,512]{3,2,1,0:T(8,128)(2,1)S(1)} collective-permute-done((bf16[2,36,8,512]{3,2,1,0:T(8,128)(2,1)}, bf16[2,36,8,512]{3,2,1,0:T(8,128)(2,1)S(1)}, u32[]{:S(2)}, u32[]{:S(2)}) %collective-permute-start.1) | collective-permute-done | bytes 589856 | tf_op jit(solution)/shard_map/ppermute | solution.py:545
  22.8 0.2 shard_map.116
  22.9 4.6 %collective-permute-start.4 = (bf16[2,12,8,512]{3,2,1,0:T(8,128)(2,1)S(1)}, bf16[2,12,8,512]{3,2,1,0:T(8,128)(2,1)S(1)}, u32[]{:S(2)}, u32[]{:S(2)}) collective-permute-start(bf16[2,12,8,512]{3,2,1,0:T(8,128)(2,1)S(1)} %get-tuple-element.52), channel_id=1, source_target_pairs={{0,16},{32,48},{64,80},{96,112},{16,0},{48,32},{80,64},{112,96},{1... | collective-permute-start | bytes 589832 | tf_op jit(solution)/shard_map/ppermute | solution.py:545
  27.5 0.8 collective-permute-start.5
  28.4 0.0 copy-start
  28.4 3.8 %shard_map.115 = (bf16[2,2,24,16,512]{4,3,2,1,0:T(8,128)(2,1)S(1)}, bf16[2,2,24,16,512]{4,3,2,1,0:T(8,128)(2,1)S(1)}, f32[2,2,16,16,512]{4,3,2,1,0:T(8,128)S(1)}...) custom-call(bf16[2,24,16,512]{3,2,1,0:T(8,128)(2,1)S(1)} %get-tuple-el, ...), custom_call_target="tpu_custom_call" | custom-call | flops 805306368 | bytes 12263424 | tf_op jit(solution)/shard_map/pallas_call | solution.py:27
  32.2 9.7 %shard_map.117 = (bf16[8,8,64,128]{3,2,1,0:T(8,128)(2,1)S(1)}, bf16[8,8,64,128]{3,2,1,0:T(8,128)(2,1)S(1)}, bf16[2,32,16,512]{3,2,1,0:T(8,128)(2,1)S(1)}, bf16[2,32,24,1024]{3,2,1,0:T(8,128)(2,1)}) custom-call(bf16[2,24,16,512]{3,2,1,0:T(8,128)(2,1)S(1)} %get-tuple-element.36.qs_ref, bf16[2,24,16,512]{3,2,1,0:T(8,128)(2,1)S(1)} %get-tuple-element.40.do_ref, ...), custom_call_target="tpu_custom_call" | custom-call | flops 2415919104 | bytes 19660800 | tf_op jit(solution)/shard_map/pallas_call | solution.py:27
  41.9 0.1 collective-permute-start.10
  42.0 2.6 %collective-permute-done.10.y_ref = bf16[8,8,64,128]{3,2,1,0:T(8,128)(2,1)S(1)} collective-permute-done((bf16[8,8,64,128]{3,2,1,0:T(8,128)(2,1)S(1)}, bf16[8,8,64,128]{3,2,1,0:T(8,128)(2,1)S(1)}, u32[]{:S(2)}, u32[]{:S(2)}) %collective-permute-start.10) | collective-permute-done | bytes 1048608 | tf_op jit(solution)/shard_map/ppermute | solution.py:629
  44.6 1.2 %shard_map.121 = bf16[8,8,64,128]{3,2,1,0:T(8,128)(2,1)} custom-call(bf16[8,8,64,128]{3,2,1,0:T(8,128)(2,1)S(1)} %get-tuple-element.61.x_ref, bf16[8,8,64,128]{3,2,1,0:T(8,128)(2,1)S(1)} %collective-permute-done.10.y_ref), custom_call_target="tpu_custom_call" | custom-call | bytes 3145728 | tf_op jit(solution)/shard_map/pallas_call | solution.py:27
  45.9 14.3 %all-to-all-start = ((bf16[64,64,128]{2,1,0:T(8,128)(2,1)}), bf16[64,64,128]{2,1,0:T(8,128)(2,1)S(1)}, u32[]{:S(2)}, u32[]{:S(2)}) async-start(bf16[64,64,128]{2,1,0:T(8,128)(2,1)} %bitcast), calls=%async_computation | async-start | bytes 2097152 | tf_op jit(solution)/shard_map/all_to_all | solution.py:631
  60.1 1.9 %copy-done.3 = bf16[2,32,24,1024]{3,2,1,0:T(8,128)(2,1)S(1)} copy-done((bf16[2,32,24,1024]{3,2,1,0:T(8,128)(2,1)S(1)}, bf16[2,32,24,1024]{3,2,1,0:T(8,128)(2,1)}, u32[]{:S(2)}) %copy-start.3) | copy-done | bytes 3145752
  62.0 1.4 %copy-done.4 = bf16[512,1536]{1,0:T(8,128)(2,1)S(1)} copy-done((bf16[512,1536]{1,0:T(8,128)(2,1)S(1)}, bf16[512,1536]{1,0:T(8,128)(2,1)}, u32[]{:S(2)}) %copy-start.4) | copy-done | bytes 1572888
  63.4 2.4 %shard_map.118 = (bf16[2,32,16,512]{3,2,1,0:T(8,128)(2,1)S(1)}, bf16[2,16,8,512]{3,2,1,0:T(8,128)(2,1)S(1)}, bf16[2,16,8,512]{3,2,1,0:T(8,128)(2,1)S(1)}) custom-call(bf16[2,32,24,1024]{3,2,1,0:T(8,128)(2,1)S(1)} %copy-done.3, bf16[2,32,16,512]{3,2,1,0:T(8,128)(2,1)S(1)} %get-tuple-element.55.dq_ref, bf16[512,1536]{1,0:T(8,128)(2,1)S(1)} %copy-done.4), custom_call_target="tpu_custom_call" | custom-call | flops 1207959552 | bytes 7340032 | tf_op jit(solution)/shard_map/pallas_call | solution.py:27
  65.8 0.7 collective-permute-start.6
  66.5 2.9 %collective-permute-start.7 = (bf16[2,16,8,512]{3,2,1,0:T(8,128)(2,1)S(1)}, bf16[2,16,8,512]{3,2,1,0:T(8,128)(2,1)S(1)}, u32[]{:S(2)}, u32[]{:S(2)}) collective-permute-start(bf16[2,16,8,512]{3,2,1,0:T(8,128)(2,1)S(1)} %get-tuple-element.58), channel_id=1, source_target_pairs={{1,2},{3,4},{5,6},{7,8},{9,10},{11,12},{13,14},{2,1},{4,3},{6,5},{... | collective-permute-start | bytes 786440 | tf_op jit(solution)/shard_map/ppermute | solution.py:545
  69.4 6.6 %collective-permute-done.7.fo_ref = bf16[2,16,8,512]{3,2,1,0:T(8,128)(2,1)S(1)} collective-permute-done((bf16[2,16,8,512]{3,2,1,0:T(8,128)(2,1)S(1)}, bf16[2,16,8,512]{3,2,1,0:T(8,128)(2,1)S(1)}, u32[]{:S(2)}, u32[]{:S(2)}) %collective-permute-start.7) | collective-permute-done | bytes 262176 | tf_op jit(solution)/shard_map/ppermute | solution.py:545
  76.1 0.1 shard_map.119
  76.2 1.3 %collective-permute-start.8 = (bf16[2,4,16,512]{3,2,1,0:T(8,128)(2,1)S(1)}, bf16[2,4,16,512]{3,2,1,0:T(8,128)(2,1)S(1)}, u32[]{:S(2)}, u32[]{:S(2)}) collective-permute-start(bf16[2,4,16,512]{3,2,1,0:T(8,128)(2,1)S(1)} %get-tuple-element.59), channel_id=1, source_target_pairs={{0,16},{32,48},{64,80},{96,112},{16,0},{48,32},{80,64},{112,96},{1... | collective-permute-start | bytes 393224 | tf_op jit(solution)/shard_map/ppermute | solution.py:545
  77.5 0.7 collective-permute-start.9
  78.1 0.8 shard_map.122
  79.0 11.3 %all-to-all-start.1 = ((f32[128,1,128]{2,1,0:T(1,128)}), f32[128,1,128]{2,1,0:T(1,128)S(1)}, u32[]{:S(2)}, u32[]{:S(2)}) async-start(f32[128,1,128]{2,1,0:T(1,128)} %bitcast.2), calls=%async_computation.1 | async-start | bytes 131072 | tf_op jit(solution)/shard_map/all_to_all | solution.py:654
  90.3 1.2 %shard_map.120 = bf16[2,24,16,512]{3,2,1,0:T(8,128)(2,1)} custom-call(bf16[2,32,16,512]{3,2,1,0:T(8,128)(2,1)S(1)} %get-tuple-element.56.gt_ref, bf16[2,16,8,512]{3,2,1,0:T(8,128)(2,1)S(1)} %collective-permute-done.6.fe_ref, bf16[2,16,8,512]{3,2,1,0:T(8,128)(2,1)S(1)} %collective-permute-done.7.fo_ref, ...), custom_call_target="tpu_custom_call" | custom-call | bytes 2621440 | tf_op jit(solution)/shard_map/pallas_call | solution.py:27
  91.5 8.3 %all-to-all-done.1 = f32[128,1,128]{2,1,0:T(1,128)S(1)} async-done(((f32[128,1,128]{2,1,0:T(1,128)}), f32[128,1,128]{2,1,0:T(1,128)S(1)}, u32[]{:S(2)}, u32[]{:S(2)}) %all-to-all-start.1) | async-done | bytes 65568 | tf_op jit(solution)/shard_map/all_to_all | solution.py:654
  99.9 0.8 shard_map.123
  (26 shorter events, 0.1 us)
Async XLA Ops:
  0.6 13.8 %copy-start.9 = (s32[2,2]{1,0:T(2,128)S(1)}, s32[2,2]{1,0:T(2,128)}, u32[]{:S(2)}) copy-start(s32[2,2]{1,0:T(2,128)} %crop_ref.1) | copy-start | bytes 52
  0.6 13.8 %copy-start.7 = (bf16[2,24,16,512]{3,2,1,0:T(8,128)(2,1)S(1)}, bf16[2,24,16,512]{3,2,1,0:T(8,128)(2,1)}, u32[]{:S(2)}) copy-start(bf16[2,24,16,512]{3,2,1,0:T(8,128)(2,1)} %g_ref.1) | copy-start | bytes 2359300
  0.7 13.8 %copy-start.6 = (bf16[2,24,16,512]{3,2,1,0:T(8,128)(2,1)S(1)}, bf16[2,24,16,512]{3,2,1,0:T(8,128)(2,1)}, u32[]{:S(2)}) copy-start(bf16[2,24,16,512]{3,2,1,0:T(8,128)(2,1)} %q_ref.1) | copy-start | bytes 2359300
  0.7 13.8 %copy-start.8 = (bf16[512,512]{1,0:T(8,128)(2,1)S(1)}, bf16[512,512]{1,0:T(8,128)(2,1)}, u32[]{:S(2)}) copy-start(bf16[512,512]{1,0:T(8,128)(2,1)} %w_ref.2) | copy-start | bytes 1572868
  3.1 11.3 %copy-start.5 = (f32[2,3,2,1536]{3,2,1,0:T(2,128)S(1)}, f32[2,3,2,1536]{3,2,1,0:T(2,128)}, u32[]{:S(2)}) copy-start(f32[2,3,2,1536]{3,2,1,0:T(2,128)} %get-tuple-element.35.fac_ref) | copy-start | bytes 221188
  3.2 29.0 %collective-permute-start.2 = (bf16[3,2,4,16,512]{4,3,2,1,0:T(8,128)(2,1)}, bf16[3,2,4,16,512]{4,3,2,1,0:T(8,128)(2,1)S(1)}, u32[]{:S(2)}, u32[]{:S(2)}) collective-permute-start(bf16[3,2,4,16,512]{4,3,2,1,0:T(8,128)(2,1)} %get-tuple-element.50), channel_id=1, source_target_pairs={{0,16},{32,48},{64,80},{96,112},{16,0},{48,32},{80,64},{112,96},{1... | collective-permute-start | bytes 1179656 | tf_op jit(solution)/shard_map/ppermute | solution.py:545
  5.7 26.5 %collective-permute-start.3 = (bf16[3,2,4,16,512]{4,3,2,1,0:T(8,128)(2,1)}, bf16[3,2,4,16,512]{4,3,2,1,0:T(8,128)(2,1)S(1)}, u32[]{:S(2)}, u32[]{:S(2)}) collective-permute-start(bf16[3,2,4,16,512]{4,3,2,1,0:T(8,128)(2,1)} %get-tuple-element.51), channel_id=1, source_target_pairs={{16,32},{48,64},{80,96},{32,16},{64,48},{96,80},{17,33},{49,65},{8... | collective-permute-start | bytes 1179656 | tf_op jit(solution)/shard_map/ppermute | solution.py:545
  10.2 6.0 %collective-permute-start = (bf16[2,36,8,512]{3,2,1,0:T(8,128)(2,1)}, bf16[2,36,8,512]{3,2,1,0:T(8,128)(2,1)S(1)}, u32[]{:S(2)}, u32[]{:S(2)}) collective-permute-start(bf16[2,36,8,512]{3,2,1,0:T(8,128)(2,1)} %get-tuple-element.37), channel_id=1, source_target_pairs={{0,1},{2,3},{4,5},{6,7},{8,9},{10,11},{12,13},{14,15},{1,0},{3,2},... | collective-permute-start | bytes 1769480 | tf_op jit(solution)/shard_map/ppermute | solution.py:545
  11.2 17.1 %copy-start.1 = (bf16[2,24,16,512]{3,2,1,0:T(8,128)(2,1)S(1)}, bf16[2,24,16,512]{3,2,1,0:T(8,128)(2,1)}, u32[]{:S(2)}) copy-start(bf16[2,24,16,512]{3,2,1,0:T(8,128)(2,1)} %k_ref.5) | copy-start | bytes 2359300
  11.2 17.1 %copy-start.2 = (bf16[2,24,16,512]{3,2,1,0:T(8,128)(2,1)S(1)}, bf16[2,24,16,512]{3,2,1,0:T(8,128)(2,1)}, u32[]{:S(2)}) copy-start(bf16[2,24,16,512]{3,2,1,0:T(8,128)(2,1)} %v_ref.5) | copy-start | bytes 2359300
  11.2 11.5 %collective-permute-start.1 = (bf16[2,36,8,512]{3,2,1,0:T(8,128)(2,1)}, bf16[2,36,8,512]{3,2,1,0:T(8,128)(2,1)S(1)}, u32[]{:S(2)}, u32[]{:S(2)}) collective-permute-start(bf16[2,36,8,512]{3,2,1,0:T(8,128)(2,1)} %get-tuple-element.38), channel_id=1, source_target_pairs={{1,2},{3,4},{5,6},{7,8},{9,10},{11,12},{13,14},{2,1},{4,3},{6,5},{... | collective-permute-start | bytes 1769480 | tf_op jit(solution)/shard_map/ppermute | solution.py:545
  22.9 9.2 %collective-permute-start.4 = (bf16[2,12,8,512]{3,2,1,0:T(8,128)(2,1)S(1)}, bf16[2,12,8,512]{3,2,1,0:T(8,128)(2,1)S(1)}, u32[]{:S(2)}, u32[]{:S(2)}) collective-permute-start(bf16[2,12,8,512]{3,2,1,0:T(8,128)(2,1)S(1)} %get-tuple-element.52), channel_id=1, source_target_pairs={{0,16},{32,48},{64,80},{96,112},{16,0},{48,32},{80,64},{112,96},{1... | collective-permute-start | bytes 589832 | tf_op jit(solution)/shard_map/ppermute | solution.py:545
  27.5 4.7 %collective-permute-start.5 = (bf16[2,12,8,512]{3,2,1,0:T(8,128)(2,1)S(1)}, bf16[2,12,8,512]{3,2,1,0:T(8,128)(2,1)S(1)}, u32[]{:S(2)}, u32[]{:S(2)}) collective-permute-start(bf16[2,12,8,512]{3,2,1,0:T(8,128)(2,1)S(1)} %get-tuple-element.53), channel_id=1, source_target_pairs={{16,32},{48,64},{80,96},{32,16},{64,48},{96,80},{17,33},{49,65},{8... | collective-permute-start | bytes 589832 | tf_op jit(solution)/shard_map/ppermute | solution.py:545
  28.4 3.8 %copy-start = (bf16[2,24,16,512]{3,2,1,0:T(8,128)(2,1)S(1)}, bf16[2,24,16,512]{3,2,1,0:T(8,128)(2,1)}, u32[]{:S(2)}) copy-start(bf16[2,24,16,512]{3,2,1,0:T(8,128)(2,1)} %tok_ref.5) | copy-start | bytes 2359300
  41.9 2.7 %collective-permute-start.10 = (bf16[8,8,64,128]{3,2,1,0:T(8,128)(2,1)S(1)}, bf16[8,8,64,128]{3,2,1,0:T(8,128)(2,1)S(1)}, u32[]{:S(2)}, u32[]{:S(2)}) collective-permute-start(bf16[8,8,64,128]{3,2,1,0:T(8,128)(2,1)S(1)} %get-tuple-element.62), channel_id=1, source_target_pairs={{0,1},{1,0},{2,3},{3,2},{4,5},{5,4},{6,7},{7,6},{8,9},{9,8},{10,11... | collective-permute-start | bytes 3145736 | tf_op jit(solution)/shard_map/ppermute | solution.py:629
  45.9 32.3 %all-to-all-start = ((bf16[64,64,128]{2,1,0:T(8,128)(2,1)}), bf16[64,64,128]{2,1,0:T(8,128)(2,1)S(1)}, u32[]{:S(2)}, u32[]{:S(2)}) async-start(bf16[64,64,128]{2,1,0:T(8,128)(2,1)} %bitcast), calls=%async_computation | async-start | bytes 2097152 | tf_op jit(solution)/shard_map/all_to_all | solution.py:631
  60.1 1.9 %copy-start.3 = (bf16[2,32,24,1024]{3,2,1,0:T(8,128)(2,1)S(1)}, bf16[2,32,24,1024]{3,2,1,0:T(8,128)(2,1)}, u32[]{:S(2)}) copy-start(bf16[2,32,24,1024]{3,2,1,0:T(8,128)(2,1)} %get-tuple-element.54.kv_ref) | copy-start | bytes 9437188
  62.0 1.4 %copy-start.4 = (bf16[512,1536]{1,0:T(8,128)(2,1)S(1)}, bf16[512,1536]{1,0:T(8,128)(2,1)}, u32[]{:S(2)}) copy-start(bf16[512,1536]{1,0:T(8,128)(2,1)} %w_ref.3) | copy-start | bytes 4718596
  65.8 3.6 %collective-permute-start.6 = (bf16[2,16,8,512]{3,2,1,0:T(8,128)(2,1)S(1)}, bf16[2,16,8,512]{3,2,1,0:T(8,128)(2,1)S(1)}, u32[]{:S(2)}, u32[]{:S(2)}) collective-permute-start(bf16[2,16,8,512]{3,2,1,0:T(8,128)(2,1)S(1)} %get-tuple-element.57), channel_id=1, source_target_pairs={{0,1},{2,3},{4,5},{6,7},{8,9},{10,11},{12,13},{14,15},{1,0},{3,2},... | collective-permute-start | bytes 786440 | tf_op jit(solution)/shard_map/ppermute | solution.py:545
  66.5 9.5 %collective-permute-start.7 = (bf16[2,16,8,512]{3,2,1,0:T(8,128)(2,1)S(1)}, bf16[2,16,8,512]{3,2,1,0:T(8,128)(2,1)S(1)}, u32[]{:S(2)}, u32[]{:S(2)}) collective-permute-start(bf16[2,16,8,512]{3,2,1,0:T(8,128)(2,1)S(1)} %get-tuple-element.58), channel_id=1, source_target_pairs={{1,2},{3,4},{5,6},{7,8},{9,10},{11,12},{13,14},{2,1},{4,3},{6,5},{... | collective-permute-start | bytes 786440 | tf_op jit(solution)/shard_map/ppermute | solution.py:545
  76.2 14.1 %collective-permute-start.8 = (bf16[2,4,16,512]{3,2,1,0:T(8,128)(2,1)S(1)}, bf16[2,4,16,512]{3,2,1,0:T(8,128)(2,1)S(1)}, u32[]{:S(2)}, u32[]{:S(2)}) collective-permute-start(bf16[2,4,16,512]{3,2,1,0:T(8,128)(2,1)S(1)} %get-tuple-element.59), channel_id=1, source_target_pairs={{0,16},{32,48},{64,80},{96,112},{16,0},{48,32},{80,64},{112,96},{1... | collective-permute-start | bytes 393224 | tf_op jit(solution)/shard_map/ppermute | solution.py:545
  77.5 12.8 %collective-permute-start.9 = (bf16[2,4,16,512]{3,2,1,0:T(8,128)(2,1)S(1)}, bf16[2,4,16,512]{3,2,1,0:T(8,128)(2,1)S(1)}, u32[]{:S(2)}, u32[]{:S(2)}) collective-permute-start(bf16[2,4,16,512]{3,2,1,0:T(8,128)(2,1)S(1)} %get-tuple-element.60), channel_id=1, source_target_pairs={{16,32},{48,64},{80,96},{32,16},{64,48},{96,80},{17,33},{49,65},{8... | collective-permute-start | bytes 393224 | tf_op jit(solution)/shard_map/ppermute | solution.py:545
  79.0 20.9 %all-to-all-start.1 = ((f32[128,1,128]{2,1,0:T(1,128)}), f32[128,1,128]{2,1,0:T(1,128)S(1)}, u32[]{:S(2)}, u32[]{:S(2)}) async-start(f32[128,1,128]{2,1,0:T(1,128)} %bitcast.2), calls=%async_computation.1 | async-start | bytes 131072 | tf_op jit(solution)/shard_map/all_to_all | solution.py:654

commit v7 on v5

--- a/solution.py
+++ b/solution.py
@@ -67,7 +67,7 @@
 
 
 def edge_kernel(
-    scale_ref, k_ref, v_ref, tok_ref, fac_ref, re_ref, ro_ref, ce_ref, co_ref, s_buf, k_buf, v_buf, t_buf, sem
+    scale_ref, k_ref, v_ref, tok_ref, fac_ref, ro_ref, re_ref, co_ref, ce_ref, s_buf, k_buf, v_buf, t_buf, sem
 ):
     members, height, breadth, features = k_ref.shape
     tiles = breadth // 8
@@ -131,7 +131,7 @@
     return jnp.where(low, x0, turn(y0)), jnp.where(low, turn(y1), x1)
 
 
-def corner_kernel(fe_ref, fo_ref, re_ref, ro_ref):
+def corner_kernel(fo_ref, fe_ref, ro_ref, re_ref):
     members, packed = fe_ref.shape[:2]
     height = packed * 2 // 3
     half = height // 2
@@ -268,7 +268,7 @@
 
 
 def middle_kernel(
-    qs_ref, do_ref, k_ref, v_ref, fac_ref, fl_ref, fr_ref, kt_ref, vt_ref, dk_ref, dv_ref, o_ref, dq_ref, bias_ref
+    qs_ref, do_ref, k_ref, v_ref, fac_ref, fr_ref, fl_ref, kt_ref, vt_ref, dk_ref, dv_ref, o_ref, dq_ref, bias_ref
 ):
     members, height, breadth, features = qs_ref.shape
     strips, tiles = height // 8, breadth // 8
@@ -300,7 +300,7 @@
 
 def main_kernel(
     qs_ref, do_ref, kt_ref, vt_ref, dkm_ref, dvm_ref, om_ref, dqm_ref, gm_ref, tok_ref,
-    fl_ref, fr_ref, he_ref, ho_ref, ke_ref, ko_ref,
+    fr_ref, fl_ref, ho_ref, he_ref, ko_ref, ke_ref,
     keep_ref, send_ref, dq_out, kv_out,
     kh_ref, vh_ref, dkt_ref, dvt_ref, o_ref, tp_ref, all_ref, dq_ref, kv_ref, bias_ref, sem,
 ):
@@ -377,7 +377,9 @@
 
     copies = [
         pltpu.make_async_copy(src, dst, sem.at[n])
-        for n, (src, dst) in enumerate(((dq_ref, dq_out), (kv_ref, kv_out)))
+        for n, (src, dst) in enumerate(
+            (x.at[b], y.at[b]) for x, y in ((dq_ref, dq_out), (kv_ref, kv_out)) for b in range(members)
+        )
     ]
     for c in copies:
         c.start()
@@ -435,7 +437,7 @@
         c.wait()
 
 
-def token_kernel(kv_ref, dq_ref, w_ref, gt_ref, ce_ref, co_ref):
+def token_kernel(kv_ref, dq_ref, w_ref, gt_ref, co_ref, ce_ref):
     members, tall, breadth, features = dq_ref.shape
     across = (((1,), (1,)), ((), ()))
     middle = tall // 2
@@ -480,7 +482,7 @@
     square_ref[...] = jnp.broadcast_to(square, square_ref.shape)
 
 
-def halo_kernel(gt_ref, fe_ref, fo_ref, re_ref, ro_ref):
+def halo_kernel(gt_ref, fo_ref, fe_ref, ro_ref, re_ref):
     members, tall = gt_ref.shape[:2]
     half = tall // 2
     for b in range(members):
@@ -492,7 +494,7 @@
         re_ref[b], ro_ref[b] = x.astype(bf16), y.astype(bf16)
 
 
-def join_kernel(gt_ref, fe_ref, fo_ref, he_ref, ho_ref, tok_ref):
+def join_kernel(gt_ref, fo_ref, fe_ref, ho_ref, he_ref, tok_ref):
     members, height = tok_ref.shape[:2]
     half = (height + 8) // 2
     for b in range(members):
@@ -519,10 +521,10 @@
     out_ref[...] = x.T[main:]
 
 
-def exchange(even, odd, axes):
+def exchange(odd, even, axes):
     size = lax.axis_size(axes)
     out = []
-    for x, first in ((even, 0), (odd, 1)):
+    for x, first in ((odd, 1), (even, 0)):
         pairs = [(i, i + 1) for i in range(first, size - 1, 2)]
         out.append(lax.ppermute(x, axes, pairs + [(j, i) for i, j in pairs]))
     return out
@@ -556,7 +558,7 @@
         smem=(0,),
         flops=2 * cells * features * features,
     )
-    halo_columns = exchange(*sides[2:4], COLS)
+    *halo_columns, do = lax.optimization_barrier((*exchange(*sides[2:4], COLS), do))
     corner = shape(members, 12, 8, features)
     corners = exchange(*call(corner_kernel, (corner, corner), halo_columns), "row")
     tiles = breadth // 8
@@ -595,7 +597,7 @@
             pltpu.VMEM((members, tall, breadth, features), bf16),
             pltpu.VMEM((members, tall, breadth + 8, 2 * features), bf16),
             pltpu.VMEM((2 * tiles, 256, features // 2), f32),
-            pltpu.SemaphoreType.DMA((2,)),
+            pltpu.SemaphoreType.DMA((2 * members,)),
         ),
         far_outs=(2, 3),
         flops=12 * cells * features * features,

time: 96.9 us -> 96.3 us (level)
  waiting for transfers between devices: 23.7 us -> 19 us
  starting transfers between devices: 42.4 us -> 46.5 us
    ppermute x10, starting transfers between devices: 15.2 us -> 23.4 us  [exchange(): out.append(lax.ppermute(x, axes, pairs + [(j, i) for i, j in pairs]))]
    ppermute x10, waiting for transfers between devices: 12.7 us -> 8.4 us  [exchange(): out.append(lax.ppermute(x, axes, pairs + [(j, i) for i, j in pairs]))]
    all_to_all x1, starting transfers between devices: 11.3 us -> 8.82 us  [body(): squares = lax.all_to_all(square, ('row', 'pair', 'core'), 0, 0, tiled=True)]
    all_to_all x1, starting transfers between devices: 15.8 us -> 13.5 us  [body(): parts = lax.all_to_all(both, ('row', 'pair'), 0, 0, tiled=True)]
  transfers between devices with their start and end apart: 13 -> 13, of which waited for: 4 -> 5; matrix products, arithmetic and copies ran while one was open for 0% -> 0% of each run, Pallas kernels for 11% -> 11%
where the time goes in v7:
time: 96.3 us; the launch traced here: 95.8 us
  starting transfers between devices  46.5 us (48%)
  Pallas kernels  25.3 us (26%)
  waiting for transfers between devices  19 us (20%)
  local copies, waits for them, and re-layouts  4.2 us (4%)
    pallas_call x11, Pallas kernels, call(): pl.pallas_call(kernel, out_shape=outs, in_specs=[SMEM if n in smem else A...  25.3 us
    ppermute x10, starting transfers between devices, exchange(): out.append(lax.ppermute(x, axes, pairs + [(j, i) for i, j in pairs]))  23.4 us
    all_to_all x1, starting transfers between devices, body(): parts = lax.all_to_all(both, ('row', 'pair'), 0, 0, tiled=True)  13.5 us
    all_to_all x1, starting transfers between devices, body(): squares = lax.all_to_all(square, ('row', 'pair', 'core'), 0, 0, tiled=True)  8.82 us
    ppermute x10, waiting for transfers between devices, exchange(): out.append(lax.ppermute(x, axes, pairs + [(j, i) for i, j in pairs]))  8.4 us
    all_to_all x1, waiting for transfers between devices, body(): squares = lax.all_to_all(square, ('row', 'pair', 'core'), 0, 0, tiled=True)  8.33 us
    unnamed x22, local copies, waits for them, and re-layouts  4.2 us
    ppermute x1, waiting for transfers between devices, body(): other = lax.ppermute(send, 'core', [(0, 1), (1, 0)])  2.29 us
  transfers between devices with their start and end apart: 13, of which 5 were waited for; matrix products, arithmetic and copies ran while one was open for 0% of the time, Pallas kernels for 11%

profile of v7, /device:TPU:1, one launch (start us, length us, event | category | flops | bytes accessed | tf_op | source)
XLA Modules:
  0.0 95.8 jit_solution(9552903128852458541)
XLA Ops:
  0.7 3.3 %shard_map.112 = (f32[2,3,2,1536]{3,2,1,0:T(2,128)}, bf16[3,2,4,16,512]{4,3,2,1,0:T(8,128)(2,1)}, bf16[3,2,4,16,512]{4,3,2,1,0:T(8,128)(2,1)}, bf16[2,36,8,512]{3,2,1,0:T(8,128)(2,1)}, bf16[2,36,8,512]{3,2,1,0:T(8,128)(2,1)}) custom-call(s32[2,3,2,24]{3,2,1,0:T(2,128)} %scale_ref.1, bf16[2,24,16,512]{3,2,1,0:T(8,128)(2,1)} %k_ref.3, ...), custom_call_target="tpu_custom_call" | custom-call | bytes 4400256 | tf_op jit(solution)/shard_map/pallas_call | solution.py:27
  4.0 4.6 %collective-permute-start = (bf16[2,36,8,512]{3,2,1,0:T(8,128)(2,1)}, bf16[2,36,8,512]{3,2,1,0:T(8,128)(2,1)S(1)}, u32[]{:S(2)}, u32[]{:S(2)}) collective-permute-start(bf16[2,36,8,512]{3,2,1,0:T(8,128)(2,1)} %get-tuple-element.37), channel_id=1, source_target_pairs={{1,2},{3,4},{5,6},{7,8},{9,10},{11,12},{13,14},{2,1},{4,3},{6,5},{... | collective-permute-start | bytes 1769480 | tf_op jit(solution)/shard_map/ppermute | solution.py:529
  8.7 0.1 collective-permute-start.1
  8.8 0.7 collective-permute-start.2
  9.5 4.6 %collective-permute-start.3 = (bf16[3,2,4,16,512]{4,3,2,1,0:T(8,128)(2,1)}, bf16[3,2,4,16,512]{4,3,2,1,0:T(8,128)(2,1)S(1)}, u32[]{:S(2)}, u32[]{:S(2)}) collective-permute-start(bf16[3,2,4,16,512]{4,3,2,1,0:T(8,128)(2,1)} %get-tuple-element.51), channel_id=1, source_target_pairs={{0,16},{32,48},{64,80},{96,112},{16,0},{48,32},{80,64},{112,96},{1... | collective-permute-start | bytes 1179656 | tf_op jit(solution)/shard_map/ppermute | solution.py:529
  14.1 0.9 copy-done.8
  14.9 1.7 %shard_map.113 = (bf16[2,24,16,512]{3,2,1,0:T(8,128)(2,1)S(1)}, bf16[2,24,16,512]{3,2,1,0:T(8,128)(2,1)S(1)}, bf16[2,24,16,512]{3,2,1,0:T(8,128)(2,1)S(1)}) custom-call(s32[2,2]{1,0:T(2,128)S(1)} %copy-done.10, bf16[2,24,16,512]{3,2,1,0:T(8,128)(2,1)S(1)} %copy-done.5, bf16[2,24,16,512]{3,2,1,0:T(8,128)(2,1)S(1)} %copy-done.6, ...), custom_call_target="tpu_custom_call" | custom-call | flops 402653184 | bytes 4530192 | tf_op jit(solution)/shard_map/pallas_call | solution.py:27
  16.7 0.1 collective-permute-done.fr_ref.fo_ref
  16.7 0.2 shard_map.115
  16.9 0.7 collective-permute-start.4
  17.6 4.8 %collective-permute-start.5 = (bf16[2,12,8,512]{3,2,1,0:T(8,128)(2,1)S(1)}, bf16[2,12,8,512]{3,2,1,0:T(8,128)(2,1)S(1)}, u32[]{:S(2)}, u32[]{:S(2)}) collective-permute-start(bf16[2,12,8,512]{3,2,1,0:T(8,128)(2,1)S(1)} %get-tuple-element.53), channel_id=1, source_target_pairs={{0,16},{32,48},{64,80},{96,112},{16,0},{48,32},{80,64},{112,96},{1... | collective-permute-start | bytes 589832 | tf_op jit(solution)/shard_map/ppermute | solution.py:529
  22.4 3.8 %shard_map.114 = (bf16[2,2,24,16,512]{4,3,2,1,0:T(8,128)(2,1)S(1)}, bf16[2,2,24,16,512]{4,3,2,1,0:T(8,128)(2,1)S(1)}, f32[2,2,16,16,512]{4,3,2,1,0:T(8,128)S(1)}...) custom-call(bf16[2,24,16,512]{3,2,1,0:T(8,128)(2,1)S(1)} %get-tuple-el, ...), custom_call_target="tpu_custom_call" | custom-call | flops 805306368 | bytes 12263424 | tf_op jit(solution)/shard_map/pallas_call | solution.py:27
  26.2 1.7 %collective-permute-done.5.ke_ref = bf16[2,12,8,512]{3,2,1,0:T(8,128)(2,1)S(1)} collective-permute-done((bf16[2,12,8,512]{3,2,1,0:T(8,128)(2,1)S(1)}, bf16[2,12,8,512]{3,2,1,0:T(8,128)(2,1)S(1)}, u32[]{:S(2)}, u32[]{:S(2)}) %collective-permute-start.5) | collective-permute-done | bytes 196640 | tf_op jit(solution)/shard_map/ppermute | solution.py:529
  27.9 9.7 %shard_map.116 = (bf16[8,8,64,128]{3,2,1,0:T(8,128)(2,1)S(1)}, bf16[8,8,64,128]{3,2,1,0:T(8,128)(2,1)S(1)}, bf16[2,32,16,512]{3,2,1,0:T(8,128)(2,1)S(1)}, bf16[2,32,24,1024]{3,2,1,0:T(8,128)(2,1)}) custom-call(bf16[2,24,16,512]{3,2,1,0:T(8,128)(2,1)S(1)} %get-tuple-element.36.qs_ref, bf16[2,24,16,512]{3,2,1,0:T(8,128)(2,1)S(1)} %get-tuple-element.40.do_ref, ...), custom_call_target="tpu_custom_call" | custom-call | flops 2415919104 | bytes 19660800 | tf_op jit(solution)/shard_map/pallas_call | solution.py:27
  37.6 0.7 collective-permute-start.10
  38.3 2.3 %collective-permute-done.10.y_ref = bf16[8,8,64,128]{3,2,1,0:T(8,128)(2,1)S(1)} collective-permute-done((bf16[8,8,64,128]{3,2,1,0:T(8,128)(2,1)S(1)}, bf16[8,8,64,128]{3,2,1,0:T(8,128)(2,1)S(1)}, u32[]{:S(2)}, u32[]{:S(2)}) %collective-permute-start.10) | collective-permute-done | bytes 1048608 | tf_op jit(solution)/shard_map/ppermute | solution.py:606
  40.6 1.2 %shard_map.120 = bf16[8,8,64,128]{3,2,1,0:T(8,128)(2,1)} custom-call(bf16[8,8,64,128]{3,2,1,0:T(8,128)(2,1)S(1)} %get-tuple-element.61.x_ref, bf16[8,8,64,128]{3,2,1,0:T(8,128)(2,1)S(1)} %collective-permute-done.10.y_ref), custom_call_target="tpu_custom_call" | custom-call | bytes 3145728 | tf_op jit(solution)/shard_map/pallas_call | solution.py:27
  41.8 13.5 %all-to-all-start = ((bf16[64,64,128]{2,1,0:T(8,128)(2,1)}), bf16[64,64,128]{2,1,0:T(8,128)(2,1)S(1)}, u32[]{:S(2)}, u32[]{:S(2)}) async-start(bf16[64,64,128]{2,1,0:T(8,128)(2,1)} %bitcast), calls=%async_computation | async-start | bytes 2097152 | tf_op jit(solution)/shard_map/all_to_all | solution.py:608
  55.4 1.9 %copy-done.1 = bf16[2,32,24,1024]{3,2,1,0:T(8,128)(2,1)S(1)} copy-done((bf16[2,32,24,1024]{3,2,1,0:T(8,128)(2,1)S(1)}, bf16[2,32,24,1024]{3,2,1,0:T(8,128)(2,1)}, u32[]{:S(2)}) %copy-start.1) | copy-done | bytes 3145752
  57.2 1.4 %copy-done.4 = bf16[512,1536]{1,0:T(8,128)(2,1)S(1)} copy-done((bf16[512,1536]{1,0:T(8,128)(2,1)S(1)}, bf16[512,1536]{1,0:T(8,128)(2,1)}, u32[]{:S(2)}) %copy-start.4) | copy-done | bytes 1572888
  58.6 2.4 %shard_map.117 = (bf16[2,32,16,512]{3,2,1,0:T(8,128)(2,1)S(1)}, bf16[2,16,8,512]{3,2,1,0:T(8,128)(2,1)S(1)}, bf16[2,16,8,512]{3,2,1,0:T(8,128)(2,1)S(1)}) custom-call(bf16[2,32,24,1024]{3,2,1,0:T(8,128)(2,1)S(1)} %copy-done.1, bf16[2,32,16,512]{3,2,1,0:T(8,128)(2,1)S(1)} %get-tuple-element.55.dq_ref, bf16[512,1536]{1,0:T(8,128)(2,1)S(1)} %copy-done.4), custom_call_target="tpu_custom_call" | custom-call | flops 1207959552 | bytes 7340032 | tf_op jit(solution)/shard_map/pallas_call | solution.py:27
  61.0 3.5 %collective-permute-start.6 = (bf16[2,16,8,512]{3,2,1,0:T(8,128)(2,1)S(1)}, bf16[2,16,8,512]{3,2,1,0:T(8,128)(2,1)S(1)}, u32[]{:S(2)}, u32[]{:S(2)}) collective-permute-start(bf16[2,16,8,512]{3,2,1,0:T(8,128)(2,1)S(1)} %get-tuple-element.57), channel_id=1, source_target_pairs={{1,2},{3,4},{5,6},{7,8},{9,10},{11,12},{13,14},{2,1},{4,3},{6,5},{... | collective-permute-start | bytes 786440 | tf_op jit(solution)/shard_map/ppermute | solution.py:529
  64.5 0.1 collective-permute-start.7
  64.6 6.6 %collective-permute-done.6.fo_ref = bf16[2,16,8,512]{3,2,1,0:T(8,128)(2,1)S(1)} collective-permute-done((bf16[2,16,8,512]{3,2,1,0:T(8,128)(2,1)S(1)}, bf16[2,16,8,512]{3,2,1,0:T(8,128)(2,1)S(1)}, u32[]{:S(2)}, u32[]{:S(2)}) %collective-permute-start.6) | collective-permute-done | bytes 262176 | tf_op jit(solution)/shard_map/ppermute | solution.py:529
  71.3 0.1 shard_map.118
  71.4 0.7 collective-permute-start.8
  72.1 3.7 %collective-permute-start.9 = (bf16[2,4,16,512]{3,2,1,0:T(8,128)(2,1)S(1)}, bf16[2,4,16,512]{3,2,1,0:T(8,128)(2,1)S(1)}, u32[]{:S(2)}, u32[]{:S(2)}) collective-permute-start(bf16[2,4,16,512]{3,2,1,0:T(8,128)(2,1)S(1)} %get-tuple-element.60), channel_id=1, source_target_pairs={{0,16},{32,48},{64,80},{96,112},{16,0},{48,32},{80,64},{112,96},{1... | collective-permute-start | bytes 393224 | tf_op jit(solution)/shard_map/ppermute | solution.py:529
  75.8 0.8 shard_map.121
  76.6 8.8 %all-to-all-start.1 = ((f32[128,1,128]{2,1,0:T(1,128)}), f32[128,1,128]{2,1,0:T(1,128)S(1)}, u32[]{:S(2)}, u32[]{:S(2)}) async-start(f32[128,1,128]{2,1,0:T(1,128)} %bitcast.2), calls=%async_computation.1 | async-start | bytes 131072 | tf_op jit(solution)/shard_map/all_to_all | solution.py:631
  85.5 1.2 %shard_map.119 = bf16[2,24,16,512]{3,2,1,0:T(8,128)(2,1)} custom-call(bf16[2,32,16,512]{3,2,1,0:T(8,128)(2,1)S(1)} %get-tuple-element.56.gt_ref, bf16[2,16,8,512]{3,2,1,0:T(8,128)(2,1)S(1)} %collective-permute-done.6.fo_ref, bf16[2,16,8,512]{3,2,1,0:T(8,128)(2,1)S(1)} %collective-permute-done.7.fe_ref, ...), custom_call_target="tpu_custom_call" | custom-call | bytes 2621440 | tf_op jit(solution)/shard_map/pallas_call | solution.py:27
  86.7 8.3 %all-to-all-done.1 = f32[128,1,128]{2,1,0:T(1,128)S(1)} async-done(((f32[128,1,128]{2,1,0:T(1,128)}), f32[128,1,128]{2,1,0:T(1,128)S(1)}, u32[]{:S(2)}, u32[]{:S(2)}) %all-to-all-start.1) | async-done | bytes 65568 | tf_op jit(solution)/shard_map/all_to_all | solution.py:631
  95.0 0.8 shard_map.122
  (27 shorter events, 0.1 us)
Async XLA Ops:
  0.6 13.4 %copy-start.10 = (s32[2,2]{1,0:T(2,128)S(1)}, s32[2,2]{1,0:T(2,128)}, u32[]{:S(2)}) copy-start(s32[2,2]{1,0:T(2,128)} %crop_ref.1) | copy-start | bytes 52
  0.6 13.4 %copy-start.6 = (bf16[2,24,16,512]{3,2,1,0:T(8,128)(2,1)S(1)}, bf16[2,24,16,512]{3,2,1,0:T(8,128)(2,1)}, u32[]{:S(2)}) copy-start(bf16[2,24,16,512]{3,2,1,0:T(8,128)(2,1)} %g_ref.1) | copy-start | bytes 2359300
  0.7 13.4 %copy-start.5 = (bf16[2,24,16,512]{3,2,1,0:T(8,128)(2,1)S(1)}, bf16[2,24,16,512]{3,2,1,0:T(8,128)(2,1)}, u32[]{:S(2)}) copy-start(bf16[2,24,16,512]{3,2,1,0:T(8,128)(2,1)} %q_ref.1) | copy-start | bytes 2359300
  0.7 13.4 %copy-start.7 = (bf16[512,512]{1,0:T(8,128)(2,1)S(1)}, bf16[512,512]{1,0:T(8,128)(2,1)}, u32[]{:S(2)}) copy-start(bf16[512,512]{1,0:T(8,128)(2,1)} %w_ref.2) | copy-start | bytes 1572868
  4.0 18.4 %copy-start.2 = (bf16[2,24,16,512]{3,2,1,0:T(8,128)(2,1)S(1)}, bf16[2,24,16,512]{3,2,1,0:T(8,128)(2,1)}, u32[]{:S(2)}) copy-start(bf16[2,24,16,512]{3,2,1,0:T(8,128)(2,1)} %k_ref.3) | copy-start | bytes 2359300
  4.0 18.4 %copy-start.3 = (bf16[2,24,16,512]{3,2,1,0:T(8,128)(2,1)S(1)}, bf16[2,24,16,512]{3,2,1,0:T(8,128)(2,1)}, u32[]{:S(2)}) copy-start(bf16[2,24,16,512]{3,2,1,0:T(8,128)(2,1)} %v_ref.3) | copy-start | bytes 2359300
  4.0 12.7 %collective-permute-start = (bf16[2,36,8,512]{3,2,1,0:T(8,128)(2,1)}, bf16[2,36,8,512]{3,2,1,0:T(8,128)(2,1)S(1)}, u32[]{:S(2)}, u32[]{:S(2)}) collective-permute-start(bf16[2,36,8,512]{3,2,1,0:T(8,128)(2,1)} %get-tuple-element.37), channel_id=1, source_target_pairs={{1,2},{3,4},{5,6},{7,8},{9,10},{11,12},{13,14},{2,1},{4,3},{6,5},{... | collective-permute-start | bytes 1769480 | tf_op jit(solution)/shard_map/ppermute | solution.py:529
  8.7 8.1 %collective-permute-start.1 = (bf16[2,36,8,512]{3,2,1,0:T(8,128)(2,1)}, bf16[2,36,8,512]{3,2,1,0:T(8,128)(2,1)S(1)}, u32[]{:S(2)}, u32[]{:S(2)}) collective-permute-start(bf16[2,36,8,512]{3,2,1,0:T(8,128)(2,1)} %get-tuple-element.38), channel_id=1, source_target_pairs={{0,1},{2,3},{4,5},{6,7},{8,9},{10,11},{12,13},{14,15},{1,0},{3,2},... | collective-permute-start | bytes 1769480 | tf_op jit(solution)/shard_map/ppermute | solution.py:529
  8.8 17.4 %collective-permute-start.2 = (bf16[3,2,4,16,512]{4,3,2,1,0:T(8,128)(2,1)}, bf16[3,2,4,16,512]{4,3,2,1,0:T(8,128)(2,1)S(1)}, u32[]{:S(2)}, u32[]{:S(2)}) collective-permute-start(bf16[3,2,4,16,512]{4,3,2,1,0:T(8,128)(2,1)} %get-tuple-element.50), channel_id=1, source_target_pairs={{16,32},{48,64},{80,96},{32,16},{64,48},{96,80},{17,33},{49,65},{8... | collective-permute-start | bytes 1179656 | tf_op jit(solution)/shard_map/ppermute | solution.py:529
  9.5 16.7 %collective-permute-start.3 = (bf16[3,2,4,16,512]{4,3,2,1,0:T(8,128)(2,1)}, bf16[3,2,4,16,512]{4,3,2,1,0:T(8,128)(2,1)S(1)}, u32[]{:S(2)}, u32[]{:S(2)}) collective-permute-start(bf16[3,2,4,16,512]{4,3,2,1,0:T(8,128)(2,1)} %get-tuple-element.51), channel_id=1, source_target_pairs={{0,16},{32,48},{64,80},{96,112},{16,0},{48,32},{80,64},{112,96},{1... | collective-permute-start | bytes 1179656 | tf_op jit(solution)/shard_map/ppermute | solution.py:529
  14.0 0.9 copy-start.8
  14.9 7.4 %copy-start.9 = (f32[2,3,2,1536]{3,2,1,0:T(2,128)S(1)}, f32[2,3,2,1536]{3,2,1,0:T(2,128)}, u32[]{:S(2)}) copy-start(f32[2,3,2,1536]{3,2,1,0:T(2,128)} %get-tuple-element.35.fac_ref) | copy-start | bytes 221188
  16.9 9.3 %collective-permute-start.4 = (bf16[2,12,8,512]{3,2,1,0:T(8,128)(2,1)S(1)}, bf16[2,12,8,512]{3,2,1,0:T(8,128)(2,1)S(1)}, u32[]{:S(2)}, u32[]{:S(2)}) collective-permute-start(bf16[2,12,8,512]{3,2,1,0:T(8,128)(2,1)S(1)} %get-tuple-element.52), channel_id=1, source_target_pairs={{16,32},{48,64},{80,96},{32,16},{64,48},{96,80},{17,33},{49,65},{8... | collective-permute-start | bytes 589832 | tf_op jit(solution)/shard_map/ppermute | solution.py:529
  17.6 10.3 %collective-permute-start.5 = (bf16[2,12,8,512]{3,2,1,0:T(8,128)(2,1)S(1)}, bf16[2,12,8,512]{3,2,1,0:T(8,128)(2,1)S(1)}, u32[]{:S(2)}, u32[]{:S(2)}) collective-permute-start(bf16[2,12,8,512]{3,2,1,0:T(8,128)(2,1)S(1)} %get-tuple-element.53), channel_id=1, source_target_pairs={{0,16},{32,48},{64,80},{96,112},{16,0},{48,32},{80,64},{112,96},{1... | collective-permute-start | bytes 589832 | tf_op jit(solution)/shard_map/ppermute | solution.py:529
  22.4 5.5 %copy-start = (bf16[2,24,16,512]{3,2,1,0:T(8,128)(2,1)S(1)}, bf16[2,24,16,512]{3,2,1,0:T(8,128)(2,1)}, u32[]{:S(2)}) copy-start(bf16[2,24,16,512]{3,2,1,0:T(8,128)(2,1)} %tok_ref.3) | copy-start | bytes 2359300
  37.6 3.0 %collective-permute-start.10 = (bf16[8,8,64,128]{3,2,1,0:T(8,128)(2,1)S(1)}, bf16[8,8,64,128]{3,2,1,0:T(8,128)(2,1)S(1)}, u32[]{:S(2)}, u32[]{:S(2)}) collective-permute-start(bf16[8,8,64,128]{3,2,1,0:T(8,128)(2,1)S(1)} %get-tuple-element.62), channel_id=1, source_target_pairs={{0,1},{1,0},{2,3},{3,2},{4,5},{5,4},{6,7},{7,6},{8,9},{9,8},{10,11... | collective-permute-start | bytes 3145736 | tf_op jit(solution)/shard_map/ppermute | solution.py:606
  41.8 34.0 %all-to-all-start = ((bf16[64,64,128]{2,1,0:T(8,128)(2,1)}), bf16[64,64,128]{2,1,0:T(8,128)(2,1)S(1)}, u32[]{:S(2)}, u32[]{:S(2)}) async-start(bf16[64,64,128]{2,1,0:T(8,128)(2,1)} %bitcast), calls=%async_computation | async-start | bytes 2097152 | tf_op jit(solution)/shard_map/all_to_all | solution.py:608
  55.3 1.9 %copy-start.1 = (bf16[2,32,24,1024]{3,2,1,0:T(8,128)(2,1)S(1)}, bf16[2,32,24,1024]{3,2,1,0:T(8,128)(2,1)}, u32[]{:S(2)}) copy-start(bf16[2,32,24,1024]{3,2,1,0:T(8,128)(2,1)} %get-tuple-element.54.kv_ref) | copy-start | bytes 9437188
  57.2 1.4 %copy-start.4 = (bf16[512,1536]{1,0:T(8,128)(2,1)S(1)}, bf16[512,1536]{1,0:T(8,128)(2,1)}, u32[]{:S(2)}) copy-start(bf16[512,1536]{1,0:T(8,128)(2,1)} %w_ref.3) | copy-start | bytes 4718596
  61.0 10.3 %collective-permute-start.6 = (bf16[2,16,8,512]{3,2,1,0:T(8,128)(2,1)S(1)}, bf16[2,16,8,512]{3,2,1,0:T(8,128)(2,1)S(1)}, u32[]{:S(2)}, u32[]{:S(2)}) collective-permute-start(bf16[2,16,8,512]{3,2,1,0:T(8,128)(2,1)S(1)} %get-tuple-element.57), channel_id=1, source_target_pairs={{1,2},{3,4},{5,6},{7,8},{9,10},{11,12},{13,14},{2,1},{4,3},{6,5},{... | collective-permute-start | bytes 786440 | tf_op jit(solution)/shard_map/ppermute | solution.py:529
  64.5 6.7 %collective-permute-start.7 = (bf16[2,16,8,512]{3,2,1,0:T(8,128)(2,1)S(1)}, bf16[2,16,8,512]{3,2,1,0:T(8,128)(2,1)S(1)}, u32[]{:S(2)}, u32[]{:S(2)}) collective-permute-start(bf16[2,16,8,512]{3,2,1,0:T(8,128)(2,1)S(1)} %get-tuple-element.58), channel_id=1, source_target_pairs={{0,1},{2,3},{4,5},{6,7},{8,9},{10,11},{12,13},{14,15},{1,0},{3,2},... | collective-permute-start | bytes 786440 | tf_op jit(solution)/shard_map/ppermute | solution.py:529
  71.4 14.0 %collective-permute-start.8 = (bf16[2,4,16,512]{3,2,1,0:T(8,128)(2,1)S(1)}, bf16[2,4,16,512]{3,2,1,0:T(8,128)(2,1)S(1)}, u32[]{:S(2)}, u32[]{:S(2)}) collective-permute-start(bf16[2,4,16,512]{3,2,1,0:T(8,128)(2,1)S(1)} %get-tuple-element.59), channel_id=1, source_target_pairs={{16,32},{48,64},{80,96},{32,16},{64,48},{96,80},{17,33},{49,65},{8... | collective-permute-start | bytes 393224 | tf_op jit(solution)/shard_map/ppermute | solution.py:529
  72.1 13.4 %collective-permute-start.9 = (bf16[2,4,16,512]{3,2,1,0:T(8,128)(2,1)S(1)}, bf16[2,4,16,512]{3,2,1,0:T(8,128)(2,1)S(1)}, u32[]{:S(2)}, u32[]{:S(2)}) collective-permute-start(bf16[2,4,16,512]{3,2,1,0:T(8,128)(2,1)S(1)} %get-tuple-element.60), channel_id=1, source_target_pairs={{0,16},{32,48},{64,80},{96,112},{16,0},{48,32},{80,64},{112,96},{1... | collective-permute-start | bytes 393224 | tf_op jit(solution)/shard_map/ppermute | solution.py:529
  76.6 18.4 %all-to-all-start.1 = ((f32[128,1,128]{2,1,0:T(1,128)}), f32[128,1,128]{2,1,0:T(1,128)S(1)}, u32[]{:S(2)}, u32[]{:S(2)}) async-start(f32[128,1,128]{2,1,0:T(1,128)} %bitcast.2), calls=%async_computation.1 | async-start | bytes 131072 | tf_op jit(solution)/shard_map/all_to_all | solution.py:631
